TPU v7x, 32 devices: a whole 2x2x4 slice. The times are simulated.
32 devices in a mesh: dir: 2 (over x), pos: 16 (over z, y, core).
Axes of the slice: x: 2, y: 2, z: 4, core: 2. Of those that a mesh axis runs over, the one named last changes fastest.
Arguments:
- coherence: bfloat16 [2, 64, 64, 64, 128], P(None, 'dir', 'pos'), may hold values from -6 to 6
- shift_first: int32 [64], replicated, may hold values from -4 to 3, as said below
- fraction_first: float32 [64], replicated, may hold values from 0.1 to 0.9
- shift_second: int32 [64], replicated, may hold values from -16 to 15, as said below
- fraction_second: float32 [64], replicated, may hold values from 0.1 to 0.9
- scatter_kernel: float32 [17, 64], replicated, may hold values from -0.1875 to 0.1875
Outputs:
- wigner_next: float32 [64, 64, 64, 128], P('dir', None, 'pos')
Inputs may be any that keep to these rules, and one draw needn't show every extreme that they name: `shift_first`: each value of the range is taken by exactly 8 directions. `shift_second`: each value of the range is taken by exactly 2 directions.
All inputs are finite; a program needn't handle non-finite values.
Results may differ from a plain program's by a relative error of at most 0.0003.
Values may be sent and summed in bfloat16 or wider, within the bound.
No kernel may reach another device: no remote copies, remote signals or barrier semaphores. Data moves between devices by JAX's collectives and lax.ppermute only.
A program may use at most 256 MiB of HBM per device.

v0:
```python
import math

import jax
import jax.numpy as jnp
from jax import lax
from jax.sharding import PartitionSpec as P

R = 8
H = 4


def with_halo(cells, sides, width, closed):
    for axis, dim in sides:
        count = lax.axis_size(axis)
        ends = count if closed else count - 1
        head = lax.slice_in_dim(cells, 0, width, axis=dim)
        tail = lax.slice_in_dim(cells, cells.shape[dim] - width, cells.shape[dim], axis=dim)
        cells = jnp.concatenate(
            [
                lax.ppermute(tail, axis, [(i, (i + 1) % count) for i in range(ends)]),
                cells,
                lax.ppermute(head, axis, [((i + 1) % count, i) for i in range(ends)]),
            ],
            axis=dim,
        )
    return cells


def phase_tables(length):
    counter = jnp.arange(length, dtype=jnp.int32)
    product = counter[:, None] * counter[None, :] % length
    angles = product.astype(jnp.float32) * (2.0 * math.pi / length)
    factor = 1.0 / math.sqrt(length)
    return (jnp.cos(angles) * factor, jnp.sin(angles) * factor)


def contract(pattern, operand_a, operand_b):
    return jnp.einsum(
        pattern,
        operand_a,
        operand_b,
        precision=lax.Precision.HIGHEST,
        preferred_element_type=jnp.float32,
    )


def finish_bands(received):
    cos_one, sin_one = phase_tables(received.shape[1])
    real_part = contract("ts,sbax->tbax", cos_one, received[0]) + contract(
        "ts,sbax->tbax", sin_one, received[1]
    )
    return lax.all_to_all(real_part, "dir", split_axis=0, concat_axis=1, tiled=True)


def shear_block(wigner, shift_first, fraction_first):
    band_count = wigner.shape[0]
    cell_count = wigner.shape[2]
    first_band = lax.axis_index("dir") * band_count
    shifts = lax.dynamic_slice_in_dim(shift_first, first_band, band_count)
    weights = lax.dynamic_slice_in_dim(fraction_first, first_band, band_count)
    padded = with_halo(wigner, (("pos", 2),), H, False)
    rows_out = jnp.arange(cell_count, dtype=jnp.int32)
    rows_in = jnp.arange(cell_count + 2 * H, dtype=jnp.int32)
    target = rows_out[None, :, None] + H - shifts[:, None, None]
    near_tap = (rows_in[None, None, :] == target).astype(jnp.float32)
    far_tap = (rows_in[None, None, :] == target - 1).astype(jnp.float32)
    band_matrix = (1.0 - weights)[:, None, None] * near_tap + weights[:, None, None] * far_tap
    return contract("kaj,kbjx->kbax", band_matrix, padded)


def convolve(circulant, source, out_rows):
    summed = jnp.zeros((out_rows,) + source.shape[1:], jnp.float32)
    for offset in range(circulant.shape[0]):
        summed = summed + contract(
            "ij,kjax->kiax", circulant[offset], source[offset : offset + out_rows]
        )
    return summed


def body(coherence, shift_first, fraction_first, shift_second, fraction_second, scatter_kernel):
    direction_count = coherence.shape[2] * lax.axis_size("pos")
    cos_two, sin_two = phase_tables(direction_count)
    cell_block = lax.all_to_all(coherence, "pos", split_axis=3, concat_axis=2, tiled=True)
    real_in = cell_block[0].astype(jnp.float32)
    imag_in = cell_block[1].astype(jnp.float32)
    real_mid = contract("ts,bsax->btax", cos_two, real_in) + contract(
        "ts,bsax->btax", sin_two, imag_in
    )
    imag_mid = contract("ts,bsax->btax", cos_two, imag_in) - contract(
        "ts,bsax->btax", sin_two, real_in
    )
    mixed = jnp.stack([real_mid, imag_mid])
    wigner = finish_bands(lax.all_to_all(mixed, "dir", split_axis=2, concat_axis=1, tiled=True))
    moved_one = shear_block(wigner, shift_first, fraction_first)
    band_count = moved_one.shape[0]
    column_count = moved_one.shape[3]
    positions = jnp.arange(column_count, dtype=jnp.int32)
    target_two = positions[None, :, None] - shift_second[:, None, None]
    near_two = (positions[None, None, :] == target_two).astype(jnp.float32)
    far_two = (positions[None, None, :] == target_two - 1).astype(jnp.float32)
    shear_matrix = (1.0 - fraction_second)[:, None, None] * near_two + fraction_second[
        :, None, None
    ] * far_two
    moved_two = contract("bxy,kbay->kbax", shear_matrix, moved_one)
    kernel_positions = jnp.arange(direction_count, dtype=jnp.int32)
    lag_index = (kernel_positions[:, None] - kernel_positions[None, :]) % direction_count
    circulant = scatter_kernel[:, lag_index]
    extended = with_halo(moved_two, (("dir", 0),), R, True)
    summed = moved_two + convolve(circulant, extended, band_count)
    return summed


def solution(mesh):
    placed = (P(None, "dir", "pos", None, None), P(), P(), P(), P(), P())
    return jax.shard_map(
        body, mesh=mesh, in_specs=placed, out_specs=P("dir", None, "pos", None), check_vma=False
    )
```

profile of v0, /device:TPU:9, one launch (start us, length us, event | category | flops | bytes accessed | tf_op | source)
XLA Modules:
  0.0 718.5 jit_solution(14800723853186895690)
XLA Ops:
  0.0 4.9 copy.182
  4.9 99.1 %all_to_all.48 = bf16[2,32,4,64,128]{4,1,2,0,3:T(8,128)(2,1)S(1)} all-to-all(bf16[2,32,4,64,128]{4,1,2,0,3:T(8,128)(2,1)S(1)} %copy.182), channel_id=1, replica_groups=mesh['dir'=2,'pos'=16] {'pos'}, dimensions={3} | all-to-all | bytes 8388608 | tf_op jit(solution)/shard_map/all_to_all | solution.py:83
  120.4 12.4 %copy.184 = f32[2,32,64,4,128]{4,3,1,0,2:T(4,128)} copy(f32[2,32,64,4,128]{4,2,3,1,0:T(8,128)} %pad_maximum_fusion) | data formatting | bytes 16777216 | tf_op jit(solution)/shard_map/stack | solution.py:92
  132.8 97.3 %all_to_all.49 = f32[2,32,64,4,128]{4,3,1,0,2:T(4,128)S(1)} all-to-all(f32[2,32,64,4,128]{4,3,1,0,2:T(4,128)} %copy.184), channel_id=1, replica_groups=mesh['dir'=2,'pos'=16] {'dir'}, dimensions={2} | all-to-all | bytes 16777216 | tf_op jit(solution)/shard_map/all_to_all | solution.py:93
  237.4 4.5 convolution_add_fusion
  244.8 49.5 %all_to_all.50 = f32[64,32,4,128]{3,2,1,0:T(4,128)S(1)} all-to-all(f32[64,32,4,128]{3,2,1,0:T(4,128)S(1)} %copy.186), channel_id=1, replica_groups=mesh['dir'=2,'pos'=16] {'dir'}, dimensions={0} | all-to-all | bytes 8388608 | tf_op jit(solution)/shard_map/all_to_all | solution.py:52
  295.6 5.6 copy.189
  307.0 88.4 %collective-permute-done = f32[32,64,4,128]{3,2,1,0:T(4,128)} collective-permute-done((f32[32,64,4,128]{3,2,1,0:T(4,128)}, f32[32,64,4,128]{3,2,1,0:T(4,128)}, u32[]{:S(2)}, u32[]{:S(2)}) %collective-permute-start) | collective-permute-done | bytes 4194336 | tf_op jit(solution)/shard_map/ppermute | solution.py:20
  398.2 18.1 %fusion.65 = f32[32,64,4,128]{3,2,1,0:T(4,128)S(1)} fusion(f32[32,64,4,128]{3,2,1,0:T(4,128)} %collective-permute-done.1, f32[32,64,4,128]{3,2,1,0:T(4,128)} %copy.189, f32[32,64,4,128]{3,2,1,0:T(4,128)} %collective-permute-done, f32[32]{0:T(128)S(1)} %get-tuple-element.6, s32[32,4]{1,0:T(8,128)S(1)} %get-tuple-element.30, f32[32]{0:T(128)S(1)} %get-tuple-element.5, ...), kind=kOutput, calls=%fused_computation.116 | convolution fusion | flops 157294080 | bytes 16778496 | tf_op jit(solution)/shard_map/kaj,kbjx->kbax/dot_general | solution.py:38
  416.4 12.0 %fusion.60 = f32[32,64,4,128]{3,0,2,1:T(8,128)S(1)} fusion(f32[32,64,4,128]{3,2,1,0:T(4,128)S(1)} %fusion.65, f32[64]{0:T(128)S(1)} %copy-done.19, s32[64,128]{1,0:T(8,128)S(1)} %get-tuple-element.32, f32[64]{0:T(128)S(1)} %broadcast_subtract_fusion.1, s32[64,128]{1,0:T(8,128)S(1)} %get-tuple-element.31), kind=kOutput, calls=%fused_computation.115 | convolution fusion | flops 1615855616 | bytes 8454656 | tf_op jit(solution)/shard_map/bxy,kbay->kbax/dot_general | solution.py:38
  432.2 10.8 %gather_fusion = f32[4096,17]{1,0:T(8,128)S(1)} fusion(f32[17,64]{0,1:T(8,128)S(1)} %copy.193, s32[4096]{0:T(1024)S(1)} %broadcast_clamp_fusion), kind=kCustom, calls=%fused_computation | custom fusion | bytes 573440 | tf_op jit(solution)/shard_map/gather | solution.py:107
  445.3 8.7 %fusion.38 = f32[32,4,128,64]{2,3,1,0:T(8,128)S(1)} fusion(f32[32,64,4,128]{3,0,2,1:T(8,128)} %copy-done, f32[17,64,64]{2,1,0:T(8,128)S(1)} %bitcast.202), kind=kOutput, calls=%fused_computation.81 | convolution fusion | flops 805306368 | bytes 8421376 | tf_op jit(solution)/shard_map/ij,kjax->kiax/dot_general | solution.py:38
  454.0 14.7 %fusion.14 = (f32[32,64,4,128]{3,0,2,1:T(8,128)}, f32[32,64,4,128]{3,0,2,1:T(8,128)}, f32[32,64,4,128]{3,0,2,1:T(8,128)}, f32[32,64,4,128]{3,0,2,1:T(8,128)}, f3...) fusion(f32[32,64,4,128]{3,0,2,1:T(8,128)S(1)} %copy-done.1, ...), kind=kLoop, calls=%fused_computation.45 | loop fusion | flops 8388608 | bytes 38797312 | tf_op jit(solution)/shard_map/concatenate | solution.py:18
  468.8 9.2 %fusion.42 = f32[32,4,128,64]{2,3,1,0:T(8,128)S(1)} fusion(f32[32,64,4,128]{3,0,2,1:T(8,128)} %get-tuple-element.16, f32[17,64,64]{2,1,0:T(8,128)S(1)} %bitcast.203), kind=kOutput, calls=%fused_computation.87 | convolution fusion | flops 805306368 | bytes 8421376 | tf_op jit(solution)/shard_map/ij,kjax->kiax/dot_general | solution.py:38
  478.0 9.1 %fusion.44 = f32[32,4,128,64]{2,3,1,0:T(8,128)} fusion(f32[32,64,4,128]{3,0,2,1:T(8,128)S(1)} %copy-done.13, f32[17,64,64]{2,1,0:T(8,128)S(1)} %bitcast.204), kind=kOutput, calls=%fused_computation.90 | convolution fusion | flops 805306368 | bytes 8421376 | tf_op jit(solution)/shard_map/ij,kjax->kiax/dot_general | solution.py:38
  487.1 9.2 %fusion.46 = f32[32,4,128,64]{2,3,1,0:T(8,128)} fusion(f32[32,64,4,128]{3,0,2,1:T(8,128)S(1)} %copy-done.11, f32[17,64,64]{2,1,0:T(8,128)S(1)} %bitcast.205), kind=kOutput, calls=%fused_computation.93 | convolution fusion | flops 805306368 | bytes 8421376 | tf_op jit(solution)/shard_map/ij,kjax->kiax/dot_general | solution.py:38
  496.3 9.3 %fusion.48 = f32[32,4,128,64]{2,3,1,0:T(8,128)} fusion(f32[32,64,4,128]{3,0,2,1:T(8,128)S(1)} %copy-done.9, f32[17,64,64]{2,1,0:T(8,128)S(1)} %bitcast.206), kind=kOutput, calls=%fused_computation.96 | convolution fusion | flops 805306368 | bytes 8421376 | tf_op jit(solution)/shard_map/ij,kjax->kiax/dot_general | solution.py:38
  505.6 9.1 %fusion.50 = f32[32,4,128,64]{2,3,1,0:T(8,128)} fusion(f32[32,64,4,128]{3,0,2,1:T(8,128)S(1)} %copy-done.7, f32[17,64,64]{2,1,0:T(8,128)S(1)} %bitcast.207), kind=kOutput, calls=%fused_computation.99 | convolution fusion | flops 805306368 | bytes 8421376 | tf_op jit(solution)/shard_map/ij,kjax->kiax/dot_general | solution.py:38
  514.7 9.1 %fusion.52 = f32[32,4,128,64]{2,3,1,0:T(8,128)} fusion(f32[32,64,4,128]{3,0,2,1:T(8,128)S(1)} %copy-done.5, f32[17,64,64]{2,1,0:T(8,128)S(1)} %bitcast.208), kind=kOutput, calls=%fused_computation.102 | convolution fusion | flops 805306368 | bytes 8421376 | tf_op jit(solution)/shard_map/ij,kjax->kiax/dot_general | solution.py:38
  523.8 9.4 %fusion.54 = f32[32,4,128,64]{2,3,1,0:T(8,128)} fusion(f32[32,64,4,128]{3,0,2,1:T(8,128)S(1)} %copy-done.3, f32[17,64,64]{2,1,0:T(8,128)S(1)} %bitcast.209), kind=kOutput, calls=%fused_computation.104 | convolution fusion | flops 805306368 | bytes 8421376 | tf_op jit(solution)/shard_map/ij,kjax->kiax/dot_general | solution.py:38
  533.1 9.1 %fusion.40 = f32[32,4,128,64]{2,3,1,0:T(8,128)} fusion(f32[32,64,4,128]{3,0,2,1:T(8,128)S(1)} %copy-done.2, f32[17,64,64]{2,1,0:T(8,128)S(1)} %bitcast.210), kind=kOutput, calls=%fused_computation.84 | convolution fusion | flops 805306368 | bytes 8421376 | tf_op jit(solution)/shard_map/ij,kjax->kiax/dot_general | solution.py:38
  542.2 13.8 %fusion.7 = (f32[32,64,4,128]{3,0,2,1:T(8,128)S(1)}, f32[32,64,4,128]{3,0,2,1:T(8,128)}, f32[32,64,4,128]{3,0,2,1:T(8,128)}, f32[32,64,4,128]{3,0,2,1:T(8,128)},...) fusion(f32[32,64,4,128]{3,0,2,1:T(8,128)S(1)} %copy-done.1, ...), kind=kLoop, calls=%fused_computation.38 | loop fusion | flops 8388608 | bytes 38797312 | tf_op jit(solution)/shard_map/concatenate | solution.py:18
  556.1 11.7 %fusion.22 = f32[32,4,128,64]{2,3,1,0:T(8,128)} fusion(f32[32,64,4,128]{3,0,2,1:T(8,128)} %get-tuple-element.23, f32[17,64,64]{2,1,0:T(8,128)S(1)} %bitcast.211), kind=kOutput, calls=%fused_computation.57 | convolution fusion | flops 805306368 | bytes 8421376 | tf_op jit(solution)/shard_map/ij,kjax->kiax/dot_general | solution.py:38
  567.7 9.1 %fusion.24 = f32[32,4,128,64]{2,3,1,0:T(8,128)} fusion(f32[32,64,4,128]{3,0,2,1:T(8,128)S(1)} %copy-done.14, f32[17,64,64]{2,1,0:T(8,128)S(1)} %bitcast.212), kind=kOutput, calls=%fused_computation.60 | convolution fusion | flops 805306368 | bytes 8421376 | tf_op jit(solution)/shard_map/ij,kjax->kiax/dot_general | solution.py:38
  576.9 9.3 %fusion.26 = f32[32,4,128,64]{2,3,1,0:T(8,128)} fusion(f32[32,64,4,128]{3,0,2,1:T(8,128)S(1)} %copy-done.12, f32[17,64,64]{2,1,0:T(8,128)S(1)} %bitcast.213), kind=kOutput, calls=%fused_computation.63 | convolution fusion | flops 805306368 | bytes 8421376 | tf_op jit(solution)/shard_map/ij,kjax->kiax/dot_general | solution.py:38
  586.2 9.1 %fusion.28 = f32[32,4,128,64]{2,3,1,0:T(8,128)} fusion(f32[32,64,4,128]{3,0,2,1:T(8,128)S(1)} %copy-done.10, f32[17,64,64]{2,1,0:T(8,128)S(1)} %bitcast.214), kind=kOutput, calls=%fused_computation.66 | convolution fusion | flops 805306368 | bytes 8421376 | tf_op jit(solution)/shard_map/ij,kjax->kiax/dot_general | solution.py:38
  595.3 9.1 %fusion.30 = f32[32,4,128,64]{2,3,1,0:T(8,128)} fusion(f32[32,64,4,128]{3,0,2,1:T(8,128)S(1)} %copy-done.8, f32[17,64,64]{2,1,0:T(8,128)S(1)} %bitcast.215), kind=kOutput, calls=%fused_computation.69 | convolution fusion | flops 805306368 | bytes 8421376 | tf_op jit(solution)/shard_map/ij,kjax->kiax/dot_general | solution.py:38
  604.4 9.5 %fusion.32 = f32[32,4,128,64]{2,3,1,0:T(8,128)} fusion(f32[32,64,4,128]{3,0,2,1:T(8,128)S(1)} %copy-done.6, f32[17,64,64]{2,1,0:T(8,128)S(1)} %bitcast.216), kind=kOutput, calls=%fused_computation.72 | convolution fusion | flops 805306368 | bytes 8421376 | tf_op jit(solution)/shard_map/ij,kjax->kiax/dot_general | solution.py:38
  614.0 9.1 %fusion.34 = f32[32,4,128,64]{2,3,1,0:T(8,128)} fusion(f32[32,64,4,128]{3,0,2,1:T(8,128)S(1)} %copy-done.4, f32[17,64,64]{2,1,0:T(8,128)S(1)} %bitcast.217), kind=kOutput, calls=%fused_computation.75 | convolution fusion | flops 805306368 | bytes 8421376 | tf_op jit(solution)/shard_map/ij,kjax->kiax/dot_general | solution.py:38
  623.1 9.1 %fusion.36 = f32[32,4,128,64]{2,3,1,0:T(8,128)} fusion(f32[32,64,4,128]{3,0,2,1:T(8,128)S(1)} %get-tuple-element.17, f32[17,64,64]{2,1,0:T(8,128)S(1)} %bitcast.218), kind=kOutput, calls=%fused_computation.78 | convolution fusion | flops 805306368 | bytes 8421376 | tf_op jit(solution)/shard_map/ij,kjax->kiax/dot_general | solution.py:38
  632.2 79.2 %bitcast_add_fusion = f32[32,64,4,128]{3,0,2,1:T(8,128)} fusion(f32[32,64,4,128]{3,0,2,1:T(8,128)S(1)} %copy-done.1, f32[32,4,128,64]{2,3,1,0:T(8,128)} %fusion.22, f32[32,4,128,64]{2,3,1,0:T(8,128)} %fusion.24, f32[32,4,128,64]{2,3,1,0:T(8,128)} %fusion.26, f32[32,4,128,64]{2,3,1,0:T(8,128)} %fusion.28, f32[32,4,128,64]{2,3,1,0:T(8,128)} %fusion.30, ...), kind=kLoop, calls=%fused_computation.55 | loop fusion | flops 17825792 | bytes 79691776 | tf_op jit(solution)/shard_map/add | solution.py:109
  711.4 6.9 copy.229
  (72 shorter events, 42.5 us)
Async XLA Ops:
  295.5 11.1 %copy-start.18 = (s32[64]{0:T(128)S(1)}, s32[64]{0:T(128)}, u32[]{:S(2)}) copy-start(s32[64]{0:T(128)} %param.7) | copy-start | bytes 772
  295.5 11.2 %copy-start.17 = (f32[64]{0:T(128)S(1)}, f32[64]{0:T(128)}, u32[]{:S(2)}) copy-start(f32[64]{0:T(128)} %param.8) | copy-start | bytes 772
  295.5 11.3 %copy-start.19 = (f32[64]{0:T(128)S(1)}, f32[64]{0:T(128)}, u32[]{:S(2)}) copy-start(f32[64]{0:T(128)} %param.10) | copy-start | bytes 772
  295.5 11.3 %copy-start.16 = (s32[64]{0:T(128)S(1)}, s32[64]{0:T(128)}, u32[]{:S(2)}) copy-start(s32[64]{0:T(128)} %param.9) | copy-start | bytes 772
  301.2 94.2 %collective-permute-start = (f32[32,64,4,128]{3,2,1,0:T(4,128)}, f32[32,64,4,128]{3,2,1,0:T(4,128)}, u32[]{:S(2)}, u32[]{:S(2)}) collective-permute-start(f32[32,64,4,128]{3,2,1,0:T(4,128)} %copy.189), channel_id=1, source_target_pairs={{0,1},{1,2},{2,3},{3,4},{4,5},{5,6},{6,7},{7,8},{8,9},{9,10},{10,1... | collective-permute-start | bytes 12582920 | tf_op jit(solution)/shard_map/ppermute | solution.py:20
  304.7 93.5 %collective-permute-start.1 = (f32[32,64,4,128]{3,2,1,0:T(4,128)}, f32[32,64,4,128]{3,2,1,0:T(4,128)}, u32[]{:S(2)}, u32[]{:S(2)}) collective-permute-start(f32[32,64,4,128]{3,2,1,0:T(4,128)} %copy.189), channel_id=1, source_target_pairs={{1,0},{2,1},{3,2},{4,3},{5,4},{6,5},{7,6},{8,7},{9,8},{10,9},{11,1... | collective-permute-start | bytes 12582920 | tf_op jit(solution)/shard_map/ppermute | solution.py:22
  428.3 2.0 copy-start
  430.4 1.8 copy-start.15
  432.0 22.0 %collective-permute-start.2 = (f32[8,64,4,128]{3,0,2,1:T(8,128)}, f32[8,64,4,128]{3,0,2,1:T(8,128)}, u32[]{:S(2)}, u32[]{:S(2)}) collective-permute-start(f32[8,64,4,128]{3,0,2,1:T(8,128)} %get-tuple-element.25), channel_id=1, source_target_pairs={{0,16},{16,0},{1,17},{17,1},{2,18},{18,2},{3,19},{19,3},{4,20},{20... | collective-permute-start | bytes 3145736 | tf_op jit(solution)/shard_map/ppermute | solution.py:20
  443.8 98.4 %collective-permute-start.3 = (f32[8,64,4,128]{3,0,2,1:T(8,128)}, f32[8,64,4,128]{3,0,2,1:T(8,128)}, u32[]{:S(2)}, u32[]{:S(2)}) collective-permute-start(f32[8,64,4,128]{3,0,2,1:T(8,128)} %get-tuple-element.26), channel_id=1, source_target_pairs={{16,0},{0,16},{17,1},{1,17},{18,2},{2,18},{19,3},{3,19},{20,4},{4,... | collective-permute-start | bytes 3145736 | tf_op jit(solution)/shard_map/ppermute | solution.py:22
  445.3 8.7 %copy-start.1 = (f32[32,64,4,128]{3,0,2,1:T(8,128)S(1)}, f32[32,64,4,128]{3,0,2,1:T(8,128)}, u32[]{:S(2)}) copy-start(f32[32,64,4,128]{3,0,2,1:T(8,128)} %copy-done) | copy-start | bytes 12582916
  468.8 9.2 %copy-start.13 = (f32[32,64,4,128]{3,0,2,1:T(8,128)S(1)}, f32[32,64,4,128]{3,0,2,1:T(8,128)}, u32[]{:S(2)}) copy-start(f32[32,64,4,128]{3,0,2,1:T(8,128)} %get-tuple-element.14) | copy-start | bytes 12582916
  477.9 9.1 %copy-start.11 = (f32[32,64,4,128]{3,0,2,1:T(8,128)S(1)}, f32[32,64,4,128]{3,0,2,1:T(8,128)}, u32[]{:S(2)}) copy-start(f32[32,64,4,128]{3,0,2,1:T(8,128)} %get-tuple-element.13) | copy-start | bytes 12582916
  487.1 9.2 %copy-start.9 = (f32[32,64,4,128]{3,0,2,1:T(8,128)S(1)}, f32[32,64,4,128]{3,0,2,1:T(8,128)}, u32[]{:S(2)}) copy-start(f32[32,64,4,128]{3,0,2,1:T(8,128)} %get-tuple-element.12) | copy-start | bytes 12582916
  496.3 9.3 %copy-start.7 = (f32[32,64,4,128]{3,0,2,1:T(8,128)S(1)}, f32[32,64,4,128]{3,0,2,1:T(8,128)}, u32[]{:S(2)}) copy-start(f32[32,64,4,128]{3,0,2,1:T(8,128)} %get-tuple-element.11) | copy-start | bytes 12582916
  505.6 9.1 %copy-start.5 = (f32[32,64,4,128]{3,0,2,1:T(8,128)S(1)}, f32[32,64,4,128]{3,0,2,1:T(8,128)}, u32[]{:S(2)}) copy-start(f32[32,64,4,128]{3,0,2,1:T(8,128)} %get-tuple-element.10) | copy-start | bytes 12582916
  514.7 9.1 %copy-start.3 = (f32[32,64,4,128]{3,0,2,1:T(8,128)S(1)}, f32[32,64,4,128]{3,0,2,1:T(8,128)}, u32[]{:S(2)}) copy-start(f32[32,64,4,128]{3,0,2,1:T(8,128)} %get-tuple-element.9) | copy-start | bytes 12582916
  523.8 9.4 %copy-start.2 = (f32[32,64,4,128]{3,0,2,1:T(8,128)S(1)}, f32[32,64,4,128]{3,0,2,1:T(8,128)}, u32[]{:S(2)}) copy-start(f32[32,64,4,128]{3,0,2,1:T(8,128)} %get-tuple-element.15) | copy-start | bytes 12582916
  556.1 11.7 %copy-start.14 = (f32[32,64,4,128]{3,0,2,1:T(8,128)S(1)}, f32[32,64,4,128]{3,0,2,1:T(8,128)}, u32[]{:S(2)}) copy-start(f32[32,64,4,128]{3,0,2,1:T(8,128)} %get-tuple-element.24) | copy-start | bytes 12582916
  567.7 9.1 %copy-start.12 = (f32[32,64,4,128]{3,0,2,1:T(8,128)S(1)}, f32[32,64,4,128]{3,0,2,1:T(8,128)}, u32[]{:S(2)}) copy-start(f32[32,64,4,128]{3,0,2,1:T(8,128)} %get-tuple-element.22) | copy-start | bytes 12582916
  576.9 9.3 %copy-start.10 = (f32[32,64,4,128]{3,0,2,1:T(8,128)S(1)}, f32[32,64,4,128]{3,0,2,1:T(8,128)}, u32[]{:S(2)}) copy-start(f32[32,64,4,128]{3,0,2,1:T(8,128)} %get-tuple-element.21) | copy-start | bytes 12582916
  586.2 9.1 %copy-start.8 = (f32[32,64,4,128]{3,0,2,1:T(8,128)S(1)}, f32[32,64,4,128]{3,0,2,1:T(8,128)}, u32[]{:S(2)}) copy-start(f32[32,64,4,128]{3,0,2,1:T(8,128)} %get-tuple-element.20) | copy-start | bytes 12582916
  595.3 9.1 %copy-start.6 = (f32[32,64,4,128]{3,0,2,1:T(8,128)S(1)}, f32[32,64,4,128]{3,0,2,1:T(8,128)}, u32[]{:S(2)}) copy-start(f32[32,64,4,128]{3,0,2,1:T(8,128)} %get-tuple-element.19) | copy-start | bytes 12582916
  604.4 9.5 %copy-start.4 = (f32[32,64,4,128]{3,0,2,1:T(8,128)S(1)}, f32[32,64,4,128]{3,0,2,1:T(8,128)}, u32[]{:S(2)}) copy-start(f32[32,64,4,128]{3,0,2,1:T(8,128)} %get-tuple-element.18) | copy-start | bytes 12582916
where the time goes:
time: 724 us; the launch traced here: 718 us
  blocking collectives  246 us (34%)
  matrix products  205 us (28%)
  other arithmetic  112 us (15%)
  waiting for transfers between devices  91.3 us (13%)
  local copies, waits for them, and re-layouts  57 us (8%)
    dot_general x25, matrix products, contract(): jnp.einsum(pattern, operand_a, operand_b, precision=lax.Precision.HIGHEST...  205 us
    all_to_all x1, blocking collectives, body(): lax.all_to_all(coherence, 'pos', split_axis=3, concat_axis=2, tiled=True)  99.1 us
    all_to_all x1, blocking collectives, body(): lax.all_to_all(mixed, 'dir', split_axis=2, concat_axis=1, tiled=True)  97.3 us
    ppermute x2, waiting for transfers between devices, with_halo(): lax.ppermute(tail, axis, [(i, (i + 1) % count) for i in range(ends)])  88.4 us
    add x1, other arithmetic, body(): summed = moved_two + convolve(circulant, extended, band_count)  79.2 us
    all_to_all x1, blocking collectives, finish_bands(): lax.all_to_all(real_part, 'dir', split_axis=0, concat_axis=1, tiled=True)  49.5 us
    concatenate x2, other arithmetic, with_halo(): jnp.concatenate([lax.ppermute(tail, axis, [(i, (i + 1) % count) for i in...  28.5 us
  transfers between devices with their start and end apart: 4, of which 2 were waited for; matrix products, arithmetic and copies ran while one was open for 15% of the time, Pallas kernels for 0%

commit v1 on v0

--- a/solution.py
+++ b/solution.py
@@ -1,12 +1,388 @@
+import functools
 import math
 
 import jax
 import jax.numpy as jnp
+import numpy as np
 from jax import lax
+from jax.experimental import pallas as pl
+from jax.experimental.pallas import tpu as pltpu
 from jax.sharding import PartitionSpec as P
 
 R = 8
 H = 4
+H2 = 16
+
+UP_NEAR = ((4, 1), (5, 0), (5, 1), (6, 0), (6, 1), (7, 0))
+UP_FAR = ((6, 1), (7, 0), (7, 1))
+DOWN_NEAR = ((3, 0), (2, 0), (2, 1), (1, 0), (1, 1), (0, 1))
+DOWN_FAR = ((1, 0), (0, 0), (0, 1))
+HALOS = (UP_NEAR, UP_FAR, DOWN_NEAR, DOWN_FAR)
+PER_SHIFT = 8
+VMEM = pltpu.VMEM
+SMEM = pltpu.SMEM
+
+
+def split_np(table):
+    high = table.astype(jnp.bfloat16)
+    low = (table - high.astype(np.float32)).astype(jnp.bfloat16)
+    return high, low
+
+
+def split(value):
+    high = value.astype(jnp.bfloat16)
+    low = (value - high.astype(jnp.float32)).astype(jnp.bfloat16)
+    return high, low
+
+
+def natural_tables(length):
+    counter = np.arange(length)
+    angles = (counter[:, None] * counter[None, :] % length) * (2.0 * math.pi / length)
+    factor = 1.0 / math.sqrt(length)
+    return np.cos(angles) * factor, np.sin(angles) * factor
+
+
+def first_tables(length, cuts):
+    cos, sin = natural_tables(length)
+    width = length // cuts
+    real, imag = [], []
+    for cut in range(cuts):
+        cols = slice(cut * width, (cut + 1) * width)
+        real += [cos[:, cols], sin[:, cols]]
+        imag += [-sin[:, cols], cos[:, cols]]
+    table = np.concatenate(real + imag, axis=1).astype(np.float32)
+    return np.concatenate(split_np(table), axis=1)
+
+
+def second_tables(length):
+    cos, sin = natural_tables(length)
+    table = np.concatenate([cos, sin], axis=1).astype(np.float32)
+    return np.concatenate(split_np(table), axis=1)
+
+
+def slot_onehot(shift_row, low, stride_shift, stride_repeat):
+    count = shift_row.shape[1]
+    across = jnp.broadcast_to(shift_row, (count, count))
+    down = across.astype(jnp.float32).T.astype(jnp.int32)
+    first = lax.broadcasted_iota(jnp.int32, (count, count), 0)
+    second = lax.broadcasted_iota(jnp.int32, (count, count), 1)
+    same = jnp.where((across == down) & (first < second), 1, 0)
+    repeat = jnp.sum(same, axis=0, keepdims=True)
+    slot = (shift_row - low) * stride_shift + repeat * stride_repeat
+    return first == slot
+
+
+def dot(lhs, rhs):
+    return jnp.dot(lhs, rhs, preferred_element_type=jnp.float32)
+
+
+def transform_kernel(
+    pairs, shift_one, shift_two, fraction_two, table_one, table_two, received,
+    out, up_near, up_far, down_near, down_far, left_one, left_two, weight_near, weight_far, middle,
+):
+    count = 64
+    lanes = out.shape[-1]
+    sources, local = received.shape[0], received.shape[1]
+    groups = sources // pairs
+    onehot_one = jnp.where(slot_onehot(shift_one[...], -H, PER_SHIFT, 1), 1.0, 0.0)
+    picked = dot(onehot_one.astype(jnp.bfloat16), table_one[...]).astype(jnp.bfloat16)
+    for part in range(4):
+        left_one[part * count : (part + 1) * count, :] = picked[:, part * 128 : (part + 1) * 128]
+    hot_two = slot_onehot(shift_two[...], -H2, 1, 2 * H2)
+    onehot_two = jnp.where(hot_two, 1.0, 0.0)
+    picked = dot(onehot_two.astype(jnp.bfloat16), table_two[...]).astype(jnp.bfloat16)
+    left_two[:count, :128] = picked[:, :128]
+    left_two[:count, 128:] = picked[:, :128]
+    left_two[count:, :128] = picked[:, 128:]
+    left_two[count:, 128:] = jnp.zeros((count, 128), jnp.bfloat16)
+    part_two = jnp.sum(
+        jnp.where(hot_two, jnp.broadcast_to(fraction_two[...], hot_two.shape), 0.0),
+        axis=1, keepdims=True,
+    )
+    rows = lax.broadcasted_iota(jnp.int32, (count, lanes), 0)
+    origin = lax.broadcasted_iota(jnp.int32, (count, lanes), 1) - (lax.rem(rows, 2 * H2) - H2)
+    weight_near[...] = jnp.where((origin >= 0) & (origin < lanes), 1.0 - part_two, 0.0)
+    weight_far[...] = jnp.where((origin >= 1) & (origin <= lanes), part_two, 0.0)
+
+    def first(group, carry):
+        for own in range(local):
+            columns = []
+            for row in range(2):
+                blocks = [
+                    received[pair * groups + group, own, part, row]
+                    for pair in range(pairs)
+                    for part in range(2)
+                ]
+                columns.append(jnp.concatenate(blocks, axis=0))
+            both = dot(left_one[...], jnp.concatenate(columns, axis=1))
+            both = both[: 2 * count] + both[2 * count :]
+            start = pl.multiple_of((group * local + own) * 2 * count, 2 * count)
+            for row in range(2):
+                middle[row, pl.ds(start, 2 * count), :] = both[:, row * lanes : (row + 1) * lanes]
+        return carry
+
+    lax.fori_loop(0, groups, first, 0)
+
+    targets = (up_near, up_far, down_near, down_far)
+    for value in range(2 * H):
+
+        def second(item, carry):
+            slot = value * PER_SHIFT + item
+            columns = []
+            for row in range(2):
+                parts = [
+                    middle[row, pl.ds(part * count + slot, count, stride=2 * count), :]
+                    for part in range(2)
+                ]
+                columns.append(jnp.concatenate(parts, axis=0))
+            both = dot(
+                left_two[...],
+                jnp.concatenate(split(jnp.concatenate(columns, axis=1)), axis=0),
+            )
+            both = both[:count] + both[count:]
+            for row in range(2):
+                pieces = []
+                for block in range(count // 8):
+                    piece = both[block * 8 : block * 8 + 8, row * lanes : (row + 1) * lanes]
+                    base = (lanes - H2 + 8 * (block % (2 * H2 // 8))) % lanes
+                    near = pltpu.roll(piece, base, 1, stride=1, stride_axis=0)
+                    far = pltpu.roll(near, 1, 1)
+                    span = slice(block * 8, block * 8 + 8)
+                    pieces.append(near * weight_near[span, :] + far * weight_far[span, :])
+                moved = jnp.concatenate(pieces, axis=0)
+                out[slot, row] = moved
+                for target, wanted in zip(targets, HALOS):
+                    if (value, row) in wanted:
+                        target[wanted.index((value, row)) * PER_SHIFT + item] = moved
+            return carry
+
+        lax.fori_loop(0, PER_SHIFT, second, 0, unroll=2)
+
+
+def scatter_table_kernel(shift_two, kernel, table, rows):
+    count = kernel.shape[1]
+    reach = kernel.shape[0]
+    offsets = lax.broadcasted_iota(jnp.int32, kernel.shape, 0)
+    lags = lax.broadcasted_iota(jnp.int32, kernel.shape, 1)
+    full = kernel[...] + jnp.where((offsets == R) & (lags == 0), 1.0, 0.0)
+    high, low = split(full)
+    lag = lax.broadcasted_iota(jnp.int32, (count, 2 * count), 0)
+    lane = lax.broadcasted_iota(jnp.int32, (count, 2 * count), 1)
+    mirror = jnp.where(lax.rem(lag + lane, count) == 0, 1.0, 0.0).astype(jnp.bfloat16)
+    rows[...] = jnp.zeros(rows.shape, jnp.float32)
+    rows[0, 3 : 3 + reach, :] = dot(high, mirror)
+    rows[1, 3 : 3 + reach, :] = dot(low, mirror)
+    onehot = jnp.where(slot_onehot(shift_two[...], -H2, 1, 2 * H2), 1.0, 0.0).T
+    blank = jnp.zeros((count, count), jnp.float32)
+    choose = jnp.concatenate(
+        [jnp.concatenate([onehot, blank], axis=1), jnp.concatenate([blank, onehot], axis=1)], axis=0
+    ).astype(jnp.bfloat16)
+    left = lane < count
+
+    def circulant(part, index):
+        row = jnp.broadcast_to(rows[part, index : index + 1, :], (8, 2 * count))
+        return jnp.concatenate(
+            [pltpu.roll(row, 8 * block, 1, stride=1, stride_axis=0) for block in range(count // 8)],
+            axis=0,
+        )
+
+    for part in range(2):
+        here = circulant(part, 0)
+        for index in range(reach + 5):
+            there = circulant(part, index + 1)
+            pair = dot(jnp.where(left, here, there).astype(jnp.bfloat16), choose)
+            pair = pair.astype(jnp.bfloat16)
+            here = there
+            for band in range(4):
+                if (index - 3 + band) % 2 == 0 and 0 <= (index - 3 + band) // 2 < 10:
+                    column = (index - 3 + band) // 2 * 128
+                    start = part * 256 + band * count
+                    table[start : start + count, column : column + 128] = pair
+
+
+def scatter_groups(first_group, groups, table, high, low, out):
+    def step(index, carry):
+        start = pl.multiple_of((first_group + index) * 256, 256)
+        both = dot(table[...], high[pl.ds(start, 1280), :])
+        rest = dot(table[:256, :], low[pl.ds(start, 1280), :])
+        total = both[:256] + both[256:] + rest
+        target = pl.multiple_of(index * 256, 256)
+        for row in range(2):
+            out[row, pl.ds(target, 256), :] = total[:, row * 128 : (row + 1) * 128]
+        return carry
+
+    lax.fori_loop(0, groups, step, 0)
+
+
+def shear_kernel(
+    shift_one, fraction_one, table, moved, up_near, up_far, down_near, down_far,
+    high, low, out, order, seen,
+):
+    count = moved.shape[0]
+    for value in range(2 * H):
+        seen[value] = 0
+
+    def place(band, carry):
+        value = shift_one[band] + H
+        repeat = seen[value]
+        order[value * PER_SHIFT + repeat] = band
+        seen[value] = repeat + 1
+        return carry
+
+    lax.fori_loop(0, count, place, 0)
+    sources = (up_near, up_far, down_near, down_far)
+
+    def fetch(value, item, row):
+        if row in (0, 1):
+            return moved[value * PER_SHIFT + item, row]
+        if row < 0:
+            kind, key = (0, (value, row + 2)) if row >= -2 else (1, (value, row + 4))
+        else:
+            kind, key = (2, (value, row - 2)) if row <= 3 else (3, (value, row - 4))
+        return sources[kind][HALOS[kind].index(key) * PER_SHIFT + item]
+
+    for value in range(2 * H):
+        shift = value - H
+
+        def shear(item, carry):
+            band = order[value * PER_SHIFT + item]
+            weight = fraction_one[band]
+            need = {
+                row: fetch(value, item, row)
+                for row in (-shift - 1, -shift, 1 - shift)
+            }
+            full = jnp.concatenate(
+                [
+                    (1.0 - weight) * need[row - shift] + weight * need[row - shift - 1]
+                    for row in range(2)
+                ],
+                axis=1,
+            )
+            top, bottom = split(full)
+
+            def put(index):
+                start = pl.multiple_of(index * count, count)
+                high[pl.ds(start, count), :] = top
+                low[pl.ds(start, count), :] = bottom
+
+            put(band + R)
+
+            @pl.when(band < R)
+            def _():
+                put(band + R + count)
+
+            @pl.when(band >= count - R)
+            def _():
+                put(band + R - count)
+
+            return carry
+
+        lax.fori_loop(0, PER_SHIFT, shear, 0)
+    half = count // 8
+    scatter_groups((1 - lax.axis_index("dir")) * half, half, table, high, low, out)
+
+
+def scatter_kernel_own(table, high, low, out):
+    half = out.shape[1] // 256
+    scatter_groups(lax.axis_index("dir") * half, half, table, high, low, out)
+
+
+def merge_kernel(own, other, out):
+    size = own.shape[1]
+    for d in range(2):
+
+        @pl.when(lax.axis_index("dir") == d)
+        def _():
+            for row in range(2):
+                out[pl.ds(2 * d + row, size, stride=4), :] = own[row]
+                out[pl.ds(2 * (1 - d) + row, size, stride=4), :] = other[row]
+
+
+def vmem(number):
+    return [pl.BlockSpec(memory_space=VMEM)] * number
+
+
+def smem(number):
+    return [pl.BlockSpec(memory_space=SMEM)] * number
+
+
+def fast_body(coherence, shift_first, fraction_first, shift_second, fraction_second, scatter_kernel):
+    f32, bf16 = jnp.float32, jnp.bfloat16
+    shape = jax.ShapeDtypeStruct
+    pairs, places = lax.axis_size("dir"), lax.axis_size("pos")
+    parts, own_first, own_second, cells, lanes = coherence.shape
+    bands = own_first * pairs
+    cut = coherence.reshape(parts, own_first, own_second, places, pairs, 2, lanes)
+    cut = cut.transpose(4, 3, 2, 0, 5, 1, 6)
+    cut = cut.reshape((pairs * places,) + cut.shape[2:])
+    received = lax.all_to_all(cut, ("dir", "pos"), split_axis=0, concat_axis=0, tiled=True)
+
+    row_one, row_two = shift_first.reshape(1, bands), shift_second.reshape(1, bands)
+    halo_shapes = [shape((len(one) * PER_SHIFT, bands, lanes), f32) for one in HALOS]
+    moved, *halos = pl.pallas_call(
+        functools.partial(transform_kernel, pairs),
+        out_shape=[shape((bands, 2, bands, lanes), f32)] + halo_shapes,
+        in_specs=vmem(6),
+        out_specs=vmem(5),
+        scratch_shapes=[
+            VMEM((4 * bands, 2 * bands), bf16),
+            VMEM((2 * bands, 4 * bands), bf16),
+            VMEM((bands, lanes), f32),
+            VMEM((bands, lanes), f32),
+            VMEM((2, 2 * bands * bands, lanes), f32),
+        ],
+        name="transform",
+    )(
+        row_one, row_two, fraction_second.reshape(1, bands),
+        jnp.asarray(first_tables(bands, pairs)), jnp.asarray(second_tables(bands)), received,
+    )
+
+    def place(block):
+        return block % pairs * places + block // pairs
+
+    total = pairs * places
+    arrived = []
+    for halo, step in zip(halos, (1, 2, -1, -2)):
+        hops = [(place(b), place(b + step)) for b in range(total) if 0 <= b + step < total]
+        arrived.append(lax.ppermute(halo, ("dir", "pos"), hops))
+
+    table = pl.pallas_call(
+        scatter_table_kernel,
+        out_shape=shape((512, 1280), bf16),
+        in_specs=vmem(2),
+        out_specs=pl.BlockSpec(memory_space=VMEM),
+        scratch_shapes=[VMEM((2, 32, 2 * bands), f32)],
+        name="scatter_table",
+    )(row_two, scatter_kernel)
+
+    wrapped = (bands + 2 * R) * bands
+    half = bands * bands // 2
+    high, low, away = pl.pallas_call(
+        shear_kernel,
+        out_shape=[shape((wrapped, 2 * lanes), bf16)] * 2 + [shape((2, half, lanes), f32)],
+        in_specs=smem(2) + vmem(6),
+        out_specs=vmem(3),
+        scratch_shapes=[SMEM((bands,), jnp.int32), SMEM((2 * H,), jnp.int32)],
+        name="shear",
+    )(shift_first, fraction_first, table, moved, *arrived)
+    other = lax.ppermute(away, "dir", [(0, 1), (1, 0)])
+    own = pl.pallas_call(
+        scatter_kernel_own,
+        out_shape=shape((2, half, lanes), f32),
+        in_specs=vmem(3),
+        out_specs=pl.BlockSpec(memory_space=VMEM),
+        name="scatter",
+    )(table, high, low)
+    steps = 8
+    merged = pl.pallas_call(
+        merge_kernel,
+        out_shape=shape((half * 4, lanes), f32),
+        grid=(steps,),
+        in_specs=[pl.BlockSpec((2, half // steps, lanes), lambda i: (0, i, 0))] * 2,
+        out_specs=pl.BlockSpec((half * 4 // steps, lanes), lambda i: (i, 0)),
+        name="merge",
+    )(own, other)
+    return merged.reshape(own_first, bands, 4, lanes)
 
 
 def with_halo(cells, sides, width, closed):
@@ -110,8 +486,19 @@
     return summed
 
 
+def fits(mesh, coherence):
+    pairs, places = mesh.shape["dir"], mesh.shape["pos"]
+    parts, first, second, cells, lanes = coherence.shape
+    return (pairs, first, second, cells, lanes) == (2, 64, 64, 4 * places, 128)
+
+
 def solution(mesh):
     placed = (P(None, "dir", "pos", None, None), P(), P(), P(), P(), P())
-    return jax.shard_map(
-        body, mesh=mesh, in_specs=placed, out_specs=P("dir", None, "pos", None), check_vma=False
-    )
+
+    def run(*arrays):
+        chosen = fast_body if fits(mesh, arrays[0]) else body
+        return jax.shard_map(
+            chosen, mesh=mesh, in_specs=placed, out_specs=P("dir", None, "pos", None), check_vma=False
+        )(*arrays)
+
+    return run

time: 724 us -> 279 us (0.39)
  the two profiles are of different devices: /device:TPU:9 before, /device:TPU:0 now
where the time goes in v1:
time: 279 us; the launch traced here: 278 us
  blocking collectives  102 us (37%)
  waiting for transfers between devices  97.2 us (35%)
  Pallas kernels  59.6 us (21%)
  starting transfers between devices  10.1 us (4%)
  local copies, waits for them, and re-layouts  9.54 us (3%)
    all_to_all x1, blocking collectives, fast_body(): lax.all_to_all(cut, ('dir', 'pos'), split_axis=0, concat_axis=0, tiled=True)  102 us
    ppermute x4, waiting for transfers between devices, fast_body(): arrived.append(lax.ppermute(halo, ('dir', 'pos'), hops))  59.2 us
    ppermute x1, waiting for transfers between devices, fast_body(): other = lax.ppermute(away, 'dir', [(0, 1), (1, 0)])  38 us
    pallas_call x1, Pallas kernels, fast_body(): pl.pallas_call(functools.partial(transform_kernel, pairs), out_shape=[sha...  25.8 us
    pallas_call x1, Pallas kernels, fast_body(): pl.pallas_call(shear_kernel, out_shape=[shape((wrapped, 2 * lanes), bf16)...  14.8 us
    pallas_call x1, Pallas kernels, fast_body(): pl.pallas_call(scatter_kernel_own, out_shape=shape((2, half, lanes), f32)...  9.78 us
    ppermute x4, starting transfers between devices, fast_body(): arrived.append(lax.ppermute(halo, ('dir', 'pos'), hops))  9.19 us
    reshape x1, local copies, waits for them, and re-layouts, fast_body(): coherence.reshape(parts, own_first, own_second, places, pairs, 2, lanes)  7.04 us
  transfers between devices with their start and end apart: 5, of which 4 were waited for; matrix products, arithmetic and copies ran while one was open for 0% of the time, Pallas kernels for 4%

profile of v1, /device:TPU:0, one launch (start us, length us, event | category | flops | bytes accessed | tf_op | source)
XLA Modules:
  0.0 278.3 jit_solution(3701202733325067737)
XLA Ops:
  0.0 7.0 %copy.9 = bf16[2,32,4,16,2,2,128]{6,1,5,0,2,3,4:T(8,128)(2,1)S(1)} copy(bf16[2,32,4,16,2,2,128]{6,5,4,3,2,1,0:T(2,128)(2,1)} %bitcast.9) | data formatting | bytes 8388608 | tf_op jit(solution)/shard_map/reshape | solution.py:315
  7.0 101.9 %all_to_all.5.received = bf16[32,4,2,2,32,128]{5,4,3,2,1,0:T(8,128)(2,1)} all-to-all(bf16[32,4,2,2,32,128]{5,4,3,2,1,0:T(8,128)(2,1)S(1)} %bitcast.8), channel_id=1, replica_groups=mesh['dir'=2,'pos'=16] {'dir','pos'}, dimensions={0} | all-to-all | bytes 8388608 | tf_op jit(solution)/shard_map/all_to_all | solution.py:318
  108.9 25.8 %transform.1 = (f32[64,2,64,128]{3,2,1,0:T(8,128)}, f32[48,64,128]{2,1,0:T(8,128)}, f32[24,64,128]{2,1,0:T(8,128)}, f32[48,64,128]{2,1,0:T(8,128)}, f32[24,64,128]{2,1,0:T(8,128)}) custom-call(s32[1,64]{1,0:T(1,128)} %bitcast.12, s32[1,64]{1,0:T(1,128)} %bitcast.10, f32[1,64]{1,0:T(1,128)} %bitcast.13, bf16[64,512]{1,0:T(8,128)(2,1)} %constant.4.clone.table_one, ...), custom_call_target="tpu_custom_call" | custom-call | tf_op jit(solution)/shard_map/transform/pallas_call | solution.py:322
  134.7 2.9 %collective-permute-start = (f32[48,64,128]{2,1,0:T(8,128)}, f32[48,64,128]{2,1,0:T(8,128)S(1)}, u32[]{:S(2)}, u32[]{:S(2)}) collective-permute-start(f32[48,64,128]{2,1,0:T(8,128)} %get-tuple-element.14), channel_id=1, source_target_pairs={{0,16},{16,1},{1,17},{17,2},{2,18},{18,3},{3,19},{19,4},{4,20},{20... | collective-permute-start | bytes 4718600 | tf_op jit(solution)/shard_map/ppermute | solution.py:347
  137.6 1.3 collective-permute-start.2
  138.9 3.7 %collective-permute-start.1 = (f32[24,64,128]{2,1,0:T(8,128)}, f32[24,64,128]{2,1,0:T(8,128)}, u32[]{:S(2)}, u32[]{:S(2)}) collective-permute-start(f32[24,64,128]{2,1,0:T(8,128)} %get-tuple-element.15), channel_id=1, source_target_pairs={{0,1},{16,17},{1,2},{17,18},{2,3},{18,19},{3,4},{19,20},{4,5},{20,... | collective-permute-start | bytes 2359304 | tf_op jit(solution)/shard_map/ppermute | solution.py:347
  142.6 1.3 collective-permute-start.3
  143.9 2.6 scatter_table.1.table
  146.5 0.0 collective-permute-done.1.up_far
  146.5 2.2 collective-permute-done.3.down_far
  148.7 40.7 %collective-permute-done.up_near = f32[48,64,128]{2,1,0:T(8,128)S(1)} collective-permute-done((f32[48,64,128]{2,1,0:T(8,128)}, f32[48,64,128]{2,1,0:T(8,128)S(1)}, u32[]{:S(2)}, u32[]{:S(2)}) %collective-permute-start) | collective-permute-done | bytes 1572896 | tf_op jit(solution)/shard_map/ppermute | solution.py:347
  189.4 0.0 copy-start.1
  189.5 16.3 %collective-permute-done.2.down_near = f32[48,64,128]{2,1,0:T(8,128)S(1)} collective-permute-done((f32[48,64,128]{2,1,0:T(8,128)}, f32[48,64,128]{2,1,0:T(8,128)S(1)}, u32[]{:S(2)}, u32[]{:S(2)}) %collective-permute-start.2) | collective-permute-done | bytes 1572896 | tf_op jit(solution)/shard_map/ppermute | solution.py:347
  205.7 0.0 copy-start.2
  205.7 0.0 copy-done.1
  205.7 1.2 copy-done.2
  206.9 14.8 %shear.1 = (bf16[5120,256]{1,0:T(8,128)(2,1)}, bf16[5120,256]{1,0:T(8,128)(2,1)}, f32[2,2048,128]{2,1,0:T(8,128)}) custom-call(s32[64]{0:T(128)} %shift_one.1, f32[64]{0:T(128)} %fraction_one.1, bf16[512,1280]{1,0:T(8,128)(2,1)} %scatter_table.1.table, f32[64,2,64,128]{3,2,1,0:T(8,128)} %get-tuple-element.13.moved, f32[48,64,128]{2,1,0:T(8,128)} %copy-done.1, ...), custom_call_target="tpu_custom_call" | custom-call | tf_op jit(solution)/shard_map/shear/pallas_call | solution.py:360
  221.7 0.9 collective-permute-start.4
  222.6 9.8 %scatter.1.own = f32[2,2048,128]{2,1,0:T(8,128)} custom-call(bf16[512,1280]{1,0:T(8,128)(2,1)} %scatter_table.1.table, bf16[5120,256]{1,0:T(8,128)(2,1)} %get-tuple-element.18.high, bf16[5120,256]{1,0:T(8,128)(2,1)} %get-tuple-element.19.low), custom_call_target="tpu_custom_call" | custom-call | tf_op jit(solution)/shard_map/scatter/pallas_call | solution.py:369
  232.4 38.0 %collective-permute-done.4.other = f32[2,2048,128]{2,1,0:T(8,128)S(1)} collective-permute-done((f32[2,2048,128]{2,1,0:T(8,128)}, f32[2,2048,128]{2,1,0:T(8,128)S(1)}, u32[]{:S(2)}, u32[]{:S(2)}) %collective-permute-start.4) | collective-permute-done | bytes 2097184 | tf_op jit(solution)/shard_map/ppermute | solution.py:368
  270.4 0.0 copy-start
  270.4 1.3 copy-done
  271.7 6.7 %merge.1 = f32[8192,128]{1,0:T(8,128)} custom-call(f32[2,2048,128]{2,1,0:T(8,128)} %scatter.1.own, f32[2,2048,128]{2,1,0:T(8,128)} %copy-done), custom_call_target="tpu_custom_call" | custom-call | tf_op jit(solution)/shard_map/merge/pallas_call | solution.py:377
Async XLA Ops:
  134.7 54.7 %collective-permute-start = (f32[48,64,128]{2,1,0:T(8,128)}, f32[48,64,128]{2,1,0:T(8,128)S(1)}, u32[]{:S(2)}, u32[]{:S(2)}) collective-permute-start(f32[48,64,128]{2,1,0:T(8,128)} %get-tuple-element.14), channel_id=1, source_target_pairs={{0,16},{16,1},{1,17},{17,2},{2,18},{18,3},{3,19},{19,4},{4,20},{20... | collective-permute-start | bytes 4718600 | tf_op jit(solution)/shard_map/ppermute | solution.py:347
  137.6 68.1 %collective-permute-start.2 = (f32[48,64,128]{2,1,0:T(8,128)}, f32[48,64,128]{2,1,0:T(8,128)S(1)}, u32[]{:S(2)}, u32[]{:S(2)}) collective-permute-start(f32[48,64,128]{2,1,0:T(8,128)} %get-tuple-element.16), channel_id=1, source_target_pairs={{16,0},{1,16},{17,1},{2,17},{18,2},{3,18},{19,3},{4,19},{20,4},{5,... | collective-permute-start | bytes 4718600 | tf_op jit(solution)/shard_map/ppermute | solution.py:347
  138.9 7.6 %collective-permute-start.1 = (f32[24,64,128]{2,1,0:T(8,128)}, f32[24,64,128]{2,1,0:T(8,128)}, u32[]{:S(2)}, u32[]{:S(2)}) collective-permute-start(f32[24,64,128]{2,1,0:T(8,128)} %get-tuple-element.15), channel_id=1, source_target_pairs={{0,1},{16,17},{1,2},{17,18},{2,3},{18,19},{3,4},{19,20},{4,5},{20,... | collective-permute-start | bytes 2359304 | tf_op jit(solution)/shard_map/ppermute | solution.py:347
  142.6 6.1 %collective-permute-start.3 = (f32[24,64,128]{2,1,0:T(8,128)}, f32[24,64,128]{2,1,0:T(8,128)}, u32[]{:S(2)}, u32[]{:S(2)}) collective-permute-start(f32[24,64,128]{2,1,0:T(8,128)} %get-tuple-element.17), channel_id=1, source_target_pairs={{1,0},{17,16},{2,1},{18,17},{3,2},{19,18},{4,3},{20,19},{5,4},{21,... | collective-permute-start | bytes 2359304 | tf_op jit(solution)/shard_map/ppermute | solution.py:347
  189.4 16.3 %copy-start.1 = (f32[48,64,128]{2,1,0:T(8,128)}, f32[48,64,128]{2,1,0:T(8,128)S(1)}, u32[]{:S(2)}) copy-start(f32[48,64,128]{2,1,0:T(8,128)S(1)} %collective-permute-done.up_near) | copy-start | bytes 4718596
  205.7 1.2 copy-start.2
  221.7 48.7 %collective-permute-start.4 = (f32[2,2048,128]{2,1,0:T(8,128)}, f32[2,2048,128]{2,1,0:T(8,128)S(1)}, u32[]{:S(2)}, u32[]{:S(2)}) collective-permute-start(f32[2,2048,128]{2,1,0:T(8,128)} %get-tuple-element.20), channel_id=1, source_target_pairs={{0,16},{16,0},{1,17},{17,1},{2,18},{18,2},{3,19},{19,3},{4,20},{20... | collective-permute-start | bytes 6291464 | tf_op jit(solution)/shard_map/ppermute | solution.py:368
  270.4 1.3 copy-start

commit v2 on v1

--- a/solution.py
+++ b/solution.py
@@ -19,6 +19,9 @@
 DOWN_FAR = ((1, 0), (0, 0), (0, 1))
 HALOS = (UP_NEAR, UP_FAR, DOWN_NEAR, DOWN_FAR)
 PER_SHIFT = 8
+TOP = 32600.0
+FINE = 8.0
+LEAST = 1e-30
 VMEM = pltpu.VMEM
 SMEM = pltpu.SMEM
 
@@ -76,9 +79,20 @@
     return jnp.dot(lhs, rhs, preferred_element_type=jnp.float32)
 
 
+def encode(columns):
+    largest = jnp.maximum(jnp.max(jnp.abs(columns), axis=0, keepdims=True), LEAST)
+    scale = jnp.ceil(jnp.log2(largest) * FINE)
+    codes = jnp.round(columns * (jnp.exp2(scale * (-1.0 / FINE)) * TOP))
+    return codes.astype(jnp.int32).astype(jnp.int16), scale
+
+
+def decode(codes, scale):
+    return codes.astype(jnp.int32).astype(jnp.float32) * (jnp.exp2(scale * (1.0 / FINE)) * (1.0 / TOP))
+
+
 def transform_kernel(
     pairs, shift_one, shift_two, fraction_two, table_one, table_two, received,
-    out, up_near, up_far, down_near, down_far, left_one, left_two, weight_near, weight_far, middle,
+    out, up_near, up_far, down_near, down_far, left_one, left_two, weight_near, weight_far, middle, scales,
 ):
     count = 64
     lanes = out.shape[-1]
@@ -151,12 +165,24 @@
                     pieces.append(near * weight_near[span, :] + far * weight_far[span, :])
                 moved = jnp.concatenate(pieces, axis=0)
                 out[slot, row] = moved
-                for target, wanted in zip(targets, HALOS):
-                    if (value, row) in wanted:
-                        target[wanted.index((value, row)) * PER_SHIFT + item] = moved
+                hits = [
+                    (kind, wanted.index((value, row)))
+                    for kind, wanted in enumerate(HALOS)
+                    if (value, row) in wanted
+                ]
+                if hits:
+                    codes, scale = encode(moved)
+                for kind, index in hits:
+                    place = index * PER_SHIFT + item
+                    start = pl.multiple_of(place * count, count)
+                    targets[kind][pl.ds(start, count), :] = codes
+                    scales[kind, pl.ds(place, 1), :] = scale
             return carry
 
         lax.fori_loop(0, PER_SHIFT, second, 0, unroll=2)
+    for kind, target in enumerate(targets):
+        entries = target.shape[0] // (count + 1)
+        target[entries * count :, :] = scales[kind, :entries, :].astype(jnp.int32).astype(jnp.int16)
 
 
 def scatter_table_kernel(shift_two, kernel, table, rows):
@@ -200,7 +226,7 @@
                     table[start : start + count, column : column + 128] = pair
 
 
-def scatter_groups(first_group, groups, table, high, low, out):
+def scatter_groups(first_group, groups, table, high, low, out, scales=None):
     def step(index, carry):
         start = pl.multiple_of((first_group + index) * 256, 256)
         both = dot(table[...], high[pl.ds(start, 1280), :])
@@ -208,7 +234,14 @@
         total = both[:256] + both[256:] + rest
         target = pl.multiple_of(index * 256, 256)
         for row in range(2):
-            out[row, pl.ds(target, 256), :] = total[:, row * 128 : (row + 1) * 128]
+            part = total[:, row * 128 : (row + 1) * 128]
+            if scales is None:
+                out[row, pl.ds(target, 256), :] = part
+                continue
+            blocks = [encode(part[band * 64 : band * 64 + 64]) for band in range(4)]
+            out[row, pl.ds(target, 256), :] = jnp.concatenate([codes for codes, _ in blocks], axis=0)
+            for band in range(4):
+                scales[row, pl.ds(index * 4 + band, 1), :] = blocks[band][1]
         return carry
 
     lax.fori_loop(0, groups, step, 0)
@@ -216,7 +249,7 @@
 
 def shear_kernel(
     shift_one, fraction_one, table, moved, up_near, up_far, down_near, down_far,
-    high, low, out, order, seen,
+    high, low, out, order, seen, arrived, sent,
 ):
     count = moved.shape[0]
     for value in range(2 * H):
@@ -231,6 +264,10 @@
 
     lax.fori_loop(0, count, place, 0)
     sources = (up_near, up_far, down_near, down_far)
+    for kind, source in enumerate(sources):
+        entries = source.shape[0] // (count + 1)
+        codes = source[entries * count :, :].astype(jnp.int32)
+        arrived[kind, :entries, :] = codes.astype(jnp.float32)
 
     def fetch(value, item, row):
         if row in (0, 1):
@@ -239,7 +276,9 @@
             kind, key = (0, (value, row + 2)) if row >= -2 else (1, (value, row + 4))
         else:
             kind, key = (2, (value, row - 2)) if row <= 3 else (3, (value, row - 4))
-        return sources[kind][HALOS[kind].index(key) * PER_SHIFT + item]
+        place = HALOS[kind].index(key) * PER_SHIFT + item
+        start = pl.multiple_of(place * count, count)
+        return decode(sources[kind][pl.ds(start, count), :], arrived[kind, pl.ds(place, 1), :])
 
     for value in range(2 * H):
         shift = value - H
@@ -279,7 +318,10 @@
 
         lax.fori_loop(0, PER_SHIFT, shear, 0)
     half = count // 8
-    scatter_groups((1 - lax.axis_index("dir")) * half, half, table, high, low, out)
+    scatter_groups((1 - lax.axis_index("dir")) * half, half, table, high, low, out, sent)
+    size = 4 * half * count
+    for row in range(2):
+        out[row, size:, :] = sent[row].astype(jnp.int32).astype(jnp.int16)
 
 
 def scatter_kernel_own(table, high, low, out):
@@ -287,15 +329,22 @@
     scatter_groups(lax.axis_index("dir") * half, half, table, high, low, out)
 
 
-def merge_kernel(own, other, out):
+def merge_kernel(own, other, scale, out, scales):
     size = own.shape[1]
+    bands = size // 64
+    for row in range(2):
+        scales[row] = scale[row].astype(jnp.int32).astype(jnp.float32)
+    step = pl.program_id(0)
     for d in range(2):
 
         @pl.when(lax.axis_index("dir") == d)
         def _():
             for row in range(2):
                 out[pl.ds(2 * d + row, size, stride=4), :] = own[row]
-                out[pl.ds(2 * (1 - d) + row, size, stride=4), :] = other[row]
+                for band in range(bands):
+                    rows = other[row, band * 64 : band * 64 + 64, :]
+                    value = decode(rows, scales[row, pl.ds(step * bands + band, 1), :])
+                    out[pl.ds(2 * (1 - d) + row + band * 256, 64, stride=4), :] = value
 
 
 def vmem(number):
@@ -318,7 +367,7 @@
     received = lax.all_to_all(cut, ("dir", "pos"), split_axis=0, concat_axis=0, tiled=True)
 
     row_one, row_two = shift_first.reshape(1, bands), shift_second.reshape(1, bands)
-    halo_shapes = [shape((len(one) * PER_SHIFT, bands, lanes), f32) for one in HALOS]
+    halo_shapes = [shape((len(one) * PER_SHIFT * (bands + 1), lanes), jnp.int16) for one in HALOS]
     moved, *halos = pl.pallas_call(
         functools.partial(transform_kernel, pairs),
         out_shape=[shape((bands, 2, bands, lanes), f32)] + halo_shapes,
@@ -330,6 +379,7 @@
             VMEM((bands, lanes), f32),
             VMEM((bands, lanes), f32),
             VMEM((2, 2 * bands * bands, lanes), f32),
+            VMEM((4, len(UP_NEAR) * PER_SHIFT, lanes), f32),
         ],
         name="transform",
     )(
@@ -359,10 +409,15 @@
     half = bands * bands // 2
     high, low, away = pl.pallas_call(
         shear_kernel,
-        out_shape=[shape((wrapped, 2 * lanes), bf16)] * 2 + [shape((2, half, lanes), f32)],
+        out_shape=[shape((wrapped, 2 * lanes), bf16)] * 2 + [shape((2, half + bands // 2, lanes), jnp.int16)],
         in_specs=smem(2) + vmem(6),
         out_specs=vmem(3),
-        scratch_shapes=[SMEM((bands,), jnp.int32), SMEM((2 * H,), jnp.int32)],
+        scratch_shapes=[
+            SMEM((bands,), jnp.int32),
+            SMEM((2 * H,), jnp.int32),
+            VMEM((4, len(UP_NEAR) * PER_SHIFT, lanes), f32),
+            VMEM((2, bands // 2, lanes), f32),
+        ],
         name="shear",
     )(shift_first, fraction_first, table, moved, *arrived)
     other = lax.ppermute(away, "dir", [(0, 1), (1, 0)])
@@ -378,10 +433,12 @@
         merge_kernel,
         out_shape=shape((half * 4, lanes), f32),
         grid=(steps,),
-        in_specs=[pl.BlockSpec((2, half // steps, lanes), lambda i: (0, i, 0))] * 2,
+        in_specs=[pl.BlockSpec((2, half // steps, lanes), lambda i: (0, i, 0))] * 2
+        + [pl.BlockSpec((2, bands // 2, lanes), lambda i: (0, half // (bands // 2), 0))],
         out_specs=pl.BlockSpec((half * 4 // steps, lanes), lambda i: (i, 0)),
+        scratch_shapes=[VMEM((2, bands // 2, lanes), f32)],
         name="merge",
-    )(own, other)
+    )(own, other, other)
     return merged.reshape(own_first, bands, 4, lanes)
 
 

time: 279 us -> 223 us (0.80)
  waiting for transfers between devices: 97.2 us -> 42.7 us
    ppermute x4, waiting for transfers between devices: 59.2 us -> 26.8 us  [fast_body(): arrived.append(lax.ppermute(halo, ('dir', 'pos'), hops))]
    ppermute x1, waiting for transfers between devices: 38 us -> 15.9 us  [fast_body(): other = lax.ppermute(away, 'dir', [(0, 1), (1, 0)])]
  transfers between devices with their start and end apart: 5 -> 5, of which waited for: 4 -> 4; matrix products, arithmetic and copies ran while one was open for 0% -> 0% of each run, Pallas kernels for 4% -> 6%
where the time goes in v2:
time: 223 us
  blocking collectives  102 us (46%)
  Pallas kernels  60.1 us (27%)
  waiting for transfers between devices  42.7 us (19%)
  starting transfers between devices  9.22 us (4%)
  local copies, waits for them, and re-layouts  8.91 us (4%)
    all_to_all x1, blocking collectives, fast_body(): lax.all_to_all(cut, ('dir', 'pos'), split_axis=0, concat_axis=0, tiled=True)  102 us
    ppermute x4, waiting for transfers between devices, fast_body(): arrived.append(lax.ppermute(halo, ('dir', 'pos'), hops))  26.8 us
    pallas_call x1, Pallas kernels, fast_body(): pl.pallas_call(functools.partial(transform_kernel, pairs), out_shape=[sha...  26.7 us
    ppermute x1, waiting for transfers between devices, fast_body(): other = lax.ppermute(away, 'dir', [(0, 1), (1, 0)])  15.9 us
    pallas_call x1, Pallas kernels, fast_body(): pl.pallas_call(shear_kernel, out_shape=[shape((wrapped, 2 * lanes), bf16)...  14.6 us
    pallas_call x1, Pallas kernels, fast_body(): pl.pallas_call(scatter_kernel_own, out_shape=shape((2, half, lanes), f32)...  9.73 us
    ppermute x4, starting transfers between devices, fast_body(): arrived.append(lax.ppermute(halo, ('dir', 'pos'), hops))  8.3 us
    reshape x1, local copies, waits for them, and re-layouts, fast_body(): coherence.reshape(parts, own_first, own_second, places, pairs, 2, lanes)  7.04 us
  transfers between devices with their start and end apart: 5, of which 4 were waited for; matrix products, arithmetic and copies ran while one was open for 0% of the time, Pallas kernels for 6%

profile of v2, /device:TPU:0, one launch (start us, length us, event | category | flops | bytes accessed | tf_op | source)
XLA Modules:
  0.0 222.9 jit_solution(14659446330170154656)
XLA Ops:
  0.0 7.0 %copy.9 = bf16[2,32,4,16,2,2,128]{6,1,5,0,2,3,4:T(8,128)(2,1)S(1)} copy(bf16[2,32,4,16,2,2,128]{6,5,4,3,2,1,0:T(2,128)(2,1)} %bitcast.9) | data formatting | bytes 8388608 | tf_op jit(solution)/shard_map/reshape | solution.py:364
  7.0 101.9 %all_to_all.5.received = bf16[32,4,2,2,32,128]{5,4,3,2,1,0:T(8,128)(2,1)} all-to-all(bf16[32,4,2,2,32,128]{5,4,3,2,1,0:T(8,128)(2,1)S(1)} %bitcast.8), channel_id=1, replica_groups=mesh['dir'=2,'pos'=16] {'dir','pos'}, dimensions={0} | all-to-all | bytes 8388608 | tf_op jit(solution)/shard_map/all_to_all | solution.py:367
  108.9 26.7 %transform.1 = (f32[64,2,64,128]{3,2,1,0:T(8,128)}, s16[3120,128]{1,0:T(8,128)(2,1)}, s16[1560,128]{1,0:T(8,128)(2,1)}, s16[3120,128]{1,0:T(8,128)(2,1)}, s16[1560,128]{1,0:T(8,128)(2,1)}) custom-call(s32[1,64]{1,0:T(1,128)} %bitcast.12, s32[1,64]{1,0:T(1,128)} %bitcast.10, f32[1,64]{1,0:T(1,128)} %bitcast.13, bf16[64,512]{1,0:T(8,128)(2,1)} %constant.4.clone.table_one, ...), custom_call_target="tpu_custom_call" | custom-call | tf_op jit(solution)/shard_map/transform/pallas_call | solution.py:371
  135.7 2.8 %collective-permute-start = (s16[3120,128]{1,0:T(8,128)(2,1)}, s16[3120,128]{1,0:T(8,128)(2,1)S(1)}, u32[]{:S(2)}, u32[]{:S(2)}) collective-permute-start(s16[3120,128]{1,0:T(8,128)(2,1)} %get-tuple-element.14), channel_id=1, source_target_pairs={{0,16},{16,1},{1,17},{17,2},{2,18},{18,3},{3,19},{19,4},{4,20},{20... | collective-permute-start | bytes 2396168 | tf_op jit(solution)/shard_map/ppermute | solution.py:397
  138.5 1.3 collective-permute-start.2
  139.8 2.9 %collective-permute-start.1 = (s16[1560,128]{1,0:T(8,128)(2,1)}, s16[1560,128]{1,0:T(8,128)(2,1)S(1)}, u32[]{:S(2)}, u32[]{:S(2)}) collective-permute-start(s16[1560,128]{1,0:T(8,128)(2,1)} %get-tuple-element.15), channel_id=1, source_target_pairs={{0,1},{16,17},{1,2},{17,18},{2,3},{18,19},{3,4},{19,20},{4,5},{20,... | collective-permute-start | bytes 1198088 | tf_op jit(solution)/shard_map/ppermute | solution.py:397
  142.7 1.3 collective-permute-start.3
  144.0 2.6 %scatter_table.1.table = bf16[512,1280]{1,0:T(8,128)(2,1)} custom-call(s32[1,64]{1,0:T(1,128)} %bitcast.11, f32[17,64]{1,0:T(8,128)} %kernel.1), custom_call_target="tpu_custom_call" | custom-call | tf_op jit(solution)/shard_map/scatter_table/pallas_call | solution.py:399
  146.6 0.0 collective-permute-done.1.up_far
  146.6 0.0 copy-start.3
  146.6 2.3 %collective-permute-done.3.down_far = s16[1560,128]{1,0:T(8,128)(2,1)S(1)} collective-permute-done((s16[1560,128]{1,0:T(8,128)(2,1)}, s16[1560,128]{1,0:T(8,128)(2,1)S(1)}, u32[]{:S(2)}, u32[]{:S(2)}) %collective-permute-start.3) | collective-permute-done | bytes 399392 | tf_op jit(solution)/shard_map/ppermute | solution.py:397
  149.0 0.0 copy-start.4
  149.0 16.5 %collective-permute-done.up_near = s16[3120,128]{1,0:T(8,128)(2,1)S(1)} collective-permute-done((s16[3120,128]{1,0:T(8,128)(2,1)}, s16[3120,128]{1,0:T(8,128)(2,1)S(1)}, u32[]{:S(2)}, u32[]{:S(2)}) %collective-permute-start) | collective-permute-done | bytes 798752 | tf_op jit(solution)/shard_map/ppermute | solution.py:397
  165.5 0.0 copy-start.1
  165.5 8.0 %collective-permute-done.2.down_near = s16[3120,128]{1,0:T(8,128)(2,1)S(1)} collective-permute-done((s16[3120,128]{1,0:T(8,128)(2,1)}, s16[3120,128]{1,0:T(8,128)(2,1)S(1)}, u32[]{:S(2)}, u32[]{:S(2)}) %collective-permute-start.2) | collective-permute-done | bytes 798752 | tf_op jit(solution)/shard_map/ppermute | solution.py:397
  173.5 0.0 copy-start.2
  173.5 0.0 copy-done.3
  173.5 0.0 copy-done.4
  173.5 0.0 copy-done.1
  173.5 0.9 copy-done.2
  174.4 14.6 %shear.1 = (bf16[5120,256]{1,0:T(8,128)(2,1)}, bf16[5120,256]{1,0:T(8,128)(2,1)}, s16[2,2080,128]{2,1,0:T(8,128)(2,1)}) custom-call(s32[64]{0:T(128)} %shift_one.1, f32[64]{0:T(128)} %fraction_one.1, bf16[512,1280]{1,0:T(8,128)(2,1)} %scatter_table.1.table, f32[64,2,64,128]{3,2,1,0:T(8,128)} %get-tuple-element.13.moved, s16[3120,128]{1,0:T(8,128)(2,1)} %copy-done.1, ...), custom_call_target="tpu_custom_call" | custom-call | tf_op jit(solution)/shard_map/shear/pallas_call | solution.py:410
  188.9 0.9 collective-permute-start.4
  189.9 9.7 %scatter.1.own = f32[2,2048,128]{2,1,0:T(8,128)} custom-call(bf16[512,1280]{1,0:T(8,128)(2,1)} %scatter_table.1.table, bf16[5120,256]{1,0:T(8,128)(2,1)} %get-tuple-element.18.high, bf16[5120,256]{1,0:T(8,128)(2,1)} %get-tuple-element.19.low), custom_call_target="tpu_custom_call" | custom-call | tf_op jit(solution)/shard_map/scatter/pallas_call | solution.py:424
  199.6 15.9 %collective-permute-done.4.other.scale = s16[2,2080,128]{2,1,0:T(8,128)(2,1)S(1)} collective-permute-done((s16[2,2080,128]{2,1,0:T(8,128)(2,1)}, s16[2,2080,128]{2,1,0:T(8,128)(2,1)S(1)}, u32[]{:S(2)}, u32[]{:S(2)}) %collective-permute-start.4) | collective-permute-done | bytes 1064992 | tf_op jit(solution)/shard_map/ppermute | solution.py:423
  215.5 0.0 copy-start
  215.5 1.0 copy-done
  216.5 6.4 %merge.1 = f32[8192,128]{1,0:T(8,128)} custom-call(f32[2,2048,128]{2,1,0:T(8,128)} %scatter.1.own, s16[2,2080,128]{2,1,0:T(8,128)(2,1)} %copy-done, s16[2,2080,128]{2,1,0:T(8,128)(2,1)} %copy-done), custom_call_target="tpu_custom_call" | custom-call | tf_op jit(solution)/shard_map/merge/pallas_call | solution.py:432
Async XLA Ops:
  135.7 29.8 %collective-permute-start = (s16[3120,128]{1,0:T(8,128)(2,1)}, s16[3120,128]{1,0:T(8,128)(2,1)S(1)}, u32[]{:S(2)}, u32[]{:S(2)}) collective-permute-start(s16[3120,128]{1,0:T(8,128)(2,1)} %get-tuple-element.14), channel_id=1, source_target_pairs={{0,16},{16,1},{1,17},{17,2},{2,18},{18,3},{3,19},{19,4},{4,20},{20... | collective-permute-start | bytes 2396168 | tf_op jit(solution)/shard_map/ppermute | solution.py:397
  138.5 35.0 %collective-permute-start.2 = (s16[3120,128]{1,0:T(8,128)(2,1)}, s16[3120,128]{1,0:T(8,128)(2,1)S(1)}, u32[]{:S(2)}, u32[]{:S(2)}) collective-permute-start(s16[3120,128]{1,0:T(8,128)(2,1)} %get-tuple-element.16), channel_id=1, source_target_pairs={{16,0},{1,16},{17,1},{2,17},{18,2},{3,18},{19,3},{4,19},{20,4},{5,... | collective-permute-start | bytes 2396168 | tf_op jit(solution)/shard_map/ppermute | solution.py:397
  139.8 6.8 %collective-permute-start.1 = (s16[1560,128]{1,0:T(8,128)(2,1)}, s16[1560,128]{1,0:T(8,128)(2,1)S(1)}, u32[]{:S(2)}, u32[]{:S(2)}) collective-permute-start(s16[1560,128]{1,0:T(8,128)(2,1)} %get-tuple-element.15), channel_id=1, source_target_pairs={{0,1},{16,17},{1,2},{17,18},{2,3},{18,19},{3,4},{19,20},{4,5},{20,... | collective-permute-start | bytes 1198088 | tf_op jit(solution)/shard_map/ppermute | solution.py:397
  142.7 6.3 %collective-permute-start.3 = (s16[1560,128]{1,0:T(8,128)(2,1)}, s16[1560,128]{1,0:T(8,128)(2,1)S(1)}, u32[]{:S(2)}, u32[]{:S(2)}) collective-permute-start(s16[1560,128]{1,0:T(8,128)(2,1)} %get-tuple-element.17), channel_id=1, source_target_pairs={{1,0},{17,16},{2,1},{18,17},{3,2},{19,18},{4,3},{20,19},{5,4},{21,... | collective-permute-start | bytes 1198088 | tf_op jit(solution)/shard_map/ppermute | solution.py:397
  146.6 26.9 %copy-start.3 = (s16[1560,128]{1,0:T(8,128)(2,1)}, s16[1560,128]{1,0:T(8,128)(2,1)S(1)}, u32[]{:S(2)}) copy-start(s16[1560,128]{1,0:T(8,128)(2,1)S(1)} %collective-permute-done.1.up_far) | copy-start | bytes 1198084
  149.0 24.5 %copy-start.4 = (s16[1560,128]{1,0:T(8,128)(2,1)}, s16[1560,128]{1,0:T(8,128)(2,1)S(1)}, u32[]{:S(2)}) copy-start(s16[1560,128]{1,0:T(8,128)(2,1)S(1)} %collective-permute-done.3.down_far) | copy-start | bytes 1198084
  165.5 8.0 %copy-start.1 = (s16[3120,128]{1,0:T(8,128)(2,1)}, s16[3120,128]{1,0:T(8,128)(2,1)S(1)}, u32[]{:S(2)}) copy-start(s16[3120,128]{1,0:T(8,128)(2,1)S(1)} %collective-permute-done.up_near) | copy-start | bytes 2396164
  173.5 0.9 copy-start.2
  188.9 26.5 %collective-permute-start.4 = (s16[2,2080,128]{2,1,0:T(8,128)(2,1)}, s16[2,2080,128]{2,1,0:T(8,128)(2,1)S(1)}, u32[]{:S(2)}, u32[]{:S(2)}) collective-permute-start(s16[2,2080,128]{2,1,0:T(8,128)(2,1)} %get-tuple-element.20), channel_id=1, source_target_pairs={{0,16},{16,0},{1,17},{17,1},{2,18},{18,2},{3,19},{19,3},{4,20},{20... | collective-permute-start | bytes 3194888 | tf_op jit(solution)/shard_map/ppermute | solution.py:423
  215.5 1.0 copy-start

commit v3 on v2

--- a/solution.py
+++ b/solution.py
@@ -79,6 +79,15 @@
     return jnp.dot(lhs, rhs, preferred_element_type=jnp.float32)
 
 
+def place_in_line(pair, block):
+    return block // 2 * 4 + (pair + block // 2) % 2 * 2 + block % 2
+
+
+def device_of(line, places):
+    quad, step = line // 4, line % 4
+    return (step // 2 + quad) % 2 * places + quad * 2 + step % 2
+
+
 def encode(columns):
     largest = jnp.maximum(jnp.max(jnp.abs(columns), axis=0, keepdims=True), LEAST)
     scale = jnp.ceil(jnp.log2(largest) * FINE)
@@ -91,13 +100,24 @@
 
 
 def transform_kernel(
-    pairs, shift_one, shift_two, fraction_two, table_one, table_two, received,
+    pairs, shift_one, shift_two, fraction_two, table_one, table_two, source,
     out, up_near, up_far, down_near, down_far, left_one, left_two, weight_near, weight_far, middle, scales,
+    received, stage, load_sem, store_sem,
 ):
     count = 64
     lanes = out.shape[-1]
-    sources, local = received.shape[0], received.shape[1]
-    groups = sources // pairs
+    local = received.shape[1]
+    lines = received.shape[0] // (count // 8)
+    loads = [
+        pltpu.make_async_copy(
+            source.at[pl.ds(block * lines, lines)],
+            received.at[pl.ds(block * lines, lines)],
+            load_sem.at[block],
+        )
+        for block in range(count // 8)
+    ]
+    for load in loads:
+        load.start()
     onehot_one = jnp.where(slot_onehot(shift_one[...], -H, PER_SHIFT, 1), 1.0, 0.0)
     picked = dot(onehot_one.astype(jnp.bfloat16), table_one[...]).astype(jnp.bfloat16)
     for part in range(4):
@@ -118,35 +138,54 @@
     weight_near[...] = jnp.where((origin >= 0) & (origin < lanes), 1.0 - part_two, 0.0)
     weight_far[...] = jnp.where((origin >= 1) & (origin <= lanes), part_two, 0.0)
 
-    def first(group, carry):
-        for own in range(local):
+    chunk = 2 * count * 8
+
+    def first(block, carry):
+        pltpu.make_async_copy(
+            source.at[pl.ds(block * lines, lines)],
+            received.at[pl.ds(block * lines, lines)],
+            load_sem.at[block],
+        ).wait()
+        for index in range(8):
+            group, own = block * (8 // local) + index // local, index % local
             columns = []
             for row in range(2):
                 blocks = [
-                    received[pair * groups + group, own, part, row]
+                    received[place_in_line(pair, group), own, part, row]
                     for pair in range(pairs)
                     for part in range(2)
                 ]
                 columns.append(jnp.concatenate(blocks, axis=0))
             both = dot(left_one[...], jnp.concatenate(columns, axis=1))
             both = both[: 2 * count] + both[2 * count :]
-            start = pl.multiple_of((group * local + own) * 2 * count, 2 * count)
+            start = pl.multiple_of(block * chunk, chunk) + index
             for row in range(2):
-                middle[row, pl.ds(start, 2 * count), :] = both[:, row * lanes : (row + 1) * lanes]
+                middle[row, pl.ds(start, 2 * count, stride=8), :] = both[
+                    :, row * lanes : (row + 1) * lanes
+                ]
         return carry
 
-    lax.fori_loop(0, groups, first, 0)
+    lax.fori_loop(0, count // 8, first, 0)
 
     targets = (up_near, up_far, down_near, down_far)
+    stores = [
+        pltpu.make_async_copy(
+            stage.at[value % 2], out.at[pl.ds(value * PER_SHIFT, PER_SHIFT)], store_sem.at[value]
+        )
+        for value in range(2 * H)
+    ]
     for value in range(2 * H):
+        if value >= 2:
+            stores[value - 2].wait()
 
         def second(item, carry):
             slot = value * PER_SHIFT + item
             columns = []
             for row in range(2):
                 parts = [
-                    middle[row, pl.ds(part * count + slot, count, stride=2 * count), :]
+                    middle[row, pl.ds(pl.multiple_of(block * chunk + (part * count + slot) * 8, 8), 8), :]
                     for part in range(2)
+                    for block in range(count // 8)
                 ]
                 columns.append(jnp.concatenate(parts, axis=0))
             both = dot(
@@ -164,7 +203,7 @@
                     span = slice(block * 8, block * 8 + 8)
                     pieces.append(near * weight_near[span, :] + far * weight_far[span, :])
                 moved = jnp.concatenate(pieces, axis=0)
-                out[slot, row] = moved
+                stage[value % 2, item, row] = moved
                 hits = [
                     (kind, wanted.index((value, row)))
                     for kind, wanted in enumerate(HALOS)
@@ -179,10 +218,13 @@
                     scales[kind, pl.ds(place, 1), :] = scale
             return carry
 
-        lax.fori_loop(0, PER_SHIFT, second, 0, unroll=2)
+        lax.fori_loop(0, PER_SHIFT, second, 0, unroll=4)
+        stores[value].start()
     for kind, target in enumerate(targets):
         entries = target.shape[0] // (count + 1)
         target[entries * count :, :] = scales[kind, :entries, :].astype(jnp.int32).astype(jnp.int16)
+    for store in stores[-2:]:
+        store.wait()
 
 
 def scatter_table_kernel(shift_two, kernel, table, rows):
@@ -226,32 +268,55 @@
                     table[start : start + count, column : column + 128] = pair
 
 
-def scatter_groups(first_group, groups, table, high, low, out, scales=None):
+def scatter_pair(index, first_group, table, high, low, out, scales):
+    start = pl.multiple_of((first_group + index * 2) * 256, 256)
+
+    def window(half):
+        return jnp.concatenate(
+            [half[pl.ds(start, 1280), :], half[pl.ds(start + 256, 1280), :]], axis=1
+        )
+
+    both = dot(table[...], window(high))
+    rest = dot(table[:256, :], window(low))
+    total = both[:256] + both[256:] + rest
+    for member in range(2):
+        target = pl.multiple_of((index * 2 + member) * 256, 256)
+        for row in range(2):
+            column = member * 256 + row * 128
+            part = total[:, column : column + 128]
+            blocks = [encode(part[band * 64 : band * 64 + 64]) for band in range(4)]
+            out[row, pl.ds(target, 256), :] = jnp.concatenate(
+                [codes for codes, _ in blocks], axis=0
+            )
+            for band in range(4):
+                scales[row, pl.ds((index * 2 + member) * 4 + band, 1), :] = blocks[band][1]
+
+
+def scatter_groups(first_group, groups, table, high, low, out, scales):
     def step(index, carry):
-        start = pl.multiple_of((first_group + index) * 256, 256)
-        both = dot(table[...], high[pl.ds(start, 1280), :])
-        rest = dot(table[:256, :], low[pl.ds(start, 1280), :])
-        total = both[:256] + both[256:] + rest
-        target = pl.multiple_of(index * 256, 256)
-        for row in range(2):
-            part = total[:, row * 128 : (row + 1) * 128]
-            if scales is None:
-                out[row, pl.ds(target, 256), :] = part
-                continue
-            blocks = [encode(part[band * 64 : band * 64 + 64]) for band in range(4)]
-            out[row, pl.ds(target, 256), :] = jnp.concatenate([codes for codes, _ in blocks], axis=0)
-            for band in range(4):
-                scales[row, pl.ds(index * 4 + band, 1), :] = blocks[band][1]
+        scatter_pair(index, first_group, table, high, low, out, scales)
         return carry
 
-    lax.fori_loop(0, groups, step, 0)
+    lax.fori_loop(0, groups // 2, step, 0)
 
 
 def shear_kernel(
-    shift_one, fraction_one, table, moved, up_near, up_far, down_near, down_far,
-    high, low, out, order, seen, arrived, sent,
+    shift_one, fraction_one, table_source, source, up_near, up_far, down_near, down_far,
+    high_out, low_out, out, order, seen, arrived, sent, table, moved, high, low, sem, load_sem,
 ):
     count = moved.shape[0]
+    loads = [
+        pltpu.make_async_copy(
+            source.at[pl.ds(value * PER_SHIFT, PER_SHIFT)],
+            moved.at[pl.ds(value * PER_SHIFT, PER_SHIFT)],
+            load_sem.at[value],
+        )
+        for value in range(2 * H)
+    ]
+    table_load = pltpu.make_async_copy(table_source, table, sem.at[0])
+    for load in loads:
+        load.start()
+    table_load.start()
     for value in range(2 * H):
         seen[value] = 0
 
@@ -282,6 +347,7 @@
 
     for value in range(2 * H):
         shift = value - H
+        loads[value].wait()
 
         def shear(item, carry):
             band = order[value * PER_SHIFT + item]
@@ -318,37 +384,114 @@
 
         lax.fori_loop(0, PER_SHIFT, shear, 0)
     half = count // 8
-    scatter_groups((1 - lax.axis_index("dir")) * half, half, table, high, low, out, sent)
-    size = 4 * half * count
+    side = lax.axis_index("dir")
+    first_row = pl.multiple_of(side * (half * 4 * count), half * 4 * count)
+    kept = high_out.shape[0]
+    keeps = [
+        pltpu.make_async_copy(held.at[pl.ds(first_row, kept)], target, sem.at[index + 1])
+        for index, (held, target) in enumerate(((high, high_out), (low, low_out)))
+    ]
+    for keep in keeps:
+        keep.start()
+    table_load.wait()
+    scatter_groups((1 - side) * half, half, table, high, low, out, sent)
+    code_scales(out, sent, 4 * half * count)
+    for keep in keeps:
+        keep.wait()
+
+
+def code_scales(out, sent, size):
     for row in range(2):
         out[row, size:, :] = sent[row].astype(jnp.int32).astype(jnp.int16)
 
 
-def scatter_kernel_own(table, high, low, out):
-    half = out.shape[1] // 256
-    scatter_groups(lax.axis_index("dir") * half, half, table, high, low, out)
-
-
-def merge_kernel(own, other, scale, out, scales):
-    size = own.shape[1]
-    bands = size // 64
-    for row in range(2):
-        scales[row] = scale[row].astype(jnp.int32).astype(jnp.float32)
-    step = pl.program_id(0)
-    for d in range(2):
-
-        @pl.when(lax.axis_index("dir") == d)
+def scatter_kernel_own(table_source, high_source, low_source, out, sent, table, high, low, sem):
+    half = high.shape[0] // 64 - 2 * R
+    table_load = pltpu.make_async_copy(table_source, table, sem.at[0])
+    table_load.start()
+    loads = []
+    for index in range(half // 8):
+        begin, end = (0, 1536) if index == 0 else (1024 + index * 512, 1536 + index * 512)
+        for part, (held, target) in enumerate(((high_source, high), (low_source, low))):
+            load = pltpu.make_async_copy(
+                held.at[pl.ds(begin, end - begin)],
+                target.at[pl.ds(begin, end - begin)],
+                sem.at[1 + index * 2 + part],
+            )
+            load.start()
+            loads.append(load)
+    table_load.wait()
+    for index in range(half // 8):
+        loads[2 * index].wait()
+        loads[2 * index + 1].wait()
+        scatter_pair(index, 0, table, high, low, out, sent)
+    code_scales(out, sent, half // 2 * 64 * 2)
+
+
+def merge_kernel(*refs):
+    pieces, out, codes, scales, stage, load_sem, store_sem = refs[:4], *refs[4:]
+    bands = scales.shape[1]
+    size = bands * 64
+    steps = store_sem.shape[0]
+    width = size // steps
+    block = lax.axis_index("pos")
+    core = lax.rem(block, 2)
+    held_here = lax.rem(lax.axis_index("dir") + lax.div(block, 2) + core, 2) == 0
+
+    def load(piece, slot):
+        for row in range(2):
+            pltpu.make_async_copy(piece.at[row], codes.at[slot, row], load_sem.at[slot, row]).start()
+
+    @pl.when(held_here)
+    def _():
+        load(pieces[0], 0)
+        load(pieces[1], 1)
+
+    @pl.when(jnp.logical_not(held_here))
+    def _():
+        load(pieces[2], 0)
+        load(pieces[3], 1)
+
+    for slot in range(2):
+        for row in range(2):
+            arrived = pltpu.make_async_copy(
+                pieces[0].at[row], codes.at[slot, row], load_sem.at[slot, row]
+            )
+            arrived.wait()
+            scale = codes[slot, row, size : size + bands, :].astype(jnp.int32)
+            scales[slot * 2 + row] = scale.astype(jnp.float32)
+    stores = [
+        pltpu.make_async_copy(
+            stage.at[pl.ds(step * width * 4, width * 4)],
+            out.at[pl.ds(step * width * 4, width * 4)],
+            store_sem.at[step],
+        )
+        for step in range(steps)
+    ]
+    for side in range(2):
+
+        @pl.when(core == side)
         def _():
-            for row in range(2):
-                out[pl.ds(2 * d + row, size, stride=4), :] = own[row]
-                for band in range(bands):
-                    rows = other[row, band * 64 : band * 64 + 64, :]
-                    value = decode(rows, scales[row, pl.ds(step * bands + band, 1), :])
-                    out[pl.ds(2 * (1 - d) + row + band * 256, 64, stride=4), :] = value
+            for step in range(steps):
+                for slot in range(2):
+                    pair = side if slot == 0 else 1 - side
+                    for row in range(2):
+                        for band in range(step * width // 64, (step + 1) * width // 64):
+                            rows = codes[slot, row, band * 64 : band * 64 + 64, :]
+                            value = decode(rows, scales[slot * 2 + row, band : band + 1, :])
+                            stage[pl.ds(2 * pair + row + band * 256, 64, stride=4), :] = value
+                stores[step].start()
+
+    for store in stores:
+        store.wait()
 
 
 def vmem(number):
     return [pl.BlockSpec(memory_space=VMEM)] * number
+
+
+def anywhere(number):
+    return [pl.BlockSpec(memory_space=pl.ANY)] * number
 
 
 def smem(number):
@@ -359,20 +502,23 @@
     f32, bf16 = jnp.float32, jnp.bfloat16
     shape = jax.ShapeDtypeStruct
     pairs, places = lax.axis_size("dir"), lax.axis_size("pos")
-    parts, own_first, own_second, cells, lanes = coherence.shape
+    parts, own_first, own_second, _, lanes = coherence.shape
     bands = own_first * pairs
-    cut = coherence.reshape(parts, own_first, own_second, places, pairs, 2, lanes)
-    cut = cut.transpose(4, 3, 2, 0, 5, 1, 6)
-    cut = cut.reshape((pairs * places,) + cut.shape[2:])
-    received = lax.all_to_all(cut, ("dir", "pos"), split_axis=0, concat_axis=0, tiled=True)
+    total = pairs * places
+    cut = coherence.reshape(parts, own_first, own_second, total, 2, lanes)
+    cut = cut.transpose(3, 2, 0, 4, 1, 5)
+    received = lax.all_to_all(
+        cut, ("dir", "pos"), split_axis=0, concat_axis=0, tiled=True,
+        axis_index_groups=[[device_of(line, places) for line in range(total)]],
+    )
 
     row_one, row_two = shift_first.reshape(1, bands), shift_second.reshape(1, bands)
     halo_shapes = [shape((len(one) * PER_SHIFT * (bands + 1), lanes), jnp.int16) for one in HALOS]
     moved, *halos = pl.pallas_call(
         functools.partial(transform_kernel, pairs),
         out_shape=[shape((bands, 2, bands, lanes), f32)] + halo_shapes,
-        in_specs=vmem(6),
-        out_specs=vmem(5),
+        in_specs=vmem(5) + [pl.BlockSpec(memory_space=pl.ANY)],
+        out_specs=[pl.BlockSpec(memory_space=pl.ANY)] + vmem(4),
         scratch_shapes=[
             VMEM((4 * bands, 2 * bands), bf16),
             VMEM((2 * bands, 4 * bands), bf16),
@@ -380,6 +526,10 @@
             VMEM((bands, lanes), f32),
             VMEM((2, 2 * bands * bands, lanes), f32),
             VMEM((4, len(UP_NEAR) * PER_SHIFT, lanes), f32),
+            VMEM(received.shape, bf16),
+            VMEM((2, PER_SHIFT, 2, bands, lanes), f32),
+            pltpu.SemaphoreType.DMA((bands // 8,)),
+            pltpu.SemaphoreType.DMA((2 * H,)),
         ],
         name="transform",
     )(
@@ -387,10 +537,9 @@
         jnp.asarray(first_tables(bands, pairs)), jnp.asarray(second_tables(bands)), received,
     )
 
-    def place(block):
-        return block % pairs * places + block // pairs
-
-    total = pairs * places
+    def place(line):
+        return device_of(line, places)
+
     arrived = []
     for halo, step in zip(halos, (1, 2, -1, -2)):
         hops = [(place(b), place(b + step)) for b in range(total) if 0 <= b + step < total]
@@ -409,36 +558,63 @@
     half = bands * bands // 2
     high, low, away = pl.pallas_call(
         shear_kernel,
-        out_shape=[shape((wrapped, 2 * lanes), bf16)] * 2 + [shape((2, half + bands // 2, lanes), jnp.int16)],
-        in_specs=smem(2) + vmem(6),
-        out_specs=vmem(3),
+        out_shape=[shape(((bands // 2 + 2 * R) * bands, 2 * lanes), bf16)] * 2
+        + [shape((2, half + bands // 2, lanes), jnp.int16)],
+        in_specs=smem(2) + anywhere(2) + vmem(4),
+        out_specs=anywhere(2) + vmem(1),
         scratch_shapes=[
             SMEM((bands,), jnp.int32),
             SMEM((2 * H,), jnp.int32),
             VMEM((4, len(UP_NEAR) * PER_SHIFT, lanes), f32),
             VMEM((2, bands // 2, lanes), f32),
+            VMEM(table.shape, bf16),
+            VMEM(moved.shape, f32),
+            VMEM((wrapped, 2 * lanes), bf16),
+            VMEM((wrapped, 2 * lanes), bf16),
+            pltpu.SemaphoreType.DMA((3,)),
+            pltpu.SemaphoreType.DMA((2 * H,)),
         ],
         name="shear",
     )(shift_first, fraction_first, table, moved, *arrived)
-    other = lax.ppermute(away, "dir", [(0, 1), (1, 0)])
+    home = [(d, q, c, (d + q) % 2) for d in range(pairs) for q in range(places // 2) for c in range(2)]
+    same = [
+        (d * places + 2 * q + c, (1 - d) * places + 2 * q + b) for d, q, c, b in home if b == c
+    ]
+    cross = [
+        (d * places + 2 * q + c, (1 - d) * places + 2 * q + b) for d, q, c, b in home if b != c
+    ]
+    inside = [(d * places + 2 * q + c, d * places + 2 * q + b) for d, q, c, b in home if b != c]
+    from_same = lax.ppermute(away, ("dir", "pos"), same)
+    from_cross = lax.ppermute(away, ("dir", "pos"), cross)
     own = pl.pallas_call(
         scatter_kernel_own,
-        out_shape=shape((2, half, lanes), f32),
-        in_specs=vmem(3),
+        out_shape=shape((2, half + bands // 2, lanes), jnp.int16),
+        in_specs=anywhere(3),
         out_specs=pl.BlockSpec(memory_space=VMEM),
+        scratch_shapes=[
+            VMEM((2, bands // 2, lanes), f32),
+            VMEM(table.shape, bf16),
+            VMEM(high.shape, bf16),
+            VMEM(low.shape, bf16),
+            pltpu.SemaphoreType.DMA((9,)),
+        ],
         name="scatter",
     )(table, high, low)
-    steps = 8
+    from_inside = lax.ppermute(own, ("dir", "pos"), inside)
     merged = pl.pallas_call(
         merge_kernel,
         out_shape=shape((half * 4, lanes), f32),
-        grid=(steps,),
-        in_specs=[pl.BlockSpec((2, half // steps, lanes), lambda i: (0, i, 0))] * 2
-        + [pl.BlockSpec((2, bands // 2, lanes), lambda i: (0, half // (bands // 2), 0))],
-        out_specs=pl.BlockSpec((half * 4 // steps, lanes), lambda i: (i, 0)),
-        scratch_shapes=[VMEM((2, bands // 2, lanes), f32)],
+        in_specs=anywhere(4),
+        out_specs=pl.BlockSpec(memory_space=pl.ANY),
+        scratch_shapes=[
+            VMEM((2, 2, half + bands // 2, lanes), jnp.int16),
+            VMEM((4, bands // 2, lanes), f32),
+            VMEM((half * 4, lanes), f32),
+            pltpu.SemaphoreType.DMA((2, 2)),
+            pltpu.SemaphoreType.DMA((8,)),
+        ],
         name="merge",
-    )(own, other, other)
+    )(own, from_inside, from_same, from_cross)
     return merged.reshape(own_first, bands, 4, lanes)
 
 
@@ -545,17 +721,19 @@
 
 def fits(mesh, coherence):
     pairs, places = mesh.shape["dir"], mesh.shape["pos"]
-    parts, first, second, cells, lanes = coherence.shape
-    return (pairs, first, second, cells, lanes) == (2, 64, 64, 4 * places, 128)
+    _, first, second, cells, lanes = coherence.shape
+    return 4 * places == second and (pairs, first, second, cells, lanes) == (2, 64, 64, 4 * places, 128)
 
 
 def solution(mesh):
     placed = (P(None, "dir", "pos", None, None), P(), P(), P(), P(), P())
 
     def run(*arrays):
-        chosen = fast_body if fits(mesh, arrays[0]) else body
-        return jax.shard_map(
-            chosen, mesh=mesh, in_specs=placed, out_specs=P("dir", None, "pos", None), check_vma=False
-        )(*arrays)
+        fast = fits(mesh, arrays[0])
+        step = jax.shard_map(
+            fast_body if fast else body,
+            mesh=mesh, in_specs=placed, out_specs=P("dir", None, "pos", None), check_vma=False,
+        )
+        return step(*arrays)
 
     return run

time: 223 us -> 205 us (0.919); the launches traced: 223 us -> 203 us
  Pallas kernels: 60.1 us -> 40.4 us
  waiting for transfers between devices: 42.7 us -> 33.2 us
  starting transfers between devices: 9.22 us -> 18.4 us
    ppermute x4, waiting for transfers between devices: 26.8 us -> 12.9 us  [fast_body(): arrived.append(lax.ppermute(halo, ('dir', 'pos'), hops))]
    pallas_call x1, Pallas kernels: 26.7 us -> 15 us  [fast_body(): pl.pallas_call(functools.partial(transform_kernel, pairs), out_shape=[sha...]
    pallas_call x3, Pallas kernels: 30.7 us -> 22.9 us  [the longest x1 11.3 us: fast_body(): pl.pallas_call(shear_kernel, out_shape=[shape(((bands // 2 + 2 * R) * ban...]
    ppermute x1 -> x3, starting transfers between devices: 0.91 us -> 7.99 us  [the longest x1 5.97 us: fast_body(): from_same = lax.ppermute(away, ('dir', 'pos'), same)]
    ppermute x1 -> x3, waiting for transfers between devices: 15.9 us -> 20.3 us  [the longest x1 20.3 us: fast_body(): from_same = lax.ppermute(away, ('dir', 'pos'), same)]
  transfers between devices with their start and end apart: 5 -> 7, of which waited for: 4 -> 3; matrix products, arithmetic and copies ran while one was open for 0% -> 0% of each run, Pallas kernels for 6% -> 1%
where the time goes in v3:
time: 205 us; the launch traced here: 203 us
  blocking collectives  101 us (49%)
  Pallas kernels  40.4 us (20%)
  waiting for transfers between devices  33.2 us (16%)
  starting transfers between devices  18.4 us (9%)
  local copies, waits for them, and re-layouts  9.31 us (5%)
    all_to_all x1, blocking collectives, fast_body(): lax.all_to_all(cut, ('dir', 'pos'), split_axis=0, concat_axis=0, tiled=Tr...  101 us
    ppermute x1, waiting for transfers between devices, fast_body(): from_same = lax.ppermute(away, ('dir', 'pos'), same)  20.3 us
    pallas_call x1, Pallas kernels, fast_body(): pl.pallas_call(functools.partial(transform_kernel, pairs), out_shape=[sha...  15 us
    ppermute x4, waiting for transfers between devices, fast_body(): arrived.append(lax.ppermute(halo, ('dir', 'pos'), hops))  12.9 us
    pallas_call x1, Pallas kernels, fast_body(): pl.pallas_call(shear_kernel, out_shape=[shape(((bands // 2 + 2 * R) * ban...  11.3 us
    ppermute x4, starting transfers between devices, fast_body(): arrived.append(lax.ppermute(halo, ('dir', 'pos'), hops))  10.4 us
    pallas_call x1, Pallas kernels, fast_body(): pl.pallas_call(scatter_kernel_own, out_shape=shape((2, half + bands // 2,...  7.85 us
    reshape x1, local copies, waits for them, and re-layouts, fast_body(): cut = coherence.reshape(parts, own_first, own_second, total, 2, lanes)  7.04 us
  transfers between devices with their start and end apart: 7, of which 3 were waited for; matrix products, arithmetic and copies ran while one was open for 0% of the time, Pallas kernels for 1%

profile of v3, /device:TPU:0, one launch (start us, length us, event | category | flops | bytes accessed | tf_op | source)
XLA Modules:
  0.0 202.5 jit_solution(10955707752082831225)
XLA Ops:
  0.0 7.0 %copy.14 = bf16[2,32,4,32,2,128]{5,1,4,0,2,3:T(8,128)(2,1)S(1)} copy(bf16[2,32,4,32,2,128]{5,4,3,2,1,0:T(2,128)(2,1)} %bitcast.9) | data formatting | bytes 8388608 | tf_op jit(solution)/shard_map/reshape | solution.py:508
  7.0 100.9 %all_to_all.5.source = bf16[32,4,2,2,32,128]{5,4,3,2,1,0:T(8,128)(2,1)} all-to-all(bf16[32,4,2,2,32,128]{5,4,3,2,1,0:T(8,128)(2,1)S(1)} %bitcast.8), channel_id=1, replica_groups={{0,1,16,17,18,19,2,3,4,5,20,21,22,23,6,7,8,9,24,25,26,27,10,11,12,13,28..., dimensions={0} | all-to-all | bytes 8388608 | tf_op jit(solution)/shard_map/all_to_all | solution.py:510
  107.9 15.0 %transform.1 = (f32[64,2,64,128]{3,2,1,0:T(8,128)}, s16[3120,128]{1,0:T(8,128)(2,1)}, s16[1560,128]{1,0:T(8,128)(2,1)}, s16[3120,128]{1,0:T(8,128)(2,1)}, s16[1560,128]{1,0:T(8,128)(2,1)}) custom-call(s32[1,64]{1,0:T(1,128)} %bitcast.12, s32[1,64]{1,0:T(1,128)} %bitcast.10, f32[1,64]{1,0:T(1,128)} %bitcast.13, bf16[64,512]{1,0:T(8,128)(2,1)} %constant.4.clone.table_one, ...), custom_call_target="tpu_custom_call" | custom-call | tf_op jit(solution)/shard_map/transform/pallas_call | solution.py:517
  122.9 2.1 %collective-permute-start = (s16[3120,128]{1,0:T(8,128)(2,1)}, s16[3120,128]{1,0:T(8,128)(2,1)S(1)}, u32[]{:S(2)}, u32[]{:S(2)}) collective-permute-start(s16[3120,128]{1,0:T(8,128)(2,1)} %get-tuple-element.14), channel_id=1, source_target_pairs={{0,1},{1,16},{16,17},{17,18},{18,19},{19,2},{2,3},{3,4},{4,5},{5,2... | collective-permute-start | bytes 2396168 | tf_op jit(solution)/shard_map/ppermute | solution.py:546
  125.0 1.3 collective-permute-start.2
  126.3 5.6 %collective-permute-start.1 = (s16[1560,128]{1,0:T(8,128)(2,1)}, s16[1560,128]{1,0:T(8,128)(2,1)S(1)}, u32[]{:S(2)}, u32[]{:S(2)}) collective-permute-start(s16[1560,128]{1,0:T(8,128)(2,1)} %get-tuple-element.15), channel_id=1, source_target_pairs={{0,16},{1,17},{16,18},{17,19},{18,2},{19,3},{2,4},{3,5},{4,20},{5,... | collective-permute-start | bytes 1198088 | tf_op jit(solution)/shard_map/ppermute | solution.py:546
  131.9 1.5 collective-permute-start.3
  133.3 2.5 %scatter_table.1.table_source = bf16[512,1280]{1,0:T(8,128)(2,1)} custom-call(s32[1,64]{1,0:T(1,128)} %bitcast.11, f32[17,64]{1,0:T(8,128)} %kernel.1), custom_call_target="tpu_custom_call" | custom-call | tf_op jit(solution)/shard_map/scatter_table/pallas_call | solution.py:548
  135.9 5.9 %collective-permute-done.1.up_far = s16[1560,128]{1,0:T(8,128)(2,1)S(1)} collective-permute-done((s16[1560,128]{1,0:T(8,128)(2,1)}, s16[1560,128]{1,0:T(8,128)(2,1)S(1)}, u32[]{:S(2)}, u32[]{:S(2)}) %collective-permute-start.1) | collective-permute-done | bytes 399392 | tf_op jit(solution)/shard_map/ppermute | solution.py:546
  141.8 0.0 copy-start.5
  141.8 7.0 %collective-permute-done.3.down_far = s16[1560,128]{1,0:T(8,128)(2,1)S(1)} collective-permute-done((s16[1560,128]{1,0:T(8,128)(2,1)}, s16[1560,128]{1,0:T(8,128)(2,1)S(1)}, u32[]{:S(2)}, u32[]{:S(2)}) %collective-permute-start.3) | collective-permute-done | bytes 399392 | tf_op jit(solution)/shard_map/ppermute | solution.py:546
  148.8 0.0 collective-permute-done.up_near
  148.8 0.0 collective-permute-done.2.down_near
  148.8 0.0 copy-start.4
  148.8 0.0 copy-done.5
  148.8 0.7 copy-done.6
  149.5 0.3 copy-done.3
  149.8 0.3 copy-done.4
  150.1 11.3 %shear.1 = (bf16[3072,256]{1,0:T(8,128)(2,1)}, bf16[3072,256]{1,0:T(8,128)(2,1)}, s16[2,2080,128]{2,1,0:T(8,128)(2,1)}) custom-call(s32[64]{0:T(128)} %shift_one.1, f32[64]{0:T(128)} %fraction_one.1, bf16[512,1280]{1,0:T(8,128)(2,1)} %scatter_table.1.table_source, f32[64,2,64,128]{3,2,1,0:T(8,128)} %get-tuple-element.13.source, s16[3120,128]{1,0:T(8,128)(2,1)} %copy-done.3, ...), custom_call_target="tpu_custom_call" | custom-call | tf_op jit(solution)/shard_map/shear/pallas_call | solution.py:559
  161.4 7.9 %scatter.1.refs_0_ = s16[2,2080,128]{2,1,0:T(8,128)(2,1)} custom-call(bf16[512,1280]{1,0:T(8,128)(2,1)} %scatter_table.1.table_source, bf16[3072,256]{1,0:T(8,128)(2,1)} %get-tuple-element.18.high_source, bf16[3072,256]{1,0:T(8,128)(2,1)} %get-tuple-element.19.low_source), custom_call_target="tpu_custom_call" | custom-call | tf_op jit(solution)/shard_map/scatter/pallas_call | solution.py:589
  169.3 1.3 collective-permute-start.4
  170.6 0.7 collective-permute-start.6
  171.3 6.0 %collective-permute-start.5 = (s16[2,2080,128]{2,1,0:T(8,128)(2,1)}, s16[2,2080,128]{2,1,0:T(8,128)(2,1)S(1)}, u32[]{:S(2)}, u32[]{:S(2)}) collective-permute-start(s16[2,2080,128]{2,1,0:T(8,128)(2,1)} %get-tuple-element.20), channel_id=1, source_target_pairs={{0,16},{3,19},{4,20},{7,23},{8,24},{11,27},{12,28},{15,31},{17,1},... | collective-permute-start | bytes 3194888 | tf_op jit(solution)/shard_map/ppermute | solution.py:587
  177.3 0.0 collective-permute-done.4.refs_1_
  177.3 0.0 copy-start
  177.3 0.0 collective-permute-done.6.refs_3_
  177.3 0.0 copy-start.1
  177.3 20.3 %collective-permute-done.5.refs_2_ = s16[2,2080,128]{2,1,0:T(8,128)(2,1)S(1)} collective-permute-done((s16[2,2080,128]{2,1,0:T(8,128)(2,1)}, s16[2,2080,128]{2,1,0:T(8,128)(2,1)S(1)}, u32[]{:S(2)}, u32[]{:S(2)}) %collective-permute-start.5) | collective-permute-done | bytes 1064992 | tf_op jit(solution)/shard_map/ppermute | solution.py:587
  197.7 0.0 copy-done
  197.7 0.0 copy-done.1
  197.7 1.0 copy-done.2
  198.7 3.7 %merge.1 = f32[8192,128]{1,0:T(8,128)} custom-call(s16[2,2080,128]{2,1,0:T(8,128)(2,1)} %scatter.1.refs_0_, s16[2,2080,128]{2,1,0:T(8,128)(2,1)} %copy-done, s16[2,2080,128]{2,1,0:T(8,128)(2,1)} %copy-done.2, s16[2,2080,128]{2,1,0:T(8,128)(2,1)} %copy-done.1), custom_call_target="tpu_custom_call" | custom-call | tf_op jit(solution)/shard_map/merge/pallas_call | solution.py:604
  (3 shorter events, 0.0 us)
Async XLA Ops:
  122.9 25.9 %collective-permute-start = (s16[3120,128]{1,0:T(8,128)(2,1)}, s16[3120,128]{1,0:T(8,128)(2,1)S(1)}, u32[]{:S(2)}, u32[]{:S(2)}) collective-permute-start(s16[3120,128]{1,0:T(8,128)(2,1)} %get-tuple-element.14), channel_id=1, source_target_pairs={{0,1},{1,16},{16,17},{17,18},{18,19},{19,2},{2,3},{3,4},{4,5},{5,2... | collective-permute-start | bytes 2396168 | tf_op jit(solution)/shard_map/ppermute | solution.py:546
  125.0 23.8 %collective-permute-start.2 = (s16[3120,128]{1,0:T(8,128)(2,1)}, s16[3120,128]{1,0:T(8,128)(2,1)S(1)}, u32[]{:S(2)}, u32[]{:S(2)}) collective-permute-start(s16[3120,128]{1,0:T(8,128)(2,1)} %get-tuple-element.16), channel_id=1, source_target_pairs={{1,0},{16,1},{17,16},{18,17},{19,18},{2,19},{3,2},{4,3},{5,4},{20,... | collective-permute-start | bytes 2396168 | tf_op jit(solution)/shard_map/ppermute | solution.py:546
  126.3 15.5 %collective-permute-start.1 = (s16[1560,128]{1,0:T(8,128)(2,1)}, s16[1560,128]{1,0:T(8,128)(2,1)S(1)}, u32[]{:S(2)}, u32[]{:S(2)}) collective-permute-start(s16[1560,128]{1,0:T(8,128)(2,1)} %get-tuple-element.15), channel_id=1, source_target_pairs={{0,16},{1,17},{16,18},{17,19},{18,2},{19,3},{2,4},{3,5},{4,20},{5,... | collective-permute-start | bytes 1198088 | tf_op jit(solution)/shard_map/ppermute | solution.py:546
  131.9 16.9 %collective-permute-start.3 = (s16[1560,128]{1,0:T(8,128)(2,1)}, s16[1560,128]{1,0:T(8,128)(2,1)S(1)}, u32[]{:S(2)}, u32[]{:S(2)}) collective-permute-start(s16[1560,128]{1,0:T(8,128)(2,1)} %get-tuple-element.17), channel_id=1, source_target_pairs={{16,0},{17,1},{18,16},{19,17},{2,18},{3,19},{4,2},{5,3},{20,4},{21... | collective-permute-start | bytes 1198088 | tf_op jit(solution)/shard_map/ppermute | solution.py:546
  141.8 7.0 %copy-start.5 = (s16[1560,128]{1,0:T(8,128)(2,1)}, s16[1560,128]{1,0:T(8,128)(2,1)S(1)}, u32[]{:S(2)}) copy-start(s16[1560,128]{1,0:T(8,128)(2,1)S(1)} %collective-permute-done.1.up_far) | copy-start | bytes 1198084
  148.8 0.7 copy-start.6
  148.8 1.0 copy-start.3
  148.8 1.3 copy-start.4
  169.3 8.0 %collective-permute-start.4 = (s16[2,2080,128]{2,1,0:T(8,128)(2,1)}, s16[2,2080,128]{2,1,0:T(8,128)(2,1)S(1)}, u32[]{:S(2)}, u32[]{:S(2)}) collective-permute-start(s16[2,2080,128]{2,1,0:T(8,128)(2,1)} %scatter.1.refs_0_), channel_id=1, source_target_pairs={{1,0},{2,3},{5,4},{6,7},{9,8},{10,11},{13,12},{14,15},{16,17},{19,... | collective-permute-start | bytes 3194888 | tf_op jit(solution)/shard_map/ppermute | solution.py:603
  170.6 6.7 %collective-permute-start.6 = (s16[2,2080,128]{2,1,0:T(8,128)(2,1)}, s16[2,2080,128]{2,1,0:T(8,128)(2,1)S(1)}, u32[]{:S(2)}, u32[]{:S(2)}) collective-permute-start(s16[2,2080,128]{2,1,0:T(8,128)(2,1)} %get-tuple-element.20), channel_id=1, source_target_pairs={{1,16},{2,19},{5,20},{6,23},{9,24},{10,27},{13,28},{14,31},{16,1},... | collective-permute-start | bytes 3194888 | tf_op jit(solution)/shard_map/ppermute | solution.py:588
  171.3 26.4 %collective-permute-start.5 = (s16[2,2080,128]{2,1,0:T(8,128)(2,1)}, s16[2,2080,128]{2,1,0:T(8,128)(2,1)S(1)}, u32[]{:S(2)}, u32[]{:S(2)}) collective-permute-start(s16[2,2080,128]{2,1,0:T(8,128)(2,1)} %get-tuple-element.20), channel_id=1, source_target_pairs={{0,16},{3,19},{4,20},{7,23},{8,24},{11,27},{12,28},{15,31},{17,1},... | collective-permute-start | bytes 3194888 | tf_op jit(solution)/shard_map/ppermute | solution.py:587
  177.3 20.4 %copy-start = (s16[2,2080,128]{2,1,0:T(8,128)(2,1)}, s16[2,2080,128]{2,1,0:T(8,128)(2,1)S(1)}, u32[]{:S(2)}) copy-start(s16[2,2080,128]{2,1,0:T(8,128)(2,1)S(1)} %collective-permute-done.4.refs_1_) | copy-start | bytes 3194884
  177.3 20.4 %copy-start.1 = (s16[2,2080,128]{2,1,0:T(8,128)(2,1)}, s16[2,2080,128]{2,1,0:T(8,128)(2,1)S(1)}, u32[]{:S(2)}) copy-start(s16[2,2080,128]{2,1,0:T(8,128)(2,1)S(1)} %collective-permute-done.6.refs_3_) | copy-start | bytes 3194884
  197.7 1.0 copy-start.2

commit v4 on v3

--- a/solution.py
+++ b/solution.py
@@ -53,7 +53,7 @@
         cols = slice(cut * width, (cut + 1) * width)
         real += [cos[:, cols], sin[:, cols]]
         imag += [-sin[:, cols], cos[:, cols]]
-    table = np.concatenate(real + imag, axis=1).astype(np.float32)
+    table = np.repeat(np.concatenate(real + imag, axis=1), 2, axis=1).astype(np.float32)
     return np.concatenate(split_np(table), axis=1)
 
 
@@ -63,7 +63,7 @@
     return np.concatenate(split_np(table), axis=1)
 
 
-def slot_onehot(shift_row, low, stride_shift, stride_repeat):
+def slot_onehot(shift_row, low, stride_shift, stride_repeat, copies=1):
     count = shift_row.shape[1]
     across = jnp.broadcast_to(shift_row, (count, count))
     down = across.astype(jnp.float32).T.astype(jnp.int32)
@@ -72,6 +72,9 @@
     same = jnp.where((across == down) & (first < second), 1, 0)
     repeat = jnp.sum(same, axis=0, keepdims=True)
     slot = (shift_row - low) * stride_shift + repeat * stride_repeat
+    if copies == 2:
+        first = lax.broadcasted_iota(jnp.int32, (2 * count, count), 0)
+        first = lax.shift_right_logical(first, 1)
     return first == slot
 
 
@@ -86,6 +89,47 @@
 def device_of(line, places):
     quad, step = line // 4, line % 4
     return (step // 2 + quad) % 2 * places + quad * 2 + step % 2
+
+
+def deal_kernel(source, out, held, sem):
+    taken = lax.broadcasted_iota(jnp.int32, (128, 128), 1)
+    given = lax.broadcasted_iota(jnp.int32, (128, 128), 0)
+    wanted = lax.rem(lax.div(given, 2), 8) * 16 + lax.div(given, 16) * 2 + lax.rem(given, 2)
+    move = jnp.where(taken == wanted, 1.0, 0.0).astype(jnp.bfloat16)
+    parts, firsts, seconds, cells, _ = source.shape
+
+    def load(part, group):
+        span = pl.ds(group * 8, 8)
+        number = part * (firsts // 8) + group
+        return pltpu.make_async_copy(source.at[part, span], held.at[part, span], sem.at[number])
+
+    groups = [(part, group) for part in range(parts) for group in range(firsts // 8)]
+    for part, group in groups:
+        load(part, group).start()
+    for part, group in groups:
+        load(part, group).wait()
+
+        def second(own, carry):
+            for tile in range(0, cells // 16, 2):
+                columns = [
+                    jnp.concatenate(
+                        [
+                            held[part, group * 8 + item, own, member * 16 : member * 16 + 16, :]
+                            for item in range(8)
+                        ],
+                        axis=0,
+                    )
+                    for member in (tile, tile + 1)
+                ]
+                moved = dot(move, jnp.concatenate(columns, axis=1)).astype(jnp.bfloat16)
+                for member in range(2):
+                    for item in range(8):
+                        out[(tile + member) * 8 + item, own, part, group * 16 : group * 16 + 16, :] = (
+                            moved[item * 16 : item * 16 + 16, member * 128 : member * 128 + 128]
+                        )
+            return carry
+
+        lax.fori_loop(0, seconds, second, 0, unroll=2)
 
 
 def encode(columns):
@@ -118,10 +162,18 @@
     ]
     for load in loads:
         load.start()
-    onehot_one = jnp.where(slot_onehot(shift_one[...], -H, PER_SHIFT, 1), 1.0, 0.0)
-    picked = dot(onehot_one.astype(jnp.bfloat16), table_one[...]).astype(jnp.bfloat16)
+    onehot_one = jnp.where(slot_onehot(shift_one[...], -H, PER_SHIFT, 1, copies=2), 1.0, 0.0)
+    picked = dot(onehot_one.astype(jnp.bfloat16), table_one[...])
+    same_row = lax.rem(
+        lax.broadcasted_iota(jnp.int32, picked.shape, 0)
+        + lax.broadcasted_iota(jnp.int32, picked.shape, 1),
+        2,
+    )
+    picked = jnp.where(same_row == 0, picked, 0.0).astype(jnp.bfloat16)
     for part in range(4):
-        left_one[part * count : (part + 1) * count, :] = picked[:, part * 128 : (part + 1) * 128]
+        left_one[part * 2 * count : (part + 1) * 2 * count, :] = picked[
+            :, part * 4 * count : (part + 1) * 4 * count
+        ]
     hot_two = slot_onehot(shift_two[...], -H2, 1, 2 * H2)
     onehot_two = jnp.where(hot_two, 1.0, 0.0)
     picked = dot(onehot_two.astype(jnp.bfloat16), table_two[...]).astype(jnp.bfloat16)
@@ -138,7 +190,7 @@
     weight_near[...] = jnp.where((origin >= 0) & (origin < lanes), 1.0 - part_two, 0.0)
     weight_far[...] = jnp.where((origin >= 1) & (origin <= lanes), part_two, 0.0)
 
-    chunk = 2 * count * 8
+    chunk = 2 * count * 2 * 8
 
     def first(block, carry):
         pltpu.make_async_copy(
@@ -146,22 +198,22 @@
             received.at[pl.ds(block * lines, lines)],
             load_sem.at[block],
         ).wait()
-        for index in range(8):
-            group, own = block * (8 // local) + index // local, index % local
+        for index in range(0, 8, 2):
             columns = []
-            for row in range(2):
+            for member in (index, index + 1):
+                group, own = block * (8 // local) + member // local, member % local
                 blocks = [
-                    received[place_in_line(pair, group), own, part, row]
+                    received[place_in_line(pair, group), own, part]
                     for pair in range(pairs)
                     for part in range(2)
                 ]
                 columns.append(jnp.concatenate(blocks, axis=0))
             both = dot(left_one[...], jnp.concatenate(columns, axis=1))
-            both = both[: 2 * count] + both[2 * count :]
-            start = pl.multiple_of(block * chunk, chunk) + index
-            for row in range(2):
-                middle[row, pl.ds(start, 2 * count, stride=8), :] = both[
-                    :, row * lanes : (row + 1) * lanes
+            both = both[: 4 * count] + both[4 * count :]
+            for member in range(2):
+                start = pl.multiple_of(block * chunk, chunk) + index + member
+                middle[pl.ds(start, 4 * count, stride=8), :] = both[
+                    :, member * lanes : (member + 1) * lanes
                 ]
         return carry
 
@@ -183,7 +235,12 @@
             columns = []
             for row in range(2):
                 parts = [
-                    middle[row, pl.ds(pl.multiple_of(block * chunk + (part * count + slot) * 8, 8), 8), :]
+                    middle[
+                        pl.ds(
+                            pl.multiple_of(block * chunk + ((part * count + slot) * 2 + row) * 8, 8), 8
+                        ),
+                        :,
+                    ]
                     for part in range(2)
                     for block in range(count // 8)
                 ]
@@ -429,7 +486,7 @@
 
 
 def merge_kernel(*refs):
-    pieces, out, codes, scales, stage, load_sem, store_sem = refs[:4], *refs[4:]
+    pieces, out, scales, stage, store_sem = refs[:4], *refs[4:]
     bands = scales.shape[1]
     size = bands * 64
     steps = store_sem.shape[0]
@@ -437,29 +494,6 @@
     block = lax.axis_index("pos")
     core = lax.rem(block, 2)
     held_here = lax.rem(lax.axis_index("dir") + lax.div(block, 2) + core, 2) == 0
-
-    def load(piece, slot):
-        for row in range(2):
-            pltpu.make_async_copy(piece.at[row], codes.at[slot, row], load_sem.at[slot, row]).start()
-
-    @pl.when(held_here)
-    def _():
-        load(pieces[0], 0)
-        load(pieces[1], 1)
-
-    @pl.when(jnp.logical_not(held_here))
-    def _():
-        load(pieces[2], 0)
-        load(pieces[3], 1)
-
-    for slot in range(2):
-        for row in range(2):
-            arrived = pltpu.make_async_copy(
-                pieces[0].at[row], codes.at[slot, row], load_sem.at[slot, row]
-            )
-            arrived.wait()
-            scale = codes[slot, row, size : size + bands, :].astype(jnp.int32)
-            scales[slot * 2 + row] = scale.astype(jnp.float32)
     stores = [
         pltpu.make_async_copy(
             stage.at[pl.ds(step * width * 4, width * 4)],
@@ -469,18 +503,24 @@
         for step in range(steps)
     ]
     for side in range(2):
-
-        @pl.when(core == side)
-        def _():
-            for step in range(steps):
+        for here in range(2):
+            used = pieces[:2] if here else pieces[2:]
+
+            @pl.when((core == side) & (held_here == (here == 1)))
+            def _():
                 for slot in range(2):
-                    pair = side if slot == 0 else 1 - side
                     for row in range(2):
-                        for band in range(step * width // 64, (step + 1) * width // 64):
-                            rows = codes[slot, row, band * 64 : band * 64 + 64, :]
-                            value = decode(rows, scales[slot * 2 + row, band : band + 1, :])
-                            stage[pl.ds(2 * pair + row + band * 256, 64, stride=4), :] = value
-                stores[step].start()
+                        scale = used[slot][row, size : size + bands, :].astype(jnp.int32)
+                        scales[slot * 2 + row] = scale.astype(jnp.float32)
+                for step in range(steps):
+                    for slot in range(2):
+                        pair = side if slot == 0 else 1 - side
+                        for row in range(2):
+                            for band in range(step * width // 64, (step + 1) * width // 64):
+                                rows = used[slot][row, band * 64 : band * 64 + 64, :]
+                                value = decode(rows, scales[slot * 2 + row, band : band + 1, :])
+                                stage[pl.ds(2 * pair + row + band * 256, 64, stride=4), :] = value
+                    stores[step].start()
 
     for store in stores:
         store.wait()
@@ -488,6 +528,14 @@
 
 def vmem(number):
     return [pl.BlockSpec(memory_space=VMEM)] * number
+
+
+def grant(mebibytes):
+    return pltpu.CompilerParams(vmem_limit_bytes=mebibytes << 20)
+
+
+def in_vmem(value):
+    return pltpu.with_memory_space_constraint(value, VMEM)
 
 
 def anywhere(number):
@@ -505,8 +553,19 @@
     parts, own_first, own_second, _, lanes = coherence.shape
     bands = own_first * pairs
     total = pairs * places
-    cut = coherence.reshape(parts, own_first, own_second, total, 2, lanes)
-    cut = cut.transpose(3, 2, 0, 4, 1, 5)
+    cut = pl.pallas_call(
+        deal_kernel,
+        out_shape=shape((total, own_second, parts, own_first * 2, lanes), bf16),
+        in_specs=[pl.BlockSpec(memory_space=pltpu.HBM)],
+        out_specs=pl.BlockSpec(memory_space=VMEM),
+        scratch_shapes=[
+            VMEM(coherence.shape, bf16),
+            pltpu.SemaphoreType.DMA((parts * own_first // 8,)),
+        ],
+        compiler_params=grant(16),
+        name="deal",
+    )(pltpu.with_memory_space_constraint(coherence, pltpu.HBM))
+    cut = in_vmem(cut)
     received = lax.all_to_all(
         cut, ("dir", "pos"), split_axis=0, concat_axis=0, tiled=True,
         axis_index_groups=[[device_of(line, places) for line in range(total)]],
@@ -520,17 +579,18 @@
         in_specs=vmem(5) + [pl.BlockSpec(memory_space=pl.ANY)],
         out_specs=[pl.BlockSpec(memory_space=pl.ANY)] + vmem(4),
         scratch_shapes=[
-            VMEM((4 * bands, 2 * bands), bf16),
+            VMEM((8 * bands, 4 * bands), bf16),
             VMEM((2 * bands, 4 * bands), bf16),
             VMEM((bands, lanes), f32),
             VMEM((bands, lanes), f32),
-            VMEM((2, 2 * bands * bands, lanes), f32),
+            VMEM((4 * bands * bands, lanes), f32),
             VMEM((4, len(UP_NEAR) * PER_SHIFT, lanes), f32),
             VMEM(received.shape, bf16),
             VMEM((2, PER_SHIFT, 2, bands, lanes), f32),
             pltpu.SemaphoreType.DMA((bands // 8,)),
             pltpu.SemaphoreType.DMA((2 * H,)),
         ],
+        compiler_params=grant(26),
         name="transform",
     )(
         row_one, row_two, fraction_second.reshape(1, bands),
@@ -543,7 +603,7 @@
     arrived = []
     for halo, step in zip(halos, (1, 2, -1, -2)):
         hops = [(place(b), place(b + step)) for b in range(total) if 0 <= b + step < total]
-        arrived.append(lax.ppermute(halo, ("dir", "pos"), hops))
+        arrived.append(in_vmem(lax.ppermute(halo, ("dir", "pos"), hops)))
 
     table = pl.pallas_call(
         scatter_table_kernel,
@@ -551,6 +611,7 @@
         in_specs=vmem(2),
         out_specs=pl.BlockSpec(memory_space=VMEM),
         scratch_shapes=[VMEM((2, 32, 2 * bands), f32)],
+        compiler_params=grant(8),
         name="scatter_table",
     )(row_two, scatter_kernel)
 
@@ -574,6 +635,7 @@
             pltpu.SemaphoreType.DMA((3,)),
             pltpu.SemaphoreType.DMA((2 * H,)),
         ],
+        compiler_params=grant(24),
         name="shear",
     )(shift_first, fraction_first, table, moved, *arrived)
     home = [(d, q, c, (d + q) % 2) for d in range(pairs) for q in range(places // 2) for c in range(2)]
@@ -598,23 +660,24 @@
             VMEM(low.shape, bf16),
             pltpu.SemaphoreType.DMA((9,)),
         ],
+        compiler_params=grant(16),
         name="scatter",
     )(table, high, low)
     from_inside = lax.ppermute(own, ("dir", "pos"), inside)
+    pieces = [own] + [in_vmem(piece) for piece in (from_inside, from_same, from_cross)]
     merged = pl.pallas_call(
         merge_kernel,
         out_shape=shape((half * 4, lanes), f32),
-        in_specs=anywhere(4),
+        in_specs=vmem(4),
         out_specs=pl.BlockSpec(memory_space=pl.ANY),
         scratch_shapes=[
-            VMEM((2, 2, half + bands // 2, lanes), jnp.int16),
             VMEM((4, bands // 2, lanes), f32),
             VMEM((half * 4, lanes), f32),
-            pltpu.SemaphoreType.DMA((2, 2)),
             pltpu.SemaphoreType.DMA((8,)),
         ],
+        compiler_params=grant(12),
         name="merge",
-    )(own, from_inside, from_same, from_cross)
+    )(*pieces)
     return merged.reshape(own_first, bands, 4, lanes)
 
 

time: 205 us -> 190 us (0.927)
  local copies, waits for them, and re-layouts: 9.31 us -> 0.05 us
  Pallas kernels: 40.4 us -> 34.6 us
    reshape x1 -> x0, local copies, waits for them, and re-layouts: 7.04 us -> none  [fast_body(): cut = coherence.reshape(parts, own_first, own_second, total, 2, lanes)]
    pallas_call x0 -> x1, Pallas kernels: none -> 4.55 us  [fast_body(): pl.pallas_call(deal_kernel, out_shape=shape((total, own_second, parts, ow...]
    pallas_call x1, Pallas kernels: 15 us -> 12.1 us  [fast_body(): pl.pallas_call(functools.partial(transform_kernel, pairs), out_shape=[sha...]
    pallas_call x1, Pallas kernels: 7.85 us -> 5.4 us  [fast_body(): pl.pallas_call(scatter_kernel_own, out_shape=shape((2, half + bands // 2,...]
    unnamed x14, local copies, waits for them, and re-layouts: 2.27 us -> 0.05 us
  transfers between devices with their start and end apart: 7 -> 7, of which waited for: 3 -> 3; matrix products, arithmetic and copies ran while one was open for 0% -> 0% of each run, Pallas kernels for 1% -> 0%
where the time goes in v4:
time: 190 us; the launch traced here: 189 us
  blocking collectives  101 us (53%)
  waiting for transfers between devices  34.7 us (18%)
  Pallas kernels  34.6 us (18%)
  starting transfers between devices  18.2 us (10%)
    all_to_all x1, blocking collectives, fast_body(): lax.all_to_all(cut, ('dir', 'pos'), split_axis=0, concat_axis=0, tiled=Tr...  101 us
    ppermute x1, waiting for transfers between devices, fast_body(): from_same = lax.ppermute(away, ('dir', 'pos'), same)  20 us
    ppermute x4, waiting for transfers between devices, fast_body(): arrived.append(in_vmem(lax.ppermute(halo, ('dir', 'pos'), hops)))  14.6 us
    pallas_call x1, Pallas kernels, fast_body(): pl.pallas_call(functools.partial(transform_kernel, pairs), out_shape=[sha...  12.1 us
    ppermute x4, starting transfers between devices, fast_body(): arrived.append(in_vmem(lax.ppermute(halo, ('dir', 'pos'), hops)))  10.2 us
    pallas_call x1, Pallas kernels, fast_body(): pl.pallas_call(shear_kernel, out_shape=[shape(((bands // 2 + 2 * R) * ban...  9.68 us
    ppermute x1, starting transfers between devices, fast_body(): from_same = lax.ppermute(away, ('dir', 'pos'), same)  5.97 us
    pallas_call x1, Pallas kernels, fast_body(): pl.pallas_call(scatter_kernel_own, out_shape=shape((2, half + bands // 2,...  5.4 us
  transfers between devices with their start and end apart: 7, of which 3 were waited for; matrix products, arithmetic and copies ran while one was open for 0% of the time, Pallas kernels for 0%

profile of v4, /device:TPU:0, one launch (start us, length us, event | category | flops | bytes accessed | tf_op | source)
XLA Modules:
  0.0 188.5 jit_solution(9189235181601342142)
XLA Ops:
  0.0 4.5 %deal.1 = bf16[32,4,2,64,128]{4,3,2,1,0:T(8,128)(2,1)S(1)} custom-call(bf16[2,32,4,64,128]{4,3,2,1,0:T(8,128)(2,1)} %source.1), custom_call_target="tpu_custom_call" | custom-call | tf_op jit(solution)/shard_map/deal/pallas_call | solution.py:556
  4.6 0.0 copy-start
  4.6 0.0 copy-start.1
  4.6 0.0 copy-start.3
  4.6 0.0 copy-start.4
  4.6 0.0 copy-start.5
  4.6 100.7 %all_to_all.5.source = bf16[32,4,2,64,128]{4,3,2,1,0:T(8,128)(2,1)S(1)} all-to-all(bf16[32,4,2,64,128]{4,3,2,1,0:T(8,128)(2,1)S(1)} %deal.1), channel_id=1, replica_groups={{0,1,16,17,18,19,2,3,4,5,20,21,22,23,6,7,8,9,24,25,26,27,10,11,12,13,28..., dimensions={0} | all-to-all | bytes 8388608 | tf_op jit(solution)/shard_map/all_to_all | solution.py:569
  105.4 0.0 copy-done
  105.4 0.0 copy-done.1
  105.4 0.0 copy-done.4
  105.4 0.0 copy-done.5
  105.4 0.0 copy-start.2
  105.4 0.0 copy-start.6
  105.4 12.1 %transform.1 = (f32[64,2,64,128]{3,2,1,0:T(8,128)S(1)}, s16[3120,128]{1,0:T(8,128)(2,1)S(1)}, s16[1560,128]{1,0:T(8,128)(2,1)S(1)}, s16[3120,128]{1,0:T(8,128)(2,1)S(1)}, s16[1560,128]{1,0:T(8,128)(2,1)S(1)}) custom-call(s32[1,64]{1,0:T(1,128)S(1)} %bitcast.6, s32[1,64]{1,0:T(1,128)S(1)} %bitcast.4, f32[1,64]{1,0:T(1,128)S(1)} %bitcast.7, ...), custom_call_target="tpu_custom_call" | custom-call | tf_op jit(solution)/shard_map/transform/pallas_call | solution.py:576
  117.5 2.1 %collective-permute-start = (s16[3120,128]{1,0:T(8,128)(2,1)S(1)}, s16[3120,128]{1,0:T(8,128)(2,1)S(1)}, u32[]{:S(2)}, u32[]{:S(2)}) collective-permute-start(s16[3120,128]{1,0:T(8,128)(2,1)S(1)} %get-tuple-element.14), channel_id=1, source_target_pairs={{0,1},{1,16},{16,17},{17,18},{18,19},{19,2},{2,3},{3,4},{4,5},{5,2... | collective-permute-start | bytes 2396168 | tf_op jit(solution)/shard_map/ppermute | solution.py:606
  119.6 1.3 collective-permute-start.2
  120.9 5.6 %collective-permute-start.1 = (s16[1560,128]{1,0:T(8,128)(2,1)S(1)}, s16[1560,128]{1,0:T(8,128)(2,1)S(1)}, u32[]{:S(2)}, u32[]{:S(2)}) collective-permute-start(s16[1560,128]{1,0:T(8,128)(2,1)S(1)} %get-tuple-element.15), channel_id=1, source_target_pairs={{0,16},{1,17},{16,18},{17,19},{18,2},{19,3},{2,4},{3,5},{4,20},{5,... | collective-permute-start | bytes 1198088 | tf_op jit(solution)/shard_map/ppermute | solution.py:606
  126.5 1.3 collective-permute-start.3
  127.8 0.8 scatter_table.1.table_source
  128.6 7.5 %collective-permute-done.1.up_far = s16[1560,128]{1,0:T(8,128)(2,1)S(1)} collective-permute-done((s16[1560,128]{1,0:T(8,128)(2,1)S(1)}, s16[1560,128]{1,0:T(8,128)(2,1)S(1)}, u32[]{:S(2)}, u32[]{:S(2)}) %collective-permute-start.1) | collective-permute-done | bytes 399392 | tf_op jit(solution)/shard_map/ppermute | solution.py:606
  136.1 7.1 %collective-permute-done.3.down_far = s16[1560,128]{1,0:T(8,128)(2,1)S(1)} collective-permute-done((s16[1560,128]{1,0:T(8,128)(2,1)S(1)}, s16[1560,128]{1,0:T(8,128)(2,1)S(1)}, u32[]{:S(2)}, u32[]{:S(2)}) %collective-permute-start.3) | collective-permute-done | bytes 399392 | tf_op jit(solution)/shard_map/ppermute | solution.py:606
  143.2 0.0 collective-permute-done.up_near
  143.2 0.0 collective-permute-done.2.down_near
  143.2 9.7 %shear.1 = (bf16[3072,256]{1,0:T(8,128)(2,1)S(1)}, bf16[3072,256]{1,0:T(8,128)(2,1)S(1)}, s16[2,2080,128]{2,1,0:T(8,128)(2,1)S(1)}) custom-call(s32[64]{0:T(128)S(1)} %copy-done.4, f32[64]{0:T(128)S(1)} %copy-done.6, bf16[512,1280]{1,0:T(8,128)(2,1)S(1)} %scatter_table.1.table_source, f32[64,2,64,128]{3,2,1,0:T(8,128)S(1)} %get-tuple-element.13.source, ...), custom_call_target="tpu_custom_call" | custom-call | tf_op jit(solution)/shard_map/shear/pallas_call | solution.py:620
  152.9 5.4 %scatter.1.refs_0_ = s16[2,2080,128]{2,1,0:T(8,128)(2,1)S(1)} custom-call(bf16[512,1280]{1,0:T(8,128)(2,1)S(1)} %scatter_table.1.table_source, bf16[3072,256]{1,0:T(8,128)(2,1)S(1)} %get-tuple-element.18.high_source, bf16[3072,256]{1,0:T(8,128)(2,1)S(1)} %get-tuple-element.19.low_source), custom_call_target="tpu_custom_call" | custom-call | tf_op jit(solution)/shard_map/scatter/pallas_call | solution.py:651
  158.3 1.3 collective-permute-start.4
  159.6 0.7 collective-permute-start.6
  160.3 6.0 %collective-permute-start.5 = (s16[2,2080,128]{2,1,0:T(8,128)(2,1)S(1)}, s16[2,2080,128]{2,1,0:T(8,128)(2,1)S(1)}, u32[]{:S(2)}, u32[]{:S(2)}) collective-permute-start(s16[2,2080,128]{2,1,0:T(8,128)(2,1)S(1)} %get-tuple-element.20), channel_id=1, source_target_pairs={{0,16},{3,19},{4,20},{7,23},{8,24},{11,27},{12,28},{15,31},{17,1},... | collective-permute-start | bytes 3194888 | tf_op jit(solution)/shard_map/ppermute | solution.py:649
  166.3 0.0 collective-permute-done.4.refs_1_
  166.3 0.0 collective-permute-done.6.refs_3_
  166.3 20.0 %collective-permute-done.5.refs_2_ = s16[2,2080,128]{2,1,0:T(8,128)(2,1)S(1)} collective-permute-done((s16[2,2080,128]{2,1,0:T(8,128)(2,1)S(1)}, s16[2,2080,128]{2,1,0:T(8,128)(2,1)S(1)}, u32[]{:S(2)}, u32[]{:S(2)}) %collective-permute-start.5) | collective-permute-done | bytes 1064992 | tf_op jit(solution)/shard_map/ppermute | solution.py:649
  186.4 2.2 %merge.1 = f32[8192,128]{1,0:T(8,128)} custom-call(s16[2,2080,128]{2,1,0:T(8,128)(2,1)S(1)} %scatter.1.refs_0_, s16[2,2080,128]{2,1,0:T(8,128)(2,1)S(1)} %collective-permute-done.4.refs_1_, s16[2,2080,128]{2,1,0:T(8,128)(2,1)S(1)} %collective-permute-done.5.refs_2_, s16[2,2080,128]{2,1,0:T(8,128)(2,1)S(1)} %collective-permute-done.6.refs_3_), custom_call_target="tpu_custom_call" | custom-call | tf_op jit(solution)/shard_map/merge/pallas_call | solution.py:668
  (3 shorter events, 0.0 us)
Async XLA Ops:
  4.6 100.8 %copy-start = (bf16[64,1024]{1,0:T(8,128)(2,1)S(1)}, bf16[64,1024]{1,0:T(8,128)(2,1)}, u32[]{:S(2)}) copy-start(bf16[64,1024]{1,0:T(8,128)(2,1)} %constant.4.clone.table_one) | copy-start | bytes 393220
  4.6 100.8 %copy-start.1 = (bf16[64,256]{1,0:T(8,128)(2,1)S(1)}, bf16[64,256]{1,0:T(8,128)(2,1)}, u32[]{:S(2)}) copy-start(bf16[64,256]{1,0:T(8,128)(2,1)} %constant.5.clone.table_two) | copy-start | bytes 98308
  4.6 100.8 %copy-start.3 = (s32[64]{0:T(128)S(1)}, s32[64]{0:T(128)}, u32[]{:S(2)}) copy-start(s32[64]{0:T(128)} %param.11) | copy-start | bytes 772
  4.6 100.8 %copy-start.4 = (s32[64]{0:T(128)S(1)}, s32[64]{0:T(128)}, u32[]{:S(2)}) copy-start(s32[64]{0:T(128)} %shift_one.1) | copy-start | bytes 772
  4.6 100.8 %copy-start.5 = (f32[64]{0:T(128)S(1)}, f32[64]{0:T(128)}, u32[]{:S(2)}) copy-start(f32[64]{0:T(128)} %param.12) | copy-start | bytes 772
  105.4 22.4 %copy-start.2 = (f32[17,64]{1,0:T(8,128)S(1)}, f32[17,64]{1,0:T(8,128)}, u32[]{:S(2)}) copy-start(f32[17,64]{1,0:T(8,128)} %kernel.1) | copy-start | bytes 13060
  105.4 37.8 %copy-start.6 = (f32[64]{0:T(128)S(1)}, f32[64]{0:T(128)}, u32[]{:S(2)}) copy-start(f32[64]{0:T(128)} %fraction_one.1) | copy-start | bytes 772
  117.5 25.7 %collective-permute-start = (s16[3120,128]{1,0:T(8,128)(2,1)S(1)}, s16[3120,128]{1,0:T(8,128)(2,1)S(1)}, u32[]{:S(2)}, u32[]{:S(2)}) collective-permute-start(s16[3120,128]{1,0:T(8,128)(2,1)S(1)} %get-tuple-element.14), channel_id=1, source_target_pairs={{0,1},{1,16},{16,17},{17,18},{18,19},{19,2},{2,3},{3,4},{4,5},{5,2... | collective-permute-start | bytes 2396168 | tf_op jit(solution)/shard_map/ppermute | solution.py:606
  119.6 23.6 %collective-permute-start.2 = (s16[3120,128]{1,0:T(8,128)(2,1)S(1)}, s16[3120,128]{1,0:T(8,128)(2,1)S(1)}, u32[]{:S(2)}, u32[]{:S(2)}) collective-permute-start(s16[3120,128]{1,0:T(8,128)(2,1)S(1)} %get-tuple-element.16), channel_id=1, source_target_pairs={{1,0},{16,1},{17,16},{18,17},{19,18},{2,19},{3,2},{4,3},{5,4},{20,... | collective-permute-start | bytes 2396168 | tf_op jit(solution)/shard_map/ppermute | solution.py:606
  120.9 15.2 %collective-permute-start.1 = (s16[1560,128]{1,0:T(8,128)(2,1)S(1)}, s16[1560,128]{1,0:T(8,128)(2,1)S(1)}, u32[]{:S(2)}, u32[]{:S(2)}) collective-permute-start(s16[1560,128]{1,0:T(8,128)(2,1)S(1)} %get-tuple-element.15), channel_id=1, source_target_pairs={{0,16},{1,17},{16,18},{17,19},{18,2},{19,3},{2,4},{3,5},{4,20},{5,... | collective-permute-start | bytes 1198088 | tf_op jit(solution)/shard_map/ppermute | solution.py:606
  126.5 16.7 %collective-permute-start.3 = (s16[1560,128]{1,0:T(8,128)(2,1)S(1)}, s16[1560,128]{1,0:T(8,128)(2,1)S(1)}, u32[]{:S(2)}, u32[]{:S(2)}) collective-permute-start(s16[1560,128]{1,0:T(8,128)(2,1)S(1)} %get-tuple-element.17), channel_id=1, source_target_pairs={{16,0},{17,1},{18,16},{19,17},{2,18},{3,19},{4,2},{5,3},{20,4},{21... | collective-permute-start | bytes 1198088 | tf_op jit(solution)/shard_map/ppermute | solution.py:606
  158.3 8.0 %collective-permute-start.4 = (s16[2,2080,128]{2,1,0:T(8,128)(2,1)S(1)}, s16[2,2080,128]{2,1,0:T(8,128)(2,1)S(1)}, u32[]{:S(2)}, u32[]{:S(2)}) collective-permute-start(s16[2,2080,128]{2,1,0:T(8,128)(2,1)S(1)} %scatter.1.refs_0_), channel_id=1, source_target_pairs={{1,0},{2,3},{5,4},{6,7},{9,8},{10,11},{13,12},{14,15},{16,17},{19,... | collective-permute-start | bytes 3194888 | tf_op jit(solution)/shard_map/ppermute | solution.py:666
  159.6 6.7 %collective-permute-start.6 = (s16[2,2080,128]{2,1,0:T(8,128)(2,1)S(1)}, s16[2,2080,128]{2,1,0:T(8,128)(2,1)S(1)}, u32[]{:S(2)}, u32[]{:S(2)}) collective-permute-start(s16[2,2080,128]{2,1,0:T(8,128)(2,1)S(1)} %get-tuple-element.20), channel_id=1, source_target_pairs={{1,16},{2,19},{5,20},{6,23},{9,24},{10,27},{13,28},{14,31},{16,1},... | collective-permute-start | bytes 3194888 | tf_op jit(solution)/shard_map/ppermute | solution.py:650
  160.3 26.0 %collective-permute-start.5 = (s16[2,2080,128]{2,1,0:T(8,128)(2,1)S(1)}, s16[2,2080,128]{2,1,0:T(8,128)(2,1)S(1)}, u32[]{:S(2)}, u32[]{:S(2)}) collective-permute-start(s16[2,2080,128]{2,1,0:T(8,128)(2,1)S(1)} %get-tuple-element.20), channel_id=1, source_target_pairs={{0,16},{3,19},{4,20},{7,23},{8,24},{11,27},{12,28},{15,31},{17,1},... | collective-permute-start | bytes 3194888 | tf_op jit(solution)/shard_map/ppermute | solution.py:649

commit v5 on v4

--- a/solution.py
+++ b/solution.py
@@ -217,7 +217,7 @@
                 ]
         return carry
 
-    lax.fori_loop(0, count // 8, first, 0)
+    lax.fori_loop(0, count // 8, first, 0, unroll=2)
 
     targets = (up_near, up_far, down_near, down_far)
     stores = [
@@ -275,7 +275,7 @@
                     scales[kind, pl.ds(place, 1), :] = scale
             return carry
 
-        lax.fori_loop(0, PER_SHIFT, second, 0, unroll=4)
+        lax.fori_loop(0, PER_SHIFT, second, 0, unroll=8)
         stores[value].start()
     for kind, target in enumerate(targets):
         entries = target.shape[0] // (count + 1)
@@ -354,12 +354,12 @@
         scatter_pair(index, first_group, table, high, low, out, scales)
         return carry
 
-    lax.fori_loop(0, groups // 2, step, 0)
+    lax.fori_loop(0, groups // 2, step, 0, unroll=4)
 
 
 def shear_kernel(
-    shift_one, fraction_one, table_source, source, up_near, up_far, down_near, down_far,
-    high_out, low_out, out, order, seen, arrived, sent, table, moved, high, low, sem, load_sem,
+    shift_one, fraction_one, table, source, up_near, up_far, down_near, down_far,
+    high, low, out, order, seen, arrived, sent, moved, load_sem,
 ):
     count = moved.shape[0]
     loads = [
@@ -370,10 +370,8 @@
         )
         for value in range(2 * H)
     ]
-    table_load = pltpu.make_async_copy(table_source, table, sem.at[0])
     for load in loads:
         load.start()
-    table_load.start()
     for value in range(2 * H):
         seen[value] = 0
 
@@ -439,54 +437,28 @@
 
             return carry
 
-        lax.fori_loop(0, PER_SHIFT, shear, 0)
-    half = count // 8
-    side = lax.axis_index("dir")
-    first_row = pl.multiple_of(side * (half * 4 * count), half * 4 * count)
-    kept = high_out.shape[0]
-    keeps = [
-        pltpu.make_async_copy(held.at[pl.ds(first_row, kept)], target, sem.at[index + 1])
-        for index, (held, target) in enumerate(((high, high_out), (low, low_out)))
-    ]
-    for keep in keeps:
-        keep.start()
-    table_load.wait()
-    scatter_groups((1 - side) * half, half, table, high, low, out, sent)
-    code_scales(out, sent, 4 * half * count)
-    for keep in keeps:
-        keep.wait()
-
-
-def code_scales(out, sent, size):
+        lax.fori_loop(0, PER_SHIFT, shear, 0, unroll=4)
+    scatter_band(1 - lax.axis_index("dir"), 0, table, high, low, out, sent)
+
+
+def scatter_band(side, first_group, table, high, low, out, sent):
+    bands = sent.shape[1]
+    first = side * (high.shape[0] // 64 - 2 * R) // 8 + first_group
+    scatter_groups(first, bands // 4, table, high, low, out, sent)
     for row in range(2):
-        out[row, size:, :] = sent[row].astype(jnp.int32).astype(jnp.int16)
-
-
-def scatter_kernel_own(table_source, high_source, low_source, out, sent, table, high, low, sem):
-    half = high.shape[0] // 64 - 2 * R
-    table_load = pltpu.make_async_copy(table_source, table, sem.at[0])
-    table_load.start()
-    loads = []
-    for index in range(half // 8):
-        begin, end = (0, 1536) if index == 0 else (1024 + index * 512, 1536 + index * 512)
-        for part, (held, target) in enumerate(((high_source, high), (low_source, low))):
-            load = pltpu.make_async_copy(
-                held.at[pl.ds(begin, end - begin)],
-                target.at[pl.ds(begin, end - begin)],
-                sem.at[1 + index * 2 + part],
-            )
-            load.start()
-            loads.append(load)
-    table_load.wait()
-    for index in range(half // 8):
-        loads[2 * index].wait()
-        loads[2 * index + 1].wait()
-        scatter_pair(index, 0, table, high, low, out, sent)
-    code_scales(out, sent, half // 2 * 64 * 2)
+        out[row, bands * 64 :, :] = sent[row].astype(jnp.int32).astype(jnp.int16)
+
+
+def scatter_away_kernel(table, high, low, out, sent):
+    scatter_band(1 - lax.axis_index("dir"), sent.shape[1] // 4, table, high, low, out, sent)
+
+
+def scatter_own_kernel(table, high, low, out, sent):
+    scatter_band(lax.axis_index("dir"), 0, table, high, low, out, sent)
 
 
 def merge_kernel(*refs):
-    pieces, out, scales, stage, store_sem = refs[:4], *refs[4:]
+    local, across, out, scales, stage, store_sem = refs[:2], refs[2:6], *refs[6:]
     bands = scales.shape[1]
     size = bands * 64
     steps = store_sem.shape[0]
@@ -504,20 +476,24 @@
     ]
     for side in range(2):
         for here in range(2):
-            used = pieces[:2] if here else pieces[2:]
+            used = ((local[0],), (local[1],)) if here else (across[:2], across[2:])
+            share = bands // len(used[0])
 
             @pl.when((core == side) & (held_here == (here == 1)))
             def _():
                 for slot in range(2):
                     for row in range(2):
-                        scale = used[slot][row, size : size + bands, :].astype(jnp.int32)
-                        scales[slot * 2 + row] = scale.astype(jnp.float32)
+                        for index, piece in enumerate(used[slot]):
+                            scale = piece[row, share * 64 : share * 65, :].astype(jnp.int32)
+                            span = slice(index * share, (index + 1) * share)
+                            scales[slot * 2 + row, span, :] = scale.astype(jnp.float32)
                 for step in range(steps):
                     for slot in range(2):
                         pair = side if slot == 0 else 1 - side
                         for row in range(2):
                             for band in range(step * width // 64, (step + 1) * width // 64):
-                                rows = used[slot][row, band * 64 : band * 64 + 64, :]
+                                begin = band % share * 64
+                                rows = used[slot][band // share][row, begin : begin + 64, :]
                                 value = decode(rows, scales[slot * 2 + row, band : band + 1, :])
                                 stage[pl.ds(2 * pair + row + band * 256, 64, stride=4), :] = value
                     stores[step].start()
@@ -600,10 +576,10 @@
     def place(line):
         return device_of(line, places)
 
-    arrived = []
-    for halo, step in zip(halos, (1, 2, -1, -2)):
+    arrived = [None] * 4
+    for kind, step in ((1, 2), (3, -2), (0, 1), (2, -1)):
         hops = [(place(b), place(b + step)) for b in range(total) if 0 <= b + step < total]
-        arrived.append(in_vmem(lax.ppermute(halo, ("dir", "pos"), hops)))
+        arrived[kind] = in_vmem(lax.ppermute(halos[kind], ("dir", "pos"), hops))
 
     table = pl.pallas_call(
         scatter_table_kernel,
@@ -615,29 +591,28 @@
         name="scatter_table",
     )(row_two, scatter_kernel)
 
+    table = in_vmem(table)
     wrapped = (bands + 2 * R) * bands
     half = bands * bands // 2
-    high, low, away = pl.pallas_call(
+    codes = shape((2, half + bands // 2, lanes), jnp.int16)
+    half_codes = shape((2, (half + bands // 2) // 2, lanes), jnp.int16)
+    high, low, away_first = pl.pallas_call(
         shear_kernel,
-        out_shape=[shape(((bands // 2 + 2 * R) * bands, 2 * lanes), bf16)] * 2
-        + [shape((2, half + bands // 2, lanes), jnp.int16)],
-        in_specs=smem(2) + anywhere(2) + vmem(4),
-        out_specs=anywhere(2) + vmem(1),
+        out_shape=[shape((wrapped, 2 * lanes), bf16)] * 2 + [half_codes],
+        in_specs=smem(2) + vmem(1) + anywhere(1) + vmem(4),
+        out_specs=vmem(3),
         scratch_shapes=[
             SMEM((bands,), jnp.int32),
             SMEM((2 * H,), jnp.int32),
             VMEM((4, len(UP_NEAR) * PER_SHIFT, lanes), f32),
-            VMEM((2, bands // 2, lanes), f32),
-            VMEM(table.shape, bf16),
+            VMEM((2, bands // 4, lanes), f32),
             VMEM(moved.shape, f32),
-            VMEM((wrapped, 2 * lanes), bf16),
-            VMEM((wrapped, 2 * lanes), bf16),
-            pltpu.SemaphoreType.DMA((3,)),
             pltpu.SemaphoreType.DMA((2 * H,)),
         ],
-        compiler_params=grant(24),
+        compiler_params=grant(16),
         name="shear",
     )(shift_first, fraction_first, table, moved, *arrived)
+    high, low = in_vmem(high), in_vmem(low)
     home = [(d, q, c, (d + q) % 2) for d in range(pairs) for q in range(places // 2) for c in range(2)]
     same = [
         (d * places + 2 * q + c, (1 - d) * places + 2 * q + b) for d, q, c, b in home if b == c
@@ -646,29 +621,31 @@
         (d * places + 2 * q + c, (1 - d) * places + 2 * q + b) for d, q, c, b in home if b != c
     ]
     inside = [(d * places + 2 * q + c, d * places + 2 * q + b) for d, q, c, b in home if b != c]
-    from_same = lax.ppermute(away, ("dir", "pos"), same)
-    from_cross = lax.ppermute(away, ("dir", "pos"), cross)
-    own = pl.pallas_call(
-        scatter_kernel_own,
-        out_shape=shape((2, half + bands // 2, lanes), jnp.int16),
-        in_specs=anywhere(3),
-        out_specs=pl.BlockSpec(memory_space=VMEM),
-        scratch_shapes=[
-            VMEM((2, bands // 2, lanes), f32),
-            VMEM(table.shape, bf16),
-            VMEM(high.shape, bf16),
-            VMEM(low.shape, bf16),
-            pltpu.SemaphoreType.DMA((9,)),
-        ],
-        compiler_params=grant(16),
-        name="scatter",
-    )(table, high, low)
+
+    def scatter(kernel, out_shape, bands_held):
+        return pl.pallas_call(
+            kernel,
+            out_shape=out_shape,
+            in_specs=vmem(3),
+            out_specs=pl.BlockSpec(memory_space=VMEM),
+            scratch_shapes=[VMEM((2, bands_held, lanes), f32)],
+            compiler_params=grant(8),
+        )(table, high, low)
+
+    from_same, from_cross = [], []
+    away = away_first
+    for part in range(2):
+        from_same.append(lax.ppermute(away, ("dir", "pos"), same))
+        from_cross.append(lax.ppermute(away, ("dir", "pos"), cross))
+        if part == 0:
+            away = scatter(scatter_away_kernel, half_codes, bands // 4)
+    own = scatter(scatter_own_kernel, codes, bands // 2)
     from_inside = lax.ppermute(own, ("dir", "pos"), inside)
-    pieces = [own] + [in_vmem(piece) for piece in (from_inside, from_same, from_cross)]
+    pieces = [own] + [in_vmem(piece) for piece in (from_inside, *from_same, *from_cross)]
     merged = pl.pallas_call(
         merge_kernel,
         out_shape=shape((half * 4, lanes), f32),
-        in_specs=vmem(4),
+        in_specs=vmem(6),
         out_specs=pl.BlockSpec(memory_space=pl.ANY),
         scratch_shapes=[
             VMEM((4, bands // 2, lanes), f32),

time: 190 us -> 187 us (0.984)
  starting transfers between devices: 18.2 us -> 22.1 us
  waiting for transfers between devices: 34.7 us -> 30.8 us
  Pallas kernels: 34.6 us -> 30.9 us
    ppermute x6 -> x8, waiting for transfers between devices: 34.7 us -> 30.8 us  [the longest x2 16.4 us: fast_body(): from_same.append(lax.ppermute(away, ('dir', 'pos'), same))]
    ppermute x6 -> x8, starting transfers between devices: 16.9 us -> 20.8 us  [the longest x4 10.4 us: fast_body(): arrived[kind] = in_vmem(lax.ppermute(halos[kind], ('dir', 'pos'), hops))]
    pallas_call x1, Pallas kernels: 12.1 us -> 10 us  [fast_body(): pl.pallas_call(functools.partial(transform_kernel, pairs), out_shape=[sha...]
    pallas_call x2 -> x3, Pallas kernels: 15.1 us -> 13.4 us  [the longest x2 6.82 us: scatter(): pl.pallas_call(kernel, out_shape=out_shape, in_specs=vmem(3), out_specs=p...]
  transfers between devices with their start and end apart: 7 -> 9, of which waited for: 3 -> 4; matrix products, arithmetic and copies ran while one was open for 0% -> 0% of each run, Pallas kernels for 0% -> 2%
where the time goes in v5:
time: 187 us; the launch traced here: 185 us
  blocking collectives  101 us (54%)
  Pallas kernels  30.9 us (17%)
  waiting for transfers between devices  30.8 us (16%)
  starting transfers between devices  22.1 us (12%)
    all_to_all x1, blocking collectives, fast_body(): lax.all_to_all(cut, ('dir', 'pos'), split_axis=0, concat_axis=0, tiled=Tr...  101 us
    ppermute x2, waiting for transfers between devices, fast_body(): from_same.append(lax.ppermute(away, ('dir', 'pos'), same))  16.4 us
    ppermute x4, waiting for transfers between devices, fast_body(): arrived[kind] = in_vmem(lax.ppermute(halos[kind], ('dir', 'pos'), hops))  14.5 us
    ppermute x4, starting transfers between devices, fast_body(): arrived[kind] = in_vmem(lax.ppermute(halos[kind], ('dir', 'pos'), hops))  10.4 us
    pallas_call x1, Pallas kernels, fast_body(): pl.pallas_call(functools.partial(transform_kernel, pairs), out_shape=[sha...  10 us
    ppermute x2, starting transfers between devices, fast_body(): from_same.append(lax.ppermute(away, ('dir', 'pos'), same))  8.96 us
    pallas_call x2, Pallas kernels, scatter(): pl.pallas_call(kernel, out_shape=out_shape, in_specs=vmem(3), out_specs=p...  6.82 us
    pallas_call x1, Pallas kernels, fast_body(): pl.pallas_call(shear_kernel, out_shape=[shape((wrapped, 2 * lanes), bf16)...  6.57 us
  transfers between devices with their start and end apart: 9, of which 4 were waited for; matrix products, arithmetic and copies ran while one was open for 0% of the time, Pallas kernels for 2%

profile of v5, /device:TPU:0, one launch (start us, length us, event | category | flops | bytes accessed | tf_op | source)
XLA Modules:
  0.0 185.0 jit_solution(10188543872597897719)
XLA Ops:
  0.0 4.5 %deal.1 = bf16[32,4,2,64,128]{4,3,2,1,0:T(8,128)(2,1)S(1)} custom-call(bf16[2,32,4,64,128]{4,3,2,1,0:T(8,128)(2,1)} %source.1), custom_call_target="tpu_custom_call" | custom-call | tf_op jit(solution)/shard_map/deal/pallas_call | solution.py:532
  4.6 0.0 copy-start
  4.6 0.0 copy-start.1
  4.6 0.0 copy-start.3
  4.6 0.0 copy-start.4
  4.6 0.0 copy-start.5
  4.6 100.8 %all_to_all.5.source = bf16[32,4,2,64,128]{4,3,2,1,0:T(8,128)(2,1)S(1)} all-to-all(bf16[32,4,2,64,128]{4,3,2,1,0:T(8,128)(2,1)S(1)} %deal.1), channel_id=1, replica_groups={{0,1,16,17,18,19,2,3,4,5,20,21,22,23,6,7,8,9,24,25,26,27,10,11,12,13,28..., dimensions={0} | all-to-all | bytes 8388608 | tf_op jit(solution)/shard_map/all_to_all | solution.py:545
  105.4 0.0 copy-done
  105.4 10.0 %transform.1 = (f32[64,2,64,128]{3,2,1,0:T(8,128)S(1)}, s16[3120,128]{1,0:T(8,128)(2,1)S(1)}, s16[1560,128]{1,0:T(8,128)(2,1)S(1)}, s16[3120,128]{1,0:T(8,128)(2,1)S(1)}, s16[1560,128]{1,0:T(8,128)(2,1)S(1)}) custom-call(s32[1,64]{1,0:T(1,128)S(1)} %bitcast.6, s32[1,64]{1,0:T(1,128)S(1)} %bitcast.4, f32[1,64]{1,0:T(1,128)S(1)} %bitcast.7, ...), custom_call_target="tpu_custom_call" | custom-call | tf_op jit(solution)/shard_map/transform/pallas_call | solution.py:552
  115.5 2.1 %collective-permute-start = (s16[3120,128]{1,0:T(8,128)(2,1)S(1)}, s16[3120,128]{1,0:T(8,128)(2,1)S(1)}, u32[]{:S(2)}, u32[]{:S(2)}) collective-permute-start(s16[3120,128]{1,0:T(8,128)(2,1)S(1)} %get-tuple-element.14), channel_id=1, source_target_pairs={{0,1},{1,16},{16,17},{17,18},{18,19},{19,2},{2,3},{3,4},{4,5},{5,2... | collective-permute-start | bytes 2396168 | tf_op jit(solution)/shard_map/ppermute | solution.py:582
  117.5 1.3 collective-permute-start.2
  118.8 5.6 %collective-permute-start.1 = (s16[1560,128]{1,0:T(8,128)(2,1)S(1)}, s16[1560,128]{1,0:T(8,128)(2,1)S(1)}, u32[]{:S(2)}, u32[]{:S(2)}) collective-permute-start(s16[1560,128]{1,0:T(8,128)(2,1)S(1)} %get-tuple-element.15), channel_id=1, source_target_pairs={{0,16},{1,17},{16,18},{17,19},{18,2},{19,3},{2,4},{3,5},{4,20},{5,... | collective-permute-start | bytes 1198088 | tf_op jit(solution)/shard_map/ppermute | solution.py:582
  124.4 1.5 collective-permute-start.3
  125.9 0.8 scatter_table.1.table
  126.7 7.3 %collective-permute-done.1.up_far = s16[1560,128]{1,0:T(8,128)(2,1)S(1)} collective-permute-done((s16[1560,128]{1,0:T(8,128)(2,1)S(1)}, s16[1560,128]{1,0:T(8,128)(2,1)S(1)}, u32[]{:S(2)}, u32[]{:S(2)}) %collective-permute-start.1) | collective-permute-done | bytes 399392 | tf_op jit(solution)/shard_map/ppermute | solution.py:582
  134.0 7.1 %collective-permute-done.3.down_far = s16[1560,128]{1,0:T(8,128)(2,1)S(1)} collective-permute-done((s16[1560,128]{1,0:T(8,128)(2,1)S(1)}, s16[1560,128]{1,0:T(8,128)(2,1)S(1)}, u32[]{:S(2)}, u32[]{:S(2)}) %collective-permute-start.3) | collective-permute-done | bytes 399392 | tf_op jit(solution)/shard_map/ppermute | solution.py:582
  141.1 0.0 collective-permute-done.up_near
  141.1 0.0 collective-permute-done.2.down_near
  141.2 6.6 %shear.1 = (bf16[5120,256]{1,0:T(8,128)(2,1)S(1)}, bf16[5120,256]{1,0:T(8,128)(2,1)S(1)}, s16[2,1040,128]{2,1,0:T(8,128)(2,1)S(1)}) custom-call(s32[64]{0:T(128)S(1)} %copy-done.4, f32[64]{0:T(128)S(1)} %copy-done.6, bf16[512,1280]{1,0:T(8,128)(2,1)S(1)} %scatter_table.1.table, f32[64,2,64,128]{3,2,1,0:T(8,128)S(1)} %get-tuple-element.13.source, ...), custom_call_target="tpu_custom_call" | custom-call | tf_op jit(solution)/shard_map/shear/pallas_call | solution.py:599
  147.7 4.3 %shard_map.82.refs_0_ = s16[2,2080,128]{2,1,0:T(8,128)(2,1)S(1)} custom-call(bf16[512,1280]{1,0:T(8,128)(2,1)S(1)} %scatter_table.1.table, bf16[5120,256]{1,0:T(8,128)(2,1)S(1)} %get-tuple-element.18.high, bf16[5120,256]{1,0:T(8,128)(2,1)S(1)} %get-tuple-element.19.low), custom_call_target="tpu_custom_call" | custom-call | tf_op jit(solution)/shard_map/pallas_call | solution.py:626
  152.0 1.3 collective-permute-start.4
  153.3 2.5 %shard_map.83 = s16[2,1040,128]{2,1,0:T(8,128)(2,1)S(1)} custom-call(bf16[512,1280]{1,0:T(8,128)(2,1)S(1)} %scatter_table.1.table, bf16[5120,256]{1,0:T(8,128)(2,1)S(1)} %get-tuple-element.18.high, bf16[5120,256]{1,0:T(8,128)(2,1)S(1)} %get-tuple-element.19.low), custom_call_target="tpu_custom_call" | custom-call | tf_op jit(solution)/shard_map/pallas_call | solution.py:626
  155.9 0.7 collective-permute-start.8
  156.6 6.0 %collective-permute-start.6 = (s16[2,1040,128]{2,1,0:T(8,128)(2,1)S(1)}, s16[2,1040,128]{2,1,0:T(8,128)(2,1)S(1)}, u32[]{:S(2)}, u32[]{:S(2)}) collective-permute-start(s16[2,1040,128]{2,1,0:T(8,128)(2,1)S(1)} %shard_map.83), channel_id=1, source_target_pairs={{0,16},{3,19},{4,20},{7,23},{8,24},{11,27},{12,28},{15,31},{17,1},... | collective-permute-start | bytes 1597448 | tf_op jit(solution)/shard_map/ppermute | solution.py:638
  162.5 0.7 collective-permute-start.7
  163.2 3.0 %collective-permute-start.5 = (s16[2,1040,128]{2,1,0:T(8,128)(2,1)S(1)}, s16[2,1040,128]{2,1,0:T(8,128)(2,1)S(1)}, u32[]{:S(2)}, u32[]{:S(2)}) collective-permute-start(s16[2,1040,128]{2,1,0:T(8,128)(2,1)S(1)} %get-tuple-element.20), channel_id=1, source_target_pairs={{0,16},{3,19},{4,20},{7,23},{8,24},{11,27},{12,28},{15,31},{17,1},... | collective-permute-start | bytes 1597448 | tf_op jit(solution)/shard_map/ppermute | solution.py:638
  166.2 0.0 collective-permute-done.8.refs_5_
  166.3 8.7 %collective-permute-done.6.refs_3_ = s16[2,1040,128]{2,1,0:T(8,128)(2,1)S(1)} collective-permute-done((s16[2,1040,128]{2,1,0:T(8,128)(2,1)S(1)}, s16[2,1040,128]{2,1,0:T(8,128)(2,1)S(1)}, u32[]{:S(2)}, u32[]{:S(2)}) %collective-permute-start.6) | collective-permute-done | bytes 532512 | tf_op jit(solution)/shard_map/ppermute | solution.py:638
  175.0 0.0 collective-permute-done.7.refs_4_
  175.0 7.7 %collective-permute-done.5.refs_2_ = s16[2,1040,128]{2,1,0:T(8,128)(2,1)S(1)} collective-permute-done((s16[2,1040,128]{2,1,0:T(8,128)(2,1)S(1)}, s16[2,1040,128]{2,1,0:T(8,128)(2,1)S(1)}, u32[]{:S(2)}, u32[]{:S(2)}) %collective-permute-start.5) | collective-permute-done | bytes 532512 | tf_op jit(solution)/shard_map/ppermute | solution.py:638
  182.6 0.0 collective-permute-done.4.refs_1_
  182.6 2.2 %merge.1 = f32[8192,128]{1,0:T(8,128)} custom-call(s16[2,2080,128]{2,1,0:T(8,128)(2,1)S(1)} %shard_map.82.refs_0_, s16[2,2080,128]{2,1,0:T(8,128)(2,1)S(1)} %collective-permute-done.4.refs_1_, s16[2,1040,128]{2,1,0:T(8,128)(2,1)S(1)} %collective-permute-done.5.refs_2_, s16[2,1040,128]{2,1,0:T(8,128)(2,1)S(1)} %collective-permute-done.6.refs_3_, ...), custom_call_target="tpu_custom_call" | custom-call | tf_op jit(solution)/shard_map/merge/pallas_call | solution.py:645
  (8 shorter events, 0.0 us)
Async XLA Ops:
  4.6 100.8 %copy-start = (bf16[64,1024]{1,0:T(8,128)(2,1)S(1)}, bf16[64,1024]{1,0:T(8,128)(2,1)}, u32[]{:S(2)}) copy-start(bf16[64,1024]{1,0:T(8,128)(2,1)} %constant.4.clone.table_one) | copy-start | bytes 393220
  4.6 100.8 %copy-start.1 = (bf16[64,256]{1,0:T(8,128)(2,1)S(1)}, bf16[64,256]{1,0:T(8,128)(2,1)}, u32[]{:S(2)}) copy-start(bf16[64,256]{1,0:T(8,128)(2,1)} %constant.5.clone.table_two) | copy-start | bytes 98308
  4.6 100.8 %copy-start.3 = (s32[64]{0:T(128)S(1)}, s32[64]{0:T(128)}, u32[]{:S(2)}) copy-start(s32[64]{0:T(128)} %param.11) | copy-start | bytes 772
  4.6 100.8 %copy-start.4 = (s32[64]{0:T(128)S(1)}, s32[64]{0:T(128)}, u32[]{:S(2)}) copy-start(s32[64]{0:T(128)} %shift_one.1) | copy-start | bytes 772
  4.6 100.8 %copy-start.5 = (f32[64]{0:T(128)S(1)}, f32[64]{0:T(128)}, u32[]{:S(2)}) copy-start(f32[64]{0:T(128)} %param.12) | copy-start | bytes 772
  105.4 20.6 %copy-start.2 = (f32[17,64]{1,0:T(8,128)S(1)}, f32[17,64]{1,0:T(8,128)}, u32[]{:S(2)}) copy-start(f32[17,64]{1,0:T(8,128)} %kernel.1) | copy-start | bytes 13060
  105.4 35.8 %copy-start.6 = (f32[64]{0:T(128)S(1)}, f32[64]{0:T(128)}, u32[]{:S(2)}) copy-start(f32[64]{0:T(128)} %fraction_one.1) | copy-start | bytes 772
  115.5 25.7 %collective-permute-start = (s16[3120,128]{1,0:T(8,128)(2,1)S(1)}, s16[3120,128]{1,0:T(8,128)(2,1)S(1)}, u32[]{:S(2)}, u32[]{:S(2)}) collective-permute-start(s16[3120,128]{1,0:T(8,128)(2,1)S(1)} %get-tuple-element.14), channel_id=1, source_target_pairs={{0,1},{1,16},{16,17},{17,18},{18,19},{19,2},{2,3},{3,4},{4,5},{5,2... | collective-permute-start | bytes 2396168 | tf_op jit(solution)/shard_map/ppermute | solution.py:582
  117.5 23.6 %collective-permute-start.2 = (s16[3120,128]{1,0:T(8,128)(2,1)S(1)}, s16[3120,128]{1,0:T(8,128)(2,1)S(1)}, u32[]{:S(2)}, u32[]{:S(2)}) collective-permute-start(s16[3120,128]{1,0:T(8,128)(2,1)S(1)} %get-tuple-element.16), channel_id=1, source_target_pairs={{1,0},{16,1},{17,16},{18,17},{19,18},{2,19},{3,2},{4,3},{5,4},{20,... | collective-permute-start | bytes 2396168 | tf_op jit(solution)/shard_map/ppermute | solution.py:582
  118.8 15.2 %collective-permute-start.1 = (s16[1560,128]{1,0:T(8,128)(2,1)S(1)}, s16[1560,128]{1,0:T(8,128)(2,1)S(1)}, u32[]{:S(2)}, u32[]{:S(2)}) collective-permute-start(s16[1560,128]{1,0:T(8,128)(2,1)S(1)} %get-tuple-element.15), channel_id=1, source_target_pairs={{0,16},{1,17},{16,18},{17,19},{18,2},{19,3},{2,4},{3,5},{4,20},{5,... | collective-permute-start | bytes 1198088 | tf_op jit(solution)/shard_map/ppermute | solution.py:582
  124.4 16.7 %collective-permute-start.3 = (s16[1560,128]{1,0:T(8,128)(2,1)S(1)}, s16[1560,128]{1,0:T(8,128)(2,1)S(1)}, u32[]{:S(2)}, u32[]{:S(2)}) collective-permute-start(s16[1560,128]{1,0:T(8,128)(2,1)S(1)} %get-tuple-element.17), channel_id=1, source_target_pairs={{16,0},{17,1},{18,16},{19,17},{2,18},{3,19},{4,2},{5,3},{20,4},{21... | collective-permute-start | bytes 1198088 | tf_op jit(solution)/shard_map/ppermute | solution.py:582
  152.0 30.6 %collective-permute-start.4 = (s16[2,2080,128]{2,1,0:T(8,128)(2,1)S(1)}, s16[2,2080,128]{2,1,0:T(8,128)(2,1)S(1)}, u32[]{:S(2)}, u32[]{:S(2)}) collective-permute-start(s16[2,2080,128]{2,1,0:T(8,128)(2,1)S(1)} %shard_map.82.refs_0_), channel_id=1, source_target_pairs={{1,0},{2,3},{5,4},{6,7},{9,8},{10,11},{13,12},{14,15},{16,17},{19,... | collective-permute-start | bytes 3194888 | tf_op jit(solution)/shard_map/ppermute | solution.py:643
  155.9 10.4 %collective-permute-start.8 = (s16[2,1040,128]{2,1,0:T(8,128)(2,1)S(1)}, s16[2,1040,128]{2,1,0:T(8,128)(2,1)S(1)}, u32[]{:S(2)}, u32[]{:S(2)}) collective-permute-start(s16[2,1040,128]{2,1,0:T(8,128)(2,1)S(1)} %shard_map.83), channel_id=1, source_target_pairs={{1,16},{2,19},{5,20},{6,23},{9,24},{10,27},{13,28},{14,31},{16,1},... | collective-permute-start | bytes 1597448 | tf_op jit(solution)/shard_map/ppermute | solution.py:639
  156.6 18.4 %collective-permute-start.6 = (s16[2,1040,128]{2,1,0:T(8,128)(2,1)S(1)}, s16[2,1040,128]{2,1,0:T(8,128)(2,1)S(1)}, u32[]{:S(2)}, u32[]{:S(2)}) collective-permute-start(s16[2,1040,128]{2,1,0:T(8,128)(2,1)S(1)} %shard_map.83), channel_id=1, source_target_pairs={{0,16},{3,19},{4,20},{7,23},{8,24},{11,27},{12,28},{15,31},{17,1},... | collective-permute-start | bytes 1597448 | tf_op jit(solution)/shard_map/ppermute | solution.py:638
  162.5 12.4 %collective-permute-start.7 = (s16[2,1040,128]{2,1,0:T(8,128)(2,1)S(1)}, s16[2,1040,128]{2,1,0:T(8,128)(2,1)S(1)}, u32[]{:S(2)}, u32[]{:S(2)}) collective-permute-start(s16[2,1040,128]{2,1,0:T(8,128)(2,1)S(1)} %get-tuple-element.20), channel_id=1, source_target_pairs={{1,16},{2,19},{5,20},{6,23},{9,24},{10,27},{13,28},{14,31},{16,1},... | collective-permute-start | bytes 1597448 | tf_op jit(solution)/shard_map/ppermute | solution.py:639
  163.2 19.4 %collective-permute-start.5 = (s16[2,1040,128]{2,1,0:T(8,128)(2,1)S(1)}, s16[2,1040,128]{2,1,0:T(8,128)(2,1)S(1)}, u32[]{:S(2)}, u32[]{:S(2)}) collective-permute-start(s16[2,1040,128]{2,1,0:T(8,128)(2,1)S(1)} %get-tuple-element.20), channel_id=1, source_target_pairs={{0,16},{3,19},{4,20},{7,23},{8,24},{11,27},{12,28},{15,31},{17,1},... | collective-permute-start | bytes 1597448 | tf_op jit(solution)/shard_map/ppermute | solution.py:638

commit v6 on v5

--- a/solution.py
+++ b/solution.py
@@ -19,6 +19,7 @@
 DOWN_FAR = ((1, 0), (0, 0), (0, 1))
 HALOS = (UP_NEAR, UP_FAR, DOWN_NEAR, DOWN_FAR)
 PER_SHIFT = 8
+OUTER, INNER = (0, 1, 6, 7), (2, 3, 4, 5)
 TOP = 32600.0
 FINE = 8.0
 LEAST = 1e-30
@@ -145,8 +146,8 @@
 
 def transform_kernel(
     pairs, shift_one, shift_two, fraction_two, table_one, table_two, source,
-    out, up_near, up_far, down_near, down_far, left_one, left_two, weight_near, weight_far, middle, scales,
-    received, stage, load_sem, store_sem,
+    out, up_near, up_far, down_near, down_far, middle, left_two, weight_near, weight_far, scales,
+    left_one, received, load_sem,
 ):
     count = 64
     lanes = out.shape[-1]
@@ -220,15 +221,34 @@
     lax.fori_loop(0, count // 8, first, 0, unroll=2)
 
     targets = (up_near, up_far, down_near, down_far)
-    stores = [
-        pltpu.make_async_copy(
-            stage.at[value % 2], out.at[pl.ds(value * PER_SHIFT, PER_SHIFT)], store_sem.at[value]
-        )
-        for value in range(2 * H)
-    ]
-    for value in range(2 * H):
-        if value >= 2:
-            stores[value - 2].wait()
+    finish_directions(OUTER, middle, left_two, weight_near, weight_far, out, targets, scales)
+    code_halo_scales(1, up_far, scales)
+    code_halo_scales(3, down_far, scales)
+
+
+def rest_kernel(
+    up_near_in, down_near_in, middle, left_two, weight_near, weight_far, scales_in,
+    out, up_near, down_near, scales,
+):
+    scales[...] = scales_in[...]
+    up_near[...] = up_near_in[...]
+    down_near[...] = down_near_in[...]
+    targets = (up_near, None, down_near, None)
+    finish_directions(INNER, middle, left_two, weight_near, weight_far, out, targets, scales)
+    code_halo_scales(0, up_near, scales)
+    code_halo_scales(2, down_near, scales)
+
+
+def code_halo_scales(kind, target, scales):
+    entries = target.shape[0] // 65
+    target[entries * 64 :, :] = scales[kind, :entries, :].astype(jnp.int32).astype(jnp.int16)
+
+
+def finish_directions(values, middle, left_two, weight_near, weight_far, out, targets, scales):
+    count = 64
+    lanes = out.shape[-1]
+    chunk = 2 * count * 2 * 8
+    for position, value in enumerate(values):
 
         def second(item, carry):
             slot = value * PER_SHIFT + item
@@ -260,7 +280,7 @@
                     span = slice(block * 8, block * 8 + 8)
                     pieces.append(near * weight_near[span, :] + far * weight_far[span, :])
                 moved = jnp.concatenate(pieces, axis=0)
-                stage[value % 2, item, row] = moved
+                out[position * PER_SHIFT + item, row] = moved
                 hits = [
                     (kind, wanted.index((value, row)))
                     for kind, wanted in enumerate(HALOS)
@@ -276,12 +296,6 @@
             return carry
 
         lax.fori_loop(0, PER_SHIFT, second, 0, unroll=8)
-        stores[value].start()
-    for kind, target in enumerate(targets):
-        entries = target.shape[0] // (count + 1)
-        target[entries * count :, :] = scales[kind, :entries, :].astype(jnp.int32).astype(jnp.int16)
-    for store in stores[-2:]:
-        store.wait()
 
 
 def scatter_table_kernel(shift_two, kernel, table, rows):
@@ -358,20 +372,10 @@
 
 
 def shear_kernel(
-    shift_one, fraction_one, table, source, up_near, up_far, down_near, down_far,
-    high, low, out, order, seen, arrived, sent, moved, load_sem,
+    shift_one, fraction_one, table, outer, inner, up_near, up_far, down_near, down_far,
+    high, low, out, order, seen, arrived, sent,
 ):
-    count = moved.shape[0]
-    loads = [
-        pltpu.make_async_copy(
-            source.at[pl.ds(value * PER_SHIFT, PER_SHIFT)],
-            moved.at[pl.ds(value * PER_SHIFT, PER_SHIFT)],
-            load_sem.at[value],
-        )
-        for value in range(2 * H)
-    ]
-    for load in loads:
-        load.start()
+    count = outer.shape[2]
     for value in range(2 * H):
         seen[value] = 0
 
@@ -391,7 +395,8 @@
 
     def fetch(value, item, row):
         if row in (0, 1):
-            return moved[value * PER_SHIFT + item, row]
+            held, values = (outer, OUTER) if value in OUTER else (inner, INNER)
+            return held[values.index(value) * PER_SHIFT + item, row]
         if row < 0:
             kind, key = (0, (value, row + 2)) if row >= -2 else (1, (value, row + 4))
         else:
@@ -402,7 +407,6 @@
 
     for value in range(2 * H):
         shift = value - H
-        loads[value].wait()
 
         def shear(item, carry):
             band = order[value * PER_SHIFT + item]
@@ -512,10 +516,6 @@
 
 def in_vmem(value):
     return pltpu.with_memory_space_constraint(value, VMEM)
-
-
-def anywhere(number):
-    return [pl.BlockSpec(memory_space=pl.ANY)] * number
 
 
 def smem(number):
@@ -549,37 +549,55 @@
 
     row_one, row_two = shift_first.reshape(1, bands), shift_second.reshape(1, bands)
     halo_shapes = [shape((len(one) * PER_SHIFT * (bands + 1), lanes), jnp.int16) for one in HALOS]
-    moved, *halos = pl.pallas_call(
+    rest_shapes = [
+        shape((4 * bands * bands, lanes), f32),
+        shape((2 * bands, 4 * bands), bf16),
+        shape((bands, lanes), f32),
+        shape((bands, lanes), f32),
+        shape((4, len(UP_NEAR) * PER_SHIFT, lanes), f32),
+    ]
+    part_shape = shape((bands // 2, 2, bands, lanes), f32)
+    outer, *halos = pl.pallas_call(
         functools.partial(transform_kernel, pairs),
-        out_shape=[shape((bands, 2, bands, lanes), f32)] + halo_shapes,
+        out_shape=[part_shape] + halo_shapes + rest_shapes,
         in_specs=vmem(5) + [pl.BlockSpec(memory_space=pl.ANY)],
-        out_specs=[pl.BlockSpec(memory_space=pl.ANY)] + vmem(4),
+        out_specs=vmem(10),
         scratch_shapes=[
             VMEM((8 * bands, 4 * bands), bf16),
-            VMEM((2 * bands, 4 * bands), bf16),
-            VMEM((bands, lanes), f32),
-            VMEM((bands, lanes), f32),
-            VMEM((4 * bands * bands, lanes), f32),
-            VMEM((4, len(UP_NEAR) * PER_SHIFT, lanes), f32),
             VMEM(received.shape, bf16),
-            VMEM((2, PER_SHIFT, 2, bands, lanes), f32),
             pltpu.SemaphoreType.DMA((bands // 8,)),
-            pltpu.SemaphoreType.DMA((2 * H,)),
         ],
-        compiler_params=grant(26),
+        compiler_params=grant(12),
         name="transform",
     )(
         row_one, row_two, fraction_second.reshape(1, bands),
         jnp.asarray(first_tables(bands, pairs)), jnp.asarray(second_tables(bands)), received,
     )
 
-    def place(line):
-        return device_of(line, places)
-
-    arrived = [None] * 4
-    for kind, step in ((1, 2), (3, -2), (0, 1), (2, -1)):
-        hops = [(place(b), place(b + step)) for b in range(total) if 0 <= b + step < total]
-        arrived[kind] = in_vmem(lax.ppermute(halos[kind], ("dir", "pos"), hops))
+    outer = in_vmem(outer)
+    rest = [in_vmem(value) for value in halos[4:]]
+
+    def send(halo, step):
+        hops = [
+            (device_of(b, places), device_of(b + step, places))
+            for b in range(total)
+            if 0 <= b + step < total
+        ]
+        return in_vmem(lax.ppermute(halo, ("dir", "pos"), hops))
+
+    far_up = send(halos[1], 2)
+    far_down = send(halos[3], -2)
+    inner, near_up, near_down = pl.pallas_call(
+        rest_kernel,
+        out_shape=[part_shape, halo_shapes[0], halo_shapes[2]],
+        in_specs=vmem(7),
+        out_specs=vmem(3),
+        scratch_shapes=[VMEM(rest_shapes[-1].shape, f32)],
+        compiler_params=grant(8),
+        name="rest",
+    )(in_vmem(halos[0]), in_vmem(halos[2]), *rest)
+    inner = in_vmem(inner)
+    arrived = [send(near_up, 1), far_up, send(near_down, -1), far_down]
 
     table = pl.pallas_call(
         scatter_table_kernel,
@@ -599,19 +617,17 @@
     high, low, away_first = pl.pallas_call(
         shear_kernel,
         out_shape=[shape((wrapped, 2 * lanes), bf16)] * 2 + [half_codes],
-        in_specs=smem(2) + vmem(1) + anywhere(1) + vmem(4),
+        in_specs=smem(2) + vmem(7),
         out_specs=vmem(3),
         scratch_shapes=[
             SMEM((bands,), jnp.int32),
             SMEM((2 * H,), jnp.int32),
             VMEM((4, len(UP_NEAR) * PER_SHIFT, lanes), f32),
             VMEM((2, bands // 4, lanes), f32),
-            VMEM(moved.shape, f32),
-            pltpu.SemaphoreType.DMA((2 * H,)),
         ],
-        compiler_params=grant(16),
+        compiler_params=grant(12),
         name="shear",
-    )(shift_first, fraction_first, table, moved, *arrived)
+    )(shift_first, fraction_first, table, outer, inner, *arrived)
     high, low = in_vmem(high), in_vmem(low)
     home = [(d, q, c, (d + q) % 2) for d in range(pairs) for q in range(places // 2) for c in range(2)]
     same = [

time: 187 us -> 184 us (0.984)
  Pallas kernels: 30.9 us -> 28.7 us
    pallas_call x1 -> x2, Pallas kernels: 10 us -> 8.15 us  [the longest x1 6.35 us: fast_body(): pl.pallas_call(functools.partial(transform_kernel, pairs), out_shape=[par...]
where the time goes in v6:
time: 184 us; the launch traced here: 183 us
  blocking collectives  101 us (55%)
  waiting for transfers between devices  32.6 us (18%)
  Pallas kernels  28.7 us (16%)
  starting transfers between devices  20.4 us (11%)
    all_to_all x1, blocking collectives, fast_body(): lax.all_to_all(cut, ('dir', 'pos'), split_axis=0, concat_axis=0, tiled=Tr...  101 us
    ppermute x2, waiting for transfers between devices, fast_body(): from_same.append(lax.ppermute(away, ('dir', 'pos'), same))  17.9 us
    ppermute x4, waiting for transfers between devices, send(): return in_vmem(lax.ppermute(halo, ('dir', 'pos'), hops))  14.6 us
    ppermute x4, starting transfers between devices, send(): return in_vmem(lax.ppermute(halo, ('dir', 'pos'), hops))  10.3 us
    ppermute x2, starting transfers between devices, fast_body(): from_same.append(lax.ppermute(away, ('dir', 'pos'), same))  7.27 us
    pallas_call x2, Pallas kernels, scatter(): pl.pallas_call(kernel, out_shape=out_shape, in_specs=vmem(3), out_specs=p...  6.87 us
    pallas_call x1, Pallas kernels, fast_body(): pl.pallas_call(functools.partial(transform_kernel, pairs), out_shape=[par...  6.35 us
    pallas_call x1, Pallas kernels, fast_body(): pl.pallas_call(shear_kernel, out_shape=[shape((wrapped, 2 * lanes), bf16)...  6.26 us
  transfers between devices with their start and end apart: 9, of which 4 were waited for; matrix products, arithmetic and copies ran while one was open for 0% of the time, Pallas kernels for 2%

profile of v6, /device:TPU:0, one launch (start us, length us, event | category | flops | bytes accessed | tf_op | source)
XLA Modules:
  0.0 182.9 jit_solution(12337131362531050943)
XLA Ops:
  0.0 4.5 %deal.1 = bf16[32,4,2,64,128]{4,3,2,1,0:T(8,128)(2,1)S(1)} custom-call(bf16[2,32,4,64,128]{4,3,2,1,0:T(8,128)(2,1)} %source.1), custom_call_target="tpu_custom_call" | custom-call | tf_op jit(solution)/shard_map/deal/pallas_call | solution.py:532
  4.6 0.0 copy-start
  4.6 0.0 copy-start.1
  4.6 0.0 copy-start.3
  4.6 0.0 copy-start.4
  4.6 0.0 copy-start.5
  4.6 100.8 %all_to_all.5.source = bf16[32,4,2,64,128]{4,3,2,1,0:T(8,128)(2,1)S(1)} all-to-all(bf16[32,4,2,64,128]{4,3,2,1,0:T(8,128)(2,1)S(1)} %deal.1), channel_id=1, replica_groups={{0,1,16,17,18,19,2,3,4,5,20,21,22,23,6,7,8,9,24,25,26,27,10,11,12,13,28..., dimensions={0} | all-to-all | bytes 8388608 | tf_op jit(solution)/shard_map/all_to_all | solution.py:545
  105.4 6.4 %transform.1 = (f32[32,2,64,128]{3,2,1,0:T(8,128)S(1)}, s16[3120,128]{1,0:T(8,128)(2,1)S(1)}, s16[1560,128]{1,0:T(8,128)(2,1)S(1)}, s16[3120,128]{1,0:T(8,128)(2...) custom-call(s32[1,64]{1,0:T(1,128)S(1)} %bitcast.6, ...), custom_call_target="tpu_custom_call" | custom-call | tf_op jit(solution)/shard_map/transform/pallas_call | solution.py:560
  111.8 0.0 copy-start.2
  111.8 0.0 copy-start.6
  111.8 1.8 rest.1
  113.6 2.1 %collective-permute-start = (s16[3120,128]{1,0:T(8,128)(2,1)S(1)}, s16[3120,128]{1,0:T(8,128)(2,1)S(1)}, u32[]{:S(2)}, u32[]{:S(2)}) collective-permute-start(s16[3120,128]{1,0:T(8,128)(2,1)S(1)} %get-tuple-element.30), channel_id=1, source_target_pairs={{0,1},{1,16},{16,17},{17,18},{18,19},{19,2},{2,3},{3,4},{4,5},{5,2... | collective-permute-start | bytes 2396168 | tf_op jit(solution)/shard_map/ppermute | solution.py:586
  115.7 1.3 collective-permute-start.2
  117.0 5.6 %collective-permute-start.1 = (s16[1560,128]{1,0:T(8,128)(2,1)S(1)}, s16[1560,128]{1,0:T(8,128)(2,1)S(1)}, u32[]{:S(2)}, u32[]{:S(2)}) collective-permute-start(s16[1560,128]{1,0:T(8,128)(2,1)S(1)} %get-tuple-element.31), channel_id=1, source_target_pairs={{0,16},{1,17},{16,18},{17,19},{18,2},{19,3},{2,4},{3,5},{4,20},{5,... | collective-permute-start | bytes 1198088 | tf_op jit(solution)/shard_map/ppermute | solution.py:586
  122.6 1.3 collective-permute-start.3
  123.9 0.8 scatter_table.1.table
  124.6 7.5 %collective-permute-done.1.up_far = s16[1560,128]{1,0:T(8,128)(2,1)S(1)} collective-permute-done((s16[1560,128]{1,0:T(8,128)(2,1)S(1)}, s16[1560,128]{1,0:T(8,128)(2,1)S(1)}, u32[]{:S(2)}, u32[]{:S(2)}) %collective-permute-start.1) | collective-permute-done | bytes 399392 | tf_op jit(solution)/shard_map/ppermute | solution.py:586
  132.2 7.1 %collective-permute-done.3.down_far = s16[1560,128]{1,0:T(8,128)(2,1)S(1)} collective-permute-done((s16[1560,128]{1,0:T(8,128)(2,1)S(1)}, s16[1560,128]{1,0:T(8,128)(2,1)S(1)}, u32[]{:S(2)}, u32[]{:S(2)}) %collective-permute-start.3) | collective-permute-done | bytes 399392 | tf_op jit(solution)/shard_map/ppermute | solution.py:586
  139.3 0.0 collective-permute-done.up_near
  139.3 0.0 collective-permute-done.2.down_near
  139.3 6.3 %shear.1 = (bf16[5120,256]{1,0:T(8,128)(2,1)S(1)}, bf16[5120,256]{1,0:T(8,128)(2,1)S(1)}, s16[2,1040,128]{2,1,0:T(8,128)(2,1)S(1)}) custom-call(s32[64]{0:T(128)S(1)} %copy-done.4, f32[64]{0:T(128)S(1)} %copy-done.6, bf16[512,1280]{1,0:T(8,128)(2,1)S(1)} %scatter_table.1.table, f32[32,2,64,128]{3,2,1,0:T(8,128)S(1)} %get-tuple-element.21.outer, ...), custom_call_target="tpu_custom_call" | custom-call | tf_op jit(solution)/shard_map/shear/pallas_call | solution.py:617
  145.6 4.3 %shard_map.82.refs_0_ = s16[2,2080,128]{2,1,0:T(8,128)(2,1)S(1)} custom-call(bf16[512,1280]{1,0:T(8,128)(2,1)S(1)} %scatter_table.1.table, bf16[5120,256]{1,0:T(8,128)(2,1)S(1)} %get-tuple-element.34.high, bf16[5120,256]{1,0:T(8,128)(2,1)S(1)} %get-tuple-element.35.low), custom_call_target="tpu_custom_call" | custom-call | tf_op jit(solution)/shard_map/pallas_call | solution.py:642
  149.9 1.5 collective-permute-start.4
  151.4 2.5 %shard_map.83 = s16[2,1040,128]{2,1,0:T(8,128)(2,1)S(1)} custom-call(bf16[512,1280]{1,0:T(8,128)(2,1)S(1)} %scatter_table.1.table, bf16[5120,256]{1,0:T(8,128)(2,1)S(1)} %get-tuple-element.34.high, bf16[5120,256]{1,0:T(8,128)(2,1)S(1)} %get-tuple-element.35.low), custom_call_target="tpu_custom_call" | custom-call | tf_op jit(solution)/shard_map/pallas_call | solution.py:642
  153.9 3.5 %collective-permute-start.6 = (s16[2,1040,128]{2,1,0:T(8,128)(2,1)S(1)}, s16[2,1040,128]{2,1,0:T(8,128)(2,1)S(1)}, u32[]{:S(2)}, u32[]{:S(2)}) collective-permute-start(s16[2,1040,128]{2,1,0:T(8,128)(2,1)S(1)} %shard_map.83), channel_id=1, source_target_pairs={{0,16},{3,19},{4,20},{7,23},{8,24},{11,27},{12,28},{15,31},{17,1},... | collective-permute-start | bytes 1597448 | tf_op jit(solution)/shard_map/ppermute | solution.py:654
  157.4 0.7 collective-permute-start.8
  158.1 3.8 %collective-permute-start.5 = (s16[2,1040,128]{2,1,0:T(8,128)(2,1)S(1)}, s16[2,1040,128]{2,1,0:T(8,128)(2,1)S(1)}, u32[]{:S(2)}, u32[]{:S(2)}) collective-permute-start(s16[2,1040,128]{2,1,0:T(8,128)(2,1)S(1)} %get-tuple-element.36), channel_id=1, source_target_pairs={{0,16},{3,19},{4,20},{7,23},{8,24},{11,27},{12,28},{15,31},{17,1},... | collective-permute-start | bytes 1597448 | tf_op jit(solution)/shard_map/ppermute | solution.py:654
  161.9 0.7 collective-permute-start.7
  162.6 6.5 %collective-permute-done.6.refs_3_ = s16[2,1040,128]{2,1,0:T(8,128)(2,1)S(1)} collective-permute-done((s16[2,1040,128]{2,1,0:T(8,128)(2,1)S(1)}, s16[2,1040,128]{2,1,0:T(8,128)(2,1)S(1)}, u32[]{:S(2)}, u32[]{:S(2)}) %collective-permute-start.6) | collective-permute-done | bytes 532512 | tf_op jit(solution)/shard_map/ppermute | solution.py:654
  169.1 0.0 collective-permute-done.8.refs_5_
  169.1 11.4 %collective-permute-done.5.refs_2_ = s16[2,1040,128]{2,1,0:T(8,128)(2,1)S(1)} collective-permute-done((s16[2,1040,128]{2,1,0:T(8,128)(2,1)S(1)}, s16[2,1040,128]{2,1,0:T(8,128)(2,1)S(1)}, u32[]{:S(2)}, u32[]{:S(2)}) %collective-permute-start.5) | collective-permute-done | bytes 532512 | tf_op jit(solution)/shard_map/ppermute | solution.py:654
  180.5 2.2 %merge.1 = f32[8192,128]{1,0:T(8,128)} custom-call(s16[2,2080,128]{2,1,0:T(8,128)(2,1)S(1)} %shard_map.82.refs_0_, s16[2,2080,128]{2,1,0:T(8,128)(2,1)S(1)} %collective-permute-done.4.refs_1_, s16[2,1040,128]{2,1,0:T(8,128)(2,1)S(1)} %collective-permute-done.5.refs_2_, s16[2,1040,128]{2,1,0:T(8,128)(2,1)S(1)} %collective-permute-done.6.refs_3_, ...), custom_call_target="tpu_custom_call" | custom-call | tf_op jit(solution)/shard_map/merge/pallas_call | solution.py:661
  (9 shorter events, 0.0 us)
Async XLA Ops:
  4.6 100.8 %copy-start = (bf16[64,1024]{1,0:T(8,128)(2,1)S(1)}, bf16[64,1024]{1,0:T(8,128)(2,1)}, u32[]{:S(2)}) copy-start(bf16[64,1024]{1,0:T(8,128)(2,1)} %constant.4.clone.table_one) | copy-start | bytes 393220
  4.6 100.8 %copy-start.1 = (bf16[64,256]{1,0:T(8,128)(2,1)S(1)}, bf16[64,256]{1,0:T(8,128)(2,1)}, u32[]{:S(2)}) copy-start(bf16[64,256]{1,0:T(8,128)(2,1)} %constant.5.clone.table_two) | copy-start | bytes 98308
  4.6 100.8 %copy-start.3 = (s32[64]{0:T(128)S(1)}, s32[64]{0:T(128)}, u32[]{:S(2)}) copy-start(s32[64]{0:T(128)} %param.11) | copy-start | bytes 772
  4.6 100.8 %copy-start.4 = (s32[64]{0:T(128)S(1)}, s32[64]{0:T(128)}, u32[]{:S(2)}) copy-start(s32[64]{0:T(128)} %shift_one.1) | copy-start | bytes 772
  4.6 100.8 %copy-start.5 = (f32[64]{0:T(128)S(1)}, f32[64]{0:T(128)}, u32[]{:S(2)}) copy-start(f32[64]{0:T(128)} %param.12) | copy-start | bytes 772
  111.8 12.1 %copy-start.2 = (f32[17,64]{1,0:T(8,128)S(1)}, f32[17,64]{1,0:T(8,128)}, u32[]{:S(2)}) copy-start(f32[17,64]{1,0:T(8,128)} %kernel.1) | copy-start | bytes 13060
  111.8 27.5 %copy-start.6 = (f32[64]{0:T(128)S(1)}, f32[64]{0:T(128)}, u32[]{:S(2)}) copy-start(f32[64]{0:T(128)} %fraction_one.1) | copy-start | bytes 772
  113.6 25.7 %collective-permute-start = (s16[3120,128]{1,0:T(8,128)(2,1)S(1)}, s16[3120,128]{1,0:T(8,128)(2,1)S(1)}, u32[]{:S(2)}, u32[]{:S(2)}) collective-permute-start(s16[3120,128]{1,0:T(8,128)(2,1)S(1)} %get-tuple-element.30), channel_id=1, source_target_pairs={{0,1},{1,16},{16,17},{17,18},{18,19},{19,2},{2,3},{3,4},{4,5},{5,2... | collective-permute-start | bytes 2396168 | tf_op jit(solution)/shard_map/ppermute | solution.py:586
  115.7 23.6 %collective-permute-start.2 = (s16[3120,128]{1,0:T(8,128)(2,1)S(1)}, s16[3120,128]{1,0:T(8,128)(2,1)S(1)}, u32[]{:S(2)}, u32[]{:S(2)}) collective-permute-start(s16[3120,128]{1,0:T(8,128)(2,1)S(1)} %get-tuple-element.32), channel_id=1, source_target_pairs={{1,0},{16,1},{17,16},{18,17},{19,18},{2,19},{3,2},{4,3},{5,4},{20,... | collective-permute-start | bytes 2396168 | tf_op jit(solution)/shard_map/ppermute | solution.py:586
  117.0 15.2 %collective-permute-start.1 = (s16[1560,128]{1,0:T(8,128)(2,1)S(1)}, s16[1560,128]{1,0:T(8,128)(2,1)S(1)}, u32[]{:S(2)}, u32[]{:S(2)}) collective-permute-start(s16[1560,128]{1,0:T(8,128)(2,1)S(1)} %get-tuple-element.31), channel_id=1, source_target_pairs={{0,16},{1,17},{16,18},{17,19},{18,2},{19,3},{2,4},{3,5},{4,20},{5,... | collective-permute-start | bytes 1198088 | tf_op jit(solution)/shard_map/ppermute | solution.py:586
  122.6 16.7 %collective-permute-start.3 = (s16[1560,128]{1,0:T(8,128)(2,1)S(1)}, s16[1560,128]{1,0:T(8,128)(2,1)S(1)}, u32[]{:S(2)}, u32[]{:S(2)}) collective-permute-start(s16[1560,128]{1,0:T(8,128)(2,1)S(1)} %get-tuple-element.33), channel_id=1, source_target_pairs={{16,0},{17,1},{18,16},{19,17},{2,18},{3,19},{4,2},{5,3},{20,4},{21... | collective-permute-start | bytes 1198088 | tf_op jit(solution)/shard_map/ppermute | solution.py:586
  149.9 30.6 %collective-permute-start.4 = (s16[2,2080,128]{2,1,0:T(8,128)(2,1)S(1)}, s16[2,2080,128]{2,1,0:T(8,128)(2,1)S(1)}, u32[]{:S(2)}, u32[]{:S(2)}) collective-permute-start(s16[2,2080,128]{2,1,0:T(8,128)(2,1)S(1)} %shard_map.82.refs_0_), channel_id=1, source_target_pairs={{1,0},{2,3},{5,4},{6,7},{9,8},{10,11},{13,12},{14,15},{16,17},{19,... | collective-permute-start | bytes 3194888 | tf_op jit(solution)/shard_map/ppermute | solution.py:659
  153.9 15.2 %collective-permute-start.6 = (s16[2,1040,128]{2,1,0:T(8,128)(2,1)S(1)}, s16[2,1040,128]{2,1,0:T(8,128)(2,1)S(1)}, u32[]{:S(2)}, u32[]{:S(2)}) collective-permute-start(s16[2,1040,128]{2,1,0:T(8,128)(2,1)S(1)} %shard_map.83), channel_id=1, source_target_pairs={{0,16},{3,19},{4,20},{7,23},{8,24},{11,27},{12,28},{15,31},{17,1},... | collective-permute-start | bytes 1597448 | tf_op jit(solution)/shard_map/ppermute | solution.py:654
  157.4 11.7 %collective-permute-start.8 = (s16[2,1040,128]{2,1,0:T(8,128)(2,1)S(1)}, s16[2,1040,128]{2,1,0:T(8,128)(2,1)S(1)}, u32[]{:S(2)}, u32[]{:S(2)}) collective-permute-start(s16[2,1040,128]{2,1,0:T(8,128)(2,1)S(1)} %shard_map.83), channel_id=1, source_target_pairs={{1,16},{2,19},{5,20},{6,23},{9,24},{10,27},{13,28},{14,31},{16,1},... | collective-permute-start | bytes 1597448 | tf_op jit(solution)/shard_map/ppermute | solution.py:655
  158.1 22.4 %collective-permute-start.5 = (s16[2,1040,128]{2,1,0:T(8,128)(2,1)S(1)}, s16[2,1040,128]{2,1,0:T(8,128)(2,1)S(1)}, u32[]{:S(2)}, u32[]{:S(2)}) collective-permute-start(s16[2,1040,128]{2,1,0:T(8,128)(2,1)S(1)} %get-tuple-element.36), channel_id=1, source_target_pairs={{0,16},{3,19},{4,20},{7,23},{8,24},{11,27},{12,28},{15,31},{17,1},... | collective-permute-start | bytes 1597448 | tf_op jit(solution)/shard_map/ppermute | solution.py:654
  161.9 18.6 %collective-permute-start.7 = (s16[2,1040,128]{2,1,0:T(8,128)(2,1)S(1)}, s16[2,1040,128]{2,1,0:T(8,128)(2,1)S(1)}, u32[]{:S(2)}, u32[]{:S(2)}) collective-permute-start(s16[2,1040,128]{2,1,0:T(8,128)(2,1)S(1)} %get-tuple-element.36), channel_id=1, source_target_pairs={{1,16},{2,19},{5,20},{6,23},{9,24},{10,27},{13,28},{14,31},{16,1},... | collective-permute-start | bytes 1597448 | tf_op jit(solution)/shard_map/ppermute | solution.py:655

commit v7 on v6

--- a/solution.py
+++ b/solution.py
@@ -130,7 +130,7 @@
                         )
             return carry
 
-        lax.fori_loop(0, seconds, second, 0, unroll=2)
+        lax.fori_loop(0, seconds, second, 0, unroll=4)
 
 
 def encode(columns):
@@ -368,7 +368,7 @@
         scatter_pair(index, first_group, table, high, low, out, scales)
         return carry
 
-    lax.fori_loop(0, groups // 2, step, 0, unroll=4)
+    lax.fori_loop(0, groups // 2, step, 0, unroll=groups // 2)
 
 
 def shear_kernel(
@@ -454,7 +454,8 @@
 
 
 def scatter_away_kernel(table, high, low, out, sent):
-    scatter_band(1 - lax.axis_index("dir"), sent.shape[1] // 4, table, high, low, out, sent)
+    whole = (high.shape[0] // 64 - 2 * R) // 2
+    scatter_band(1 - lax.axis_index("dir"), (whole - sent.shape[1]) // 4, table, high, low, out, sent)
 
 
 def scatter_own_kernel(table, high, low, out, sent):
@@ -481,23 +482,25 @@
     for side in range(2):
         for here in range(2):
             used = ((local[0],), (local[1],)) if here else (across[:2], across[2:])
-            share = bands // len(used[0])
+            shares = [piece.shape[1] // 65 for piece in used[0]]
+            place = [(index, band) for index, held in enumerate(shares) for band in range(held)]
 
             @pl.when((core == side) & (held_here == (here == 1)))
             def _():
                 for slot in range(2):
                     for row in range(2):
                         for index, piece in enumerate(used[slot]):
-                            scale = piece[row, share * 64 : share * 65, :].astype(jnp.int32)
-                            span = slice(index * share, (index + 1) * share)
+                            held, begin = shares[index], sum(shares[:index])
+                            scale = piece[row, held * 64 : held * 65, :].astype(jnp.int32)
+                            span = slice(begin, begin + held)
                             scales[slot * 2 + row, span, :] = scale.astype(jnp.float32)
                 for step in range(steps):
                     for slot in range(2):
                         pair = side if slot == 0 else 1 - side
                         for row in range(2):
                             for band in range(step * width // 64, (step + 1) * width // 64):
-                                begin = band % share * 64
-                                rows = used[slot][band // share][row, begin : begin + 64, :]
+                                index, begin = place[band][0], place[band][1] * 64
+                                rows = used[slot][index][row, begin : begin + 64, :]
                                 value = decode(rows, scales[slot * 2 + row, band : band + 1, :])
                                 stage[pl.ds(2 * pair + row + band * 256, 64, stride=4), :] = value
                     stores[step].start()
@@ -613,17 +616,19 @@
     wrapped = (bands + 2 * R) * bands
     half = bands * bands // 2
     codes = shape((2, half + bands // 2, lanes), jnp.int16)
-    half_codes = shape((2, (half + bands // 2) // 2, lanes), jnp.int16)
+    early = bands // 8
+    early_codes = shape((2, early * (bands + 1), lanes), jnp.int16)
+    late_codes = shape((2, (bands // 2 - early) * (bands + 1), lanes), jnp.int16)
     high, low, away_first = pl.pallas_call(
         shear_kernel,
-        out_shape=[shape((wrapped, 2 * lanes), bf16)] * 2 + [half_codes],
+        out_shape=[shape((wrapped, 2 * lanes), bf16)] * 2 + [early_codes],
         in_specs=smem(2) + vmem(7),
         out_specs=vmem(3),
         scratch_shapes=[
             SMEM((bands,), jnp.int32),
             SMEM((2 * H,), jnp.int32),
             VMEM((4, len(UP_NEAR) * PER_SHIFT, lanes), f32),
-            VMEM((2, bands // 4, lanes), f32),
+            VMEM((2, early, lanes), f32),
         ],
         compiler_params=grant(12),
         name="shear",
@@ -654,7 +659,7 @@
         from_same.append(lax.ppermute(away, ("dir", "pos"), same))
         from_cross.append(lax.ppermute(away, ("dir", "pos"), cross))
         if part == 0:
-            away = scatter(scatter_away_kernel, half_codes, bands // 4)
+            away = scatter(scatter_away_kernel, late_codes, bands // 2 - early)
     own = scatter(scatter_own_kernel, codes, bands // 2)
     from_inside = lax.ppermute(own, ("dir", "pos"), inside)
     pieces = [own] + [in_vmem(piece) for piece in (from_inside, *from_same, *from_cross)]

time: 184 us -> 183 us (level)
  transfers between devices with their start and end apart: 9 -> 9, of which waited for: 4 -> 3; matrix products, arithmetic and copies ran while one was open for 0% -> 0% of each run, Pallas kernels for 2% -> 2%
where the time goes in v7:
time: 183 us; the launch traced here: 181 us
  blocking collectives  101 us (55%)
  waiting for transfers between devices  32.5 us (18%)
  Pallas kernels  27.1 us (15%)
  starting transfers between devices  20.3 us (11%)
    all_to_all x1, blocking collectives, fast_body(): lax.all_to_all(cut, ('dir', 'pos'), split_axis=0, concat_axis=0, tiled=Tr...  101 us
    ppermute x2, waiting for transfers between devices, fast_body(): from_same.append(lax.ppermute(away, ('dir', 'pos'), same))  18 us
    ppermute x4, waiting for transfers between devices, send(): return in_vmem(lax.ppermute(halo, ('dir', 'pos'), hops))  14.5 us
    ppermute x4, starting transfers between devices, send(): return in_vmem(lax.ppermute(halo, ('dir', 'pos'), hops))  10.4 us
    pallas_call x2, Pallas kernels, scatter(): pl.pallas_call(kernel, out_shape=out_shape, in_specs=vmem(3), out_specs=p...  7.68 us
    ppermute x2, starting transfers between devices, fast_body(): from_same.append(lax.ppermute(away, ('dir', 'pos'), same))  7.22 us
    pallas_call x1, Pallas kernels, fast_body(): pl.pallas_call(functools.partial(transform_kernel, pairs), out_shape=[par...  6.33 us
    pallas_call x1, Pallas kernels, fast_body(): pl.pallas_call(shear_kernel, out_shape=[shape((wrapped, 2 * lanes), bf16)...  5 us
  transfers between devices with their start and end apart: 9, of which 3 were waited for; matrix products, arithmetic and copies ran while one was open for 0% of the time, Pallas kernels for 2%

profile of v7, /device:TPU:0, one launch (start us, length us, event | category | flops | bytes accessed | tf_op | source)
XLA Modules:
  0.0 181.1 jit_solution(4638546029216513820)
XLA Ops:
  0.0 3.4 %deal.1 = bf16[32,4,2,64,128]{4,3,2,1,0:T(8,128)(2,1)S(1)} custom-call(bf16[2,32,4,64,128]{4,3,2,1,0:T(8,128)(2,1)} %source.1), custom_call_target="tpu_custom_call" | custom-call | tf_op jit(solution)/shard_map/deal/pallas_call | solution.py:535
  3.4 0.0 copy-start
  3.4 0.0 copy-start.1
  3.4 0.0 copy-start.3
  3.4 0.0 copy-start.4
  3.5 0.0 copy-start.5
  3.5 100.8 %all_to_all.5.source = bf16[32,4,2,64,128]{4,3,2,1,0:T(8,128)(2,1)S(1)} all-to-all(bf16[32,4,2,64,128]{4,3,2,1,0:T(8,128)(2,1)S(1)} %deal.1), channel_id=1, replica_groups={{0,1,16,17,18,19,2,3,4,5,20,21,22,23,6,7,8,9,24,25,26,27,10,11,12,13,28..., dimensions={0} | all-to-all | bytes 8388608 | tf_op jit(solution)/shard_map/all_to_all | solution.py:548
  104.3 6.3 %transform.1 = (f32[32,2,64,128]{3,2,1,0:T(8,128)S(1)}, s16[3120,128]{1,0:T(8,128)(2,1)S(1)}, s16[1560,128]{1,0:T(8,128)(2,1)S(1)}, s16[3120,128]{1,0:T(8,128)(2...) custom-call(s32[1,64]{1,0:T(1,128)S(1)} %bitcast.6, ...), custom_call_target="tpu_custom_call" | custom-call | tf_op jit(solution)/shard_map/transform/pallas_call | solution.py:563
  110.6 0.0 copy-start.2
  110.6 0.0 copy-start.6
  110.6 1.8 rest.1
  112.4 2.1 %collective-permute-start = (s16[3120,128]{1,0:T(8,128)(2,1)S(1)}, s16[3120,128]{1,0:T(8,128)(2,1)S(1)}, u32[]{:S(2)}, u32[]{:S(2)}) collective-permute-start(s16[3120,128]{1,0:T(8,128)(2,1)S(1)} %get-tuple-element.30), channel_id=1, source_target_pairs={{0,1},{1,16},{16,17},{17,18},{18,19},{19,2},{2,3},{3,4},{4,5},{5,2... | collective-permute-start | bytes 2396168 | tf_op jit(solution)/shard_map/ppermute | solution.py:589
  114.5 1.3 collective-permute-start.2
  115.8 5.6 %collective-permute-start.1 = (s16[1560,128]{1,0:T(8,128)(2,1)S(1)}, s16[1560,128]{1,0:T(8,128)(2,1)S(1)}, u32[]{:S(2)}, u32[]{:S(2)}) collective-permute-start(s16[1560,128]{1,0:T(8,128)(2,1)S(1)} %get-tuple-element.31), channel_id=1, source_target_pairs={{0,16},{1,17},{16,18},{17,19},{18,2},{19,3},{2,4},{3,5},{4,20},{5,... | collective-permute-start | bytes 1198088 | tf_op jit(solution)/shard_map/ppermute | solution.py:589
  121.4 1.5 collective-permute-start.3
  122.9 0.8 scatter_table.1.table
  123.6 7.3 %collective-permute-done.1.up_far = s16[1560,128]{1,0:T(8,128)(2,1)S(1)} collective-permute-done((s16[1560,128]{1,0:T(8,128)(2,1)S(1)}, s16[1560,128]{1,0:T(8,128)(2,1)S(1)}, u32[]{:S(2)}, u32[]{:S(2)}) %collective-permute-start.1) | collective-permute-done | bytes 399392 | tf_op jit(solution)/shard_map/ppermute | solution.py:589
  131.0 7.1 %collective-permute-done.3.down_far = s16[1560,128]{1,0:T(8,128)(2,1)S(1)} collective-permute-done((s16[1560,128]{1,0:T(8,128)(2,1)S(1)}, s16[1560,128]{1,0:T(8,128)(2,1)S(1)}, u32[]{:S(2)}, u32[]{:S(2)}) %collective-permute-start.3) | collective-permute-done | bytes 399392 | tf_op jit(solution)/shard_map/ppermute | solution.py:589
  138.1 0.0 collective-permute-done.up_near
  138.1 0.0 collective-permute-done.2.down_near
  138.1 5.0 %shear.1 = (bf16[5120,256]{1,0:T(8,128)(2,1)S(1)}, bf16[5120,256]{1,0:T(8,128)(2,1)S(1)}, s16[2,520,128]{2,1,0:T(8,128)(2,1)S(1)}) custom-call(s32[64]{0:T(128)S(1)} %copy-done.4, f32[64]{0:T(128)S(1)} %copy-done.6, bf16[512,1280]{1,0:T(8,128)(2,1)S(1)} %scatter_table.1.table, f32[32,2,64,128]{3,2,1,0:T(8,128)S(1)} %get-tuple-element.21.outer, ...), custom_call_target="tpu_custom_call" | custom-call | tf_op jit(solution)/shard_map/shear/pallas_call | solution.py:622
  143.1 4.3 %shard_map.82.refs_0_ = s16[2,2080,128]{2,1,0:T(8,128)(2,1)S(1)} custom-call(bf16[512,1280]{1,0:T(8,128)(2,1)S(1)} %scatter_table.1.table, bf16[5120,256]{1,0:T(8,128)(2,1)S(1)} %get-tuple-element.34.high, bf16[5120,256]{1,0:T(8,128)(2,1)S(1)} %get-tuple-element.35.low), custom_call_target="tpu_custom_call" | custom-call | tf_op jit(solution)/shard_map/pallas_call | solution.py:647
  147.4 1.3 collective-permute-start.4
  148.7 3.3 %shard_map.83 = s16[2,1560,128]{2,1,0:T(8,128)(2,1)S(1)} custom-call(bf16[512,1280]{1,0:T(8,128)(2,1)S(1)} %scatter_table.1.table, bf16[5120,256]{1,0:T(8,128)(2,1)S(1)} %get-tuple-element.34.high, bf16[5120,256]{1,0:T(8,128)(2,1)S(1)} %get-tuple-element.35.low), custom_call_target="tpu_custom_call" | custom-call | tf_op jit(solution)/shard_map/pallas_call | solution.py:647
  152.1 3.5 %collective-permute-start.6 = (s16[2,1560,128]{2,1,0:T(8,128)(2,1)S(1)}, s16[2,1560,128]{2,1,0:T(8,128)(2,1)S(1)}, u32[]{:S(2)}, u32[]{:S(2)}) collective-permute-start(s16[2,1560,128]{2,1,0:T(8,128)(2,1)S(1)} %shard_map.83), channel_id=1, source_target_pairs={{0,16},{3,19},{4,20},{7,23},{8,24},{11,27},{12,28},{15,31},{17,1},... | collective-permute-start | bytes 2396168 | tf_op jit(solution)/shard_map/ppermute | solution.py:659
  155.6 0.7 collective-permute-start.8
  156.3 3.7 %collective-permute-start.5 = (s16[2,520,128]{2,1,0:T(8,128)(2,1)S(1)}, s16[2,520,128]{2,1,0:T(8,128)(2,1)S(1)}, u32[]{:S(2)}, u32[]{:S(2)}) collective-permute-start(s16[2,520,128]{2,1,0:T(8,128)(2,1)S(1)} %get-tuple-element.36), channel_id=1, source_target_pairs={{0,16},{3,19},{4,20},{7,23},{8,24},{11,27},{12,28},{15,31},{17,1},... | collective-permute-start | bytes 798728 | tf_op jit(solution)/shard_map/ppermute | solution.py:659
  160.0 0.7 collective-permute-start.7
  160.7 18.0 %collective-permute-done.5.refs_2_ = s16[2,520,128]{2,1,0:T(8,128)(2,1)S(1)} collective-permute-done((s16[2,520,128]{2,1,0:T(8,128)(2,1)S(1)}, s16[2,520,128]{2,1,0:T(8,128)(2,1)S(1)}, u32[]{:S(2)}, u32[]{:S(2)}) %collective-permute-start.5) | collective-permute-done | bytes 266272 | tf_op jit(solution)/shard_map/ppermute | solution.py:659
  178.7 0.0 collective-permute-done.7.refs_4_
  178.7 0.0 collective-permute-done.6.refs_3_
  178.8 2.2 %merge.1 = f32[8192,128]{1,0:T(8,128)} custom-call(s16[2,2080,128]{2,1,0:T(8,128)(2,1)S(1)} %shard_map.82.refs_0_, s16[2,2080,128]{2,1,0:T(8,128)(2,1)S(1)} %collective-permute-done.4.refs_1_, s16[2,520,128]{2,1,0:T(8,128)(2,1)S(1)} %collective-permute-done.5.refs_2_, s16[2,1560,128]{2,1,0:T(8,128)(2,1)S(1)} %collective-permute-done.6.refs_3_, ...), custom_call_target="tpu_custom_call" | custom-call | tf_op jit(solution)/shard_map/merge/pallas_call | solution.py:666
  (9 shorter events, 0.0 us)
Async XLA Ops:
  3.4 100.8 %copy-start = (bf16[64,1024]{1,0:T(8,128)(2,1)S(1)}, bf16[64,1024]{1,0:T(8,128)(2,1)}, u32[]{:S(2)}) copy-start(bf16[64,1024]{1,0:T(8,128)(2,1)} %constant.4.clone.table_one) | copy-start | bytes 393220
  3.4 100.8 %copy-start.1 = (bf16[64,256]{1,0:T(8,128)(2,1)S(1)}, bf16[64,256]{1,0:T(8,128)(2,1)}, u32[]{:S(2)}) copy-start(bf16[64,256]{1,0:T(8,128)(2,1)} %constant.5.clone.table_two) | copy-start | bytes 98308
  3.4 100.8 %copy-start.3 = (s32[64]{0:T(128)S(1)}, s32[64]{0:T(128)}, u32[]{:S(2)}) copy-start(s32[64]{0:T(128)} %param.11) | copy-start | bytes 772
  3.4 100.8 %copy-start.4 = (s32[64]{0:T(128)S(1)}, s32[64]{0:T(128)}, u32[]{:S(2)}) copy-start(s32[64]{0:T(128)} %shift_one.1) | copy-start | bytes 772
  3.5 100.8 %copy-start.5 = (f32[64]{0:T(128)S(1)}, f32[64]{0:T(128)}, u32[]{:S(2)}) copy-start(f32[64]{0:T(128)} %param.12) | copy-start | bytes 772
  110.6 12.3 %copy-start.2 = (f32[17,64]{1,0:T(8,128)S(1)}, f32[17,64]{1,0:T(8,128)}, u32[]{:S(2)}) copy-start(f32[17,64]{1,0:T(8,128)} %kernel.1) | copy-start | bytes 13060
  110.6 27.5 %copy-start.6 = (f32[64]{0:T(128)S(1)}, f32[64]{0:T(128)}, u32[]{:S(2)}) copy-start(f32[64]{0:T(128)} %fraction_one.1) | copy-start | bytes 772
  112.4 25.7 %collective-permute-start = (s16[3120,128]{1,0:T(8,128)(2,1)S(1)}, s16[3120,128]{1,0:T(8,128)(2,1)S(1)}, u32[]{:S(2)}, u32[]{:S(2)}) collective-permute-start(s16[3120,128]{1,0:T(8,128)(2,1)S(1)} %get-tuple-element.30), channel_id=1, source_target_pairs={{0,1},{1,16},{16,17},{17,18},{18,19},{19,2},{2,3},{3,4},{4,5},{5,2... | collective-permute-start | bytes 2396168 | tf_op jit(solution)/shard_map/ppermute | solution.py:589
  114.5 23.6 %collective-permute-start.2 = (s16[3120,128]{1,0:T(8,128)(2,1)S(1)}, s16[3120,128]{1,0:T(8,128)(2,1)S(1)}, u32[]{:S(2)}, u32[]{:S(2)}) collective-permute-start(s16[3120,128]{1,0:T(8,128)(2,1)S(1)} %get-tuple-element.32), channel_id=1, source_target_pairs={{1,0},{16,1},{17,16},{18,17},{19,18},{2,19},{3,2},{4,3},{5,4},{20,... | collective-permute-start | bytes 2396168 | tf_op jit(solution)/shard_map/ppermute | solution.py:589
  115.8 15.2 %collective-permute-start.1 = (s16[1560,128]{1,0:T(8,128)(2,1)S(1)}, s16[1560,128]{1,0:T(8,128)(2,1)S(1)}, u32[]{:S(2)}, u32[]{:S(2)}) collective-permute-start(s16[1560,128]{1,0:T(8,128)(2,1)S(1)} %get-tuple-element.31), channel_id=1, source_target_pairs={{0,16},{1,17},{16,18},{17,19},{18,2},{19,3},{2,4},{3,5},{4,20},{5,... | collective-permute-start | bytes 1198088 | tf_op jit(solution)/shard_map/ppermute | solution.py:589
  121.4 16.7 %collective-permute-start.3 = (s16[1560,128]{1,0:T(8,128)(2,1)S(1)}, s16[1560,128]{1,0:T(8,128)(2,1)S(1)}, u32[]{:S(2)}, u32[]{:S(2)}) collective-permute-start(s16[1560,128]{1,0:T(8,128)(2,1)S(1)} %get-tuple-element.33), channel_id=1, source_target_pairs={{16,0},{17,1},{18,16},{19,17},{2,18},{3,19},{4,2},{5,3},{20,4},{21... | collective-permute-start | bytes 1198088 | tf_op jit(solution)/shard_map/ppermute | solution.py:589
  147.4 31.3 %collective-permute-start.4 = (s16[2,2080,128]{2,1,0:T(8,128)(2,1)S(1)}, s16[2,2080,128]{2,1,0:T(8,128)(2,1)S(1)}, u32[]{:S(2)}, u32[]{:S(2)}) collective-permute-start(s16[2,2080,128]{2,1,0:T(8,128)(2,1)S(1)} %shard_map.82.refs_0_), channel_id=1, source_target_pairs={{1,0},{2,3},{5,4},{6,7},{9,8},{10,11},{13,12},{14,15},{16,17},{19,... | collective-permute-start | bytes 3194888 | tf_op jit(solution)/shard_map/ppermute | solution.py:664
  152.1 26.6 %collective-permute-start.6 = (s16[2,1560,128]{2,1,0:T(8,128)(2,1)S(1)}, s16[2,1560,128]{2,1,0:T(8,128)(2,1)S(1)}, u32[]{:S(2)}, u32[]{:S(2)}) collective-permute-start(s16[2,1560,128]{2,1,0:T(8,128)(2,1)S(1)} %shard_map.83), channel_id=1, source_target_pairs={{0,16},{3,19},{4,20},{7,23},{8,24},{11,27},{12,28},{15,31},{17,1},... | collective-permute-start | bytes 2396168 | tf_op jit(solution)/shard_map/ppermute | solution.py:659
  155.6 23.1 %collective-permute-start.8 = (s16[2,1560,128]{2,1,0:T(8,128)(2,1)S(1)}, s16[2,1560,128]{2,1,0:T(8,128)(2,1)S(1)}, u32[]{:S(2)}, u32[]{:S(2)}) collective-permute-start(s16[2,1560,128]{2,1,0:T(8,128)(2,1)S(1)} %shard_map.83), channel_id=1, source_target_pairs={{1,16},{2,19},{5,20},{6,23},{9,24},{10,27},{13,28},{14,31},{16,1},... | collective-permute-start | bytes 2396168 | tf_op jit(solution)/shard_map/ppermute | solution.py:660
  156.3 22.4 %collective-permute-start.5 = (s16[2,520,128]{2,1,0:T(8,128)(2,1)S(1)}, s16[2,520,128]{2,1,0:T(8,128)(2,1)S(1)}, u32[]{:S(2)}, u32[]{:S(2)}) collective-permute-start(s16[2,520,128]{2,1,0:T(8,128)(2,1)S(1)} %get-tuple-element.36), channel_id=1, source_target_pairs={{0,16},{3,19},{4,20},{7,23},{8,24},{11,27},{12,28},{15,31},{17,1},... | collective-permute-start | bytes 798728 | tf_op jit(solution)/shard_map/ppermute | solution.py:659
  160.0 18.7 %collective-permute-start.7 = (s16[2,520,128]{2,1,0:T(8,128)(2,1)S(1)}, s16[2,520,128]{2,1,0:T(8,128)(2,1)S(1)}, u32[]{:S(2)}, u32[]{:S(2)}) collective-permute-start(s16[2,520,128]{2,1,0:T(8,128)(2,1)S(1)} %get-tuple-element.36), channel_id=1, source_target_pairs={{1,16},{2,19},{5,20},{6,23},{9,24},{10,27},{13,28},{14,31},{16,1},... | collective-permute-start | bytes 798728 | tf_op jit(solution)/shard_map/ppermute | solution.py:660
